TPU v7x, 32 devices: a whole 2x2x4 slice. The times are simulated.
32 devices in a mesh: dp: 8 (over z, x), fsdp: 4 (over y, core).
Axes of the slice: x: 2, y: 2, z: 4, core: 2. Of those that a mesh axis runs over, the one named last changes fastest.
Arguments:
- frames: bfloat16 [32768, 1024], P(('dp', 'fsdp')), may hold values from -6 to 6
- segment_ids: int32 [32, 1024], P(('dp', 'fsdp')), may hold values from 0 to 3, as said below
- positions: int32 [32, 1024], P(('dp', 'fsdp')), may hold values from 0 to 1023, as said below
- cotangent: bfloat16 [32768, 1024], P(('dp', 'fsdp')), may hold values from -6 to 6
- norm1_gain: bfloat16 [1024], P(('dp', 'fsdp')), may hold values from 0.099609375 to 1.8984375
- norm1_shift: bfloat16 [1024], P(('dp', 'fsdp')), may hold values from -3 to 3
- qkv_weight: bfloat16 [1024, 3072], P('dp', 'fsdp'), may hold values from -0.1875 to 0.1875
- query_bias: bfloat16 [1024], P(('dp', 'fsdp')), may hold values from -3 to 3
- value_bias: bfloat16 [1024], P(('dp', 'fsdp')), may hold values from -3 to 3
- out_weight: bfloat16 [1024, 1024], P('dp', 'fsdp'), may hold values from -0.75 to 0.75
- out_bias: bfloat16 [1024], P(('dp', 'fsdp')), may hold values from -3 to 3
- norm2_gain: bfloat16 [1024], P(('dp', 'fsdp')), may hold values from 0.099609375 to 1.8984375
- norm2_shift: bfloat16 [1024], P(('dp', 'fsdp')), may hold values from -3 to 3
- up_weight: bfloat16 [1024, 4096], P('dp', 'fsdp'), may hold values from -0.1875 to 0.1875
- up_bias: bfloat16 [4096], P(('dp', 'fsdp')), may hold values from -3 to 3
- down_weight: bfloat16 [4096, 1024], P('dp', 'fsdp'), may hold values from -0.09375 to 0.09375
- down_bias: bfloat16 [1024], P(('dp', 'fsdp')), may hold values from -3 to 3
Outputs:
- output: bfloat16 [32768, 1024], P(('dp', 'fsdp'))
- frames_grad: bfloat16 [32768, 1024], P(('dp', 'fsdp'))
- norm1_gain_grad: float32 [1024], P(('dp', 'fsdp'))
- norm1_shift_grad: float32 [1024], P(('dp', 'fsdp'))
- qkv_weight_grad: float32 [1024, 3072], P('dp', 'fsdp')
- query_bias_grad: float32 [1024], P(('dp', 'fsdp'))
- value_bias_grad: float32 [1024], P(('dp', 'fsdp'))
- out_weight_grad: float32 [1024, 1024], P('dp', 'fsdp')
- out_bias_grad: float32 [1024], P(('dp', 'fsdp'))
- norm2_gain_grad: float32 [1024], P(('dp', 'fsdp'))
- norm2_shift_grad: float32 [1024], P(('dp', 'fsdp'))
- up_weight_grad: float32 [1024, 4096], P('dp', 'fsdp')
- up_bias_grad: float32 [4096], P(('dp', 'fsdp'))
- down_weight_grad: float32 [4096, 1024], P('dp', 'fsdp')
- down_bias_grad: float32 [1024], P(('dp', 'fsdp'))
Inputs may be any that keep to these rules, and one draw needn't show every extreme that they name: `segment_ids`: within each packed row the utterance numbers start at 0 and rise by one at each utterance's start; the first packed row holds one utterance, every other row exactly four. `positions`: A position is 0 where a row or an utterance begins and one more than the position before it otherwise.
All inputs are finite; a program needn't handle non-finite values.
Results may differ from a plain program's by a relative error of at most 0.02.
Values may be sent and summed in bfloat16 or wider, within the bound.
A program may use at most 320 MiB of HBM per device.

v0:
```python
from functools import partial
import math

import jax
import jax.numpy as jnp
from jax import lax
from jax.sharding import PartitionSpec as P

HEADS = 16
HEAD_DIM = 64


eps = 1e-05


def sinusoid(places, width):
    halves = jnp.arange(width // 2, dtype=jnp.float32)
    rates = jnp.exp(halves * (-2.0 * math.log(10000.0) / width))
    angles = places.astype(jnp.float32)[..., None] * rates
    return jnp.stack([jnp.sin(angles), jnp.cos(angles)], axis=-1).reshape(places.shape + (width,))


def affine_norm(values, gain, shift):
    centered = values - jnp.mean(values, axis=-1, keepdims=True)
    spread = jnp.mean(centered * centered, axis=-1, keepdims=True)
    return centered * lax.rsqrt(spread + eps) * gain + shift


def collect(params):
    pieces = tuple((item if item.ndim == 2 else item.reshape(1, -1) for item in params))
    wider = (
        lax.all_gather(pieces[0], "fsdp", axis=1, tiled=True),
        lax.all_gather(pieces[1], "fsdp", axis=1, tiled=True),
        lax.all_gather(pieces[2], "fsdp", axis=1, tiled=True),
        lax.all_gather(pieces[3], "fsdp", axis=1, tiled=True),
        lax.all_gather(pieces[4], "fsdp", axis=1, tiled=True),
        lax.all_gather(pieces[5], "fsdp", axis=1, tiled=True),
        lax.all_gather(pieces[6], "fsdp", axis=1, tiled=True),
        lax.all_gather(pieces[7], "fsdp", axis=1, tiled=True),
        lax.all_gather(pieces[8], "fsdp", axis=1, tiled=True),
        lax.all_gather(pieces[9], "fsdp", axis=1, tiled=True),
        lax.all_gather(pieces[10], "fsdp", axis=1, tiled=True),
        lax.all_gather(pieces[11], "fsdp", axis=1, tiled=True),
        lax.all_gather(pieces[12], "fsdp", axis=1, tiled=True),
    )
    whole = (
        lax.all_gather(wider[0], "dp", axis=0, tiled=True),
        lax.all_gather(wider[1], "dp", axis=0, tiled=True),
        lax.all_gather(wider[2], "dp", axis=0, tiled=True),
        lax.all_gather(wider[3], "dp", axis=0, tiled=True),
        lax.all_gather(wider[4], "dp", axis=0, tiled=True),
        lax.all_gather(wider[5], "dp", axis=0, tiled=True),
        lax.all_gather(wider[6], "dp", axis=0, tiled=True),
        lax.all_gather(wider[7], "dp", axis=0, tiled=True),
        lax.all_gather(wider[8], "dp", axis=0, tiled=True),
        lax.all_gather(wider[9], "dp", axis=0, tiled=True),
        lax.all_gather(wider[10], "dp", axis=0, tiled=True),
        lax.all_gather(wider[11], "dp", axis=0, tiled=True),
        lax.all_gather(wider[12], "dp", axis=0, tiled=True),
    )
    return tuple(
        (item if source.ndim == 2 else item.reshape(-1) for item, source in zip(whole, params))
    )


def spread_grads(grads):
    outer_count = lax.axis_size("dp")
    pieces = tuple((item if item.ndim == 2 else item.reshape(outer_count, -1) for item in grads))
    reduced = (
        lax.psum_scatter(
            pieces[0].astype(jnp.bfloat16), "dp", scatter_dimension=0, tiled=True
        ).astype(jnp.float32),
        lax.psum_scatter(
            pieces[1].astype(jnp.bfloat16), "dp", scatter_dimension=0, tiled=True
        ).astype(jnp.float32),
        lax.psum_scatter(
            pieces[2].astype(jnp.bfloat16), "dp", scatter_dimension=0, tiled=True
        ).astype(jnp.float32),
        lax.psum_scatter(
            pieces[3].astype(jnp.bfloat16), "dp", scatter_dimension=0, tiled=True
        ).astype(jnp.float32),
        lax.psum_scatter(
            pieces[4].astype(jnp.bfloat16), "dp", scatter_dimension=0, tiled=True
        ).astype(jnp.float32),
        lax.psum_scatter(
            pieces[5].astype(jnp.bfloat16), "dp", scatter_dimension=0, tiled=True
        ).astype(jnp.float32),
        lax.psum_scatter(
            pieces[6].astype(jnp.bfloat16), "dp", scatter_dimension=0, tiled=True
        ).astype(jnp.float32),
        lax.psum_scatter(
            pieces[7].astype(jnp.bfloat16), "dp", scatter_dimension=0, tiled=True
        ).astype(jnp.float32),
        lax.psum_scatter(
            pieces[8].astype(jnp.bfloat16), "dp", scatter_dimension=0, tiled=True
        ).astype(jnp.float32),
        lax.psum_scatter(
            pieces[9].astype(jnp.bfloat16), "dp", scatter_dimension=0, tiled=True
        ).astype(jnp.float32),
        lax.psum_scatter(
            pieces[10].astype(jnp.bfloat16), "dp", scatter_dimension=0, tiled=True
        ).astype(jnp.float32),
        lax.psum_scatter(
            pieces[11].astype(jnp.bfloat16), "dp", scatter_dimension=0, tiled=True
        ).astype(jnp.float32),
        lax.psum_scatter(
            pieces[12].astype(jnp.bfloat16), "dp", scatter_dimension=0, tiled=True
        ).astype(jnp.float32),
    )
    owned = (
        lax.psum_scatter(
            reduced[0].astype(jnp.bfloat16), "fsdp", scatter_dimension=1, tiled=True
        ).astype(jnp.float32),
        lax.psum_scatter(
            reduced[1].astype(jnp.bfloat16), "fsdp", scatter_dimension=1, tiled=True
        ).astype(jnp.float32),
        lax.psum_scatter(
            reduced[2].astype(jnp.bfloat16), "fsdp", scatter_dimension=1, tiled=True
        ).astype(jnp.float32),
        lax.psum_scatter(
            reduced[3].astype(jnp.bfloat16), "fsdp", scatter_dimension=1, tiled=True
        ).astype(jnp.float32),
        lax.psum_scatter(
            reduced[4].astype(jnp.bfloat16), "fsdp", scatter_dimension=1, tiled=True
        ).astype(jnp.float32),
        lax.psum_scatter(
            reduced[5].astype(jnp.bfloat16), "fsdp", scatter_dimension=1, tiled=True
        ).astype(jnp.float32),
        lax.psum_scatter(
            reduced[6].astype(jnp.bfloat16), "fsdp", scatter_dimension=1, tiled=True
        ).astype(jnp.float32),
        lax.psum_scatter(
            reduced[7].astype(jnp.bfloat16), "fsdp", scatter_dimension=1, tiled=True
        ).astype(jnp.float32),
        lax.psum_scatter(
            reduced[8].astype(jnp.bfloat16), "fsdp", scatter_dimension=1, tiled=True
        ).astype(jnp.float32),
        lax.psum_scatter(
            reduced[9].astype(jnp.bfloat16), "fsdp", scatter_dimension=1, tiled=True
        ).astype(jnp.float32),
        lax.psum_scatter(
            reduced[10].astype(jnp.bfloat16), "fsdp", scatter_dimension=1, tiled=True
        ).astype(jnp.float32),
        lax.psum_scatter(
            reduced[11].astype(jnp.bfloat16), "fsdp", scatter_dimension=1, tiled=True
        ).astype(jnp.float32),
        lax.psum_scatter(
            reduced[12].astype(jnp.bfloat16), "fsdp", scatter_dimension=1, tiled=True
        ).astype(jnp.float32),
    )
    return tuple(
        (item if source.ndim == 2 else item.reshape(-1) for item, source in zip(owned, grads))
    )


def block_scores(query_part, key_part, segment_query, segment_key, place_query, place_key):
    scale = 1.0 / math.sqrt(HEAD_DIM)
    raw = (
        jnp.einsum("qhd,khd->hqk", query_part, key_part, preferred_element_type=jnp.float32) * scale
    )
    allowed = (segment_query[:, None] == segment_key[None, :]) & (
        place_key[None, :] <= place_query[:, None]
    )
    return jnp.where(allowed[None], raw, -1e30)


def body(
    frames,
    segment_ids,
    positions,
    cotangent,
    norm1_gain,
    norm1_shift,
    qkv_weight,
    query_bias,
    value_bias,
    out_weight,
    out_bias,
    norm2_gain,
    norm2_shift,
    up_weight,
    up_bias,
    down_weight,
    down_bias,
):
    params = (
        norm1_gain,
        norm1_shift,
        qkv_weight,
        query_bias,
        value_bias,
        out_weight,
        out_bias,
        norm2_gain,
        norm2_shift,
        up_weight,
        up_bias,
        down_weight,
        down_bias,
    )
    length, width = frames.shape
    heads = HEADS
    scale = 1.0 / math.sqrt(HEAD_DIM)
    block = min(512, length)
    blocks = length // block
    segment_row = segment_ids[0]
    place_row = positions[0]
    (
        gain_first,
        shift_first,
        weight_in,
        bias_query,
        bias_value,
        weight_out,
        bias_out,
        gain_second,
        shift_second,
        weight_up,
        bias_up,
        weight_down,
        bias_down,
    ) = collect(params)
    gain_one = gain_first.astype(jnp.float32)
    shift_one = shift_first.astype(jnp.float32)
    gain_two = gain_second.astype(jnp.float32)
    shift_two = shift_second.astype(jnp.float32)
    inputs = frames.astype(jnp.float32) + sinusoid(place_row, width)
    normed_one = affine_norm(inputs, gain_one, shift_one).astype(jnp.bfloat16)
    projected = jnp.dot(normed_one, weight_in, preferred_element_type=jnp.float32)
    query = (
        (projected[:, :width] + bias_query.astype(jnp.float32))
        .astype(jnp.bfloat16)
        .reshape(length, heads, HEAD_DIM)
    )
    keys = projected[:, width : 2 * width].astype(jnp.bfloat16).reshape(length, heads, HEAD_DIM)
    values = (
        (projected[:, 2 * width :] + bias_value.astype(jnp.float32))
        .astype(jnp.bfloat16)
        .reshape(length, heads, HEAD_DIM)
    )

    def rows_of(index):
        return slice(index * block, (index + 1) * block)

    def scores_for(row_block, col_block):
        rows = rows_of(row_block)
        cols = rows_of(col_block)
        return block_scores(
            query[rows],
            keys[cols],
            segment_row[rows],
            segment_row[cols],
            place_row[rows],
            place_row[cols],
        )

    log_totals = []
    attended_all = []
    for row_block in range(blocks):
        peak = jnp.full((heads, block), -1e30, jnp.float32)
        total = jnp.zeros((heads, block), jnp.float32)
        for col_block in range(row_block + 1):
            scores = scores_for(row_block, col_block)
            new_peak = jnp.maximum(peak, jnp.max(scores, axis=-1))
            total = total * jnp.exp(peak - new_peak) + jnp.sum(
                jnp.exp(scores - new_peak[..., None]), axis=-1
            )
            peak = new_peak
        log_total = peak + jnp.log(total)
        attended = jnp.zeros((block, heads, HEAD_DIM), jnp.float32)
        for col_block in range(row_block + 1):
            probs = jnp.exp(scores_for(row_block, col_block) - log_total[..., None]).astype(
                jnp.bfloat16
            )
            attended = attended + jnp.einsum(
                "hqk,khd->qhd",
                probs,
                values[rows_of(col_block)],
                preferred_element_type=jnp.float32,
            )
        log_totals.append(log_total)
        attended_all.append(attended)
    mixed = jnp.concatenate(attended_all, axis=0).reshape(length, width).astype(jnp.bfloat16)
    resid_two = (
        inputs
        + jnp.dot(mixed, weight_out, preferred_element_type=jnp.float32)
        + bias_out.astype(jnp.float32)
    )
    normed_two = affine_norm(resid_two, gain_two, shift_two).astype(jnp.bfloat16)
    hidden = jnp.dot(normed_two, weight_up, preferred_element_type=jnp.float32) + bias_up.astype(
        jnp.float32
    )
    activated = jax.nn.gelu(hidden, approximate=False).astype(jnp.bfloat16)
    result = (
        resid_two
        + jnp.dot(activated, weight_down, preferred_element_type=jnp.float32)
        + bias_down.astype(jnp.float32)
    )
    output = result.astype(jnp.bfloat16)
    (
        gain_first,
        shift_first,
        weight_in,
        bias_query,
        bias_value,
        weight_out,
        bias_out,
        gain_second,
        shift_second,
        weight_up,
        bias_up,
        weight_down,
        bias_down,
    ) = collect(params)
    grad_out = cotangent.astype(jnp.float32)
    down_grad = jnp.einsum("tf,td->fd", activated, cotangent, preferred_element_type=jnp.float32)
    down_bias_grad = jnp.sum(cotangent.astype(jnp.float32), axis=0)
    grad_act = jnp.einsum("td,fd->tf", cotangent, weight_down, preferred_element_type=jnp.float32)
    _, gelu_back = jax.vjp(partial(jax.nn.gelu, approximate=False), hidden)
    grad_hidden = gelu_back(grad_act)[0].astype(jnp.bfloat16)
    up_grad = jnp.einsum("td,tf->df", normed_two, grad_hidden, preferred_element_type=jnp.float32)
    up_bias_grad = jnp.sum(grad_hidden.astype(jnp.float32), axis=0)
    grad_normed_two = jnp.einsum(
        "tf,df->td", grad_hidden, weight_up, preferred_element_type=jnp.float32
    )
    _, norm_back_two = jax.vjp(affine_norm, resid_two, gain_two, shift_two)
    grad_resid_two, gain_two_grad, shift_two_grad = norm_back_two(grad_normed_two)
    grad_two = grad_out + grad_resid_two
    grad_branch = grad_two.astype(jnp.bfloat16)
    out_grad = jnp.einsum("to,td->od", mixed, grad_branch, preferred_element_type=jnp.float32)
    out_bias_grad = jnp.sum(grad_branch.astype(jnp.float32), axis=0)
    grad_mixed = jnp.einsum(
        "td,od->to", grad_branch, weight_out, preferred_element_type=jnp.float32
    )
    grad_mixed = grad_mixed.astype(jnp.bfloat16).reshape(length, heads, HEAD_DIM)
    grad_query = jnp.zeros((length, heads, HEAD_DIM), jnp.float32)
    grad_keys = jnp.zeros((length, heads, HEAD_DIM), jnp.float32)
    grad_values = jnp.zeros((length, heads, HEAD_DIM), jnp.float32)
    for row_block in range(blocks):
        rows = rows_of(row_block)
        grad_part = grad_mixed[rows]
        log_total = log_totals[row_block]
        delta = jnp.zeros((heads, block), jnp.float32)
        for col_block in range(row_block + 1):
            probs = jnp.exp(scores_for(row_block, col_block) - log_total[..., None])
            grad_probs = jnp.einsum(
                "qhd,khd->hqk",
                grad_part,
                values[rows_of(col_block)],
                preferred_element_type=jnp.float32,
            )
            delta = delta + jnp.sum(probs * grad_probs, axis=-1)
        for col_block in range(row_block + 1):
            cols = rows_of(col_block)
            probs = jnp.exp(scores_for(row_block, col_block) - log_total[..., None])
            grad_probs = jnp.einsum(
                "qhd,khd->hqk", grad_part, values[cols], preferred_element_type=jnp.float32
            )
            grad_scores = (probs * (grad_probs - delta[..., None])).astype(jnp.bfloat16)
            grad_values = grad_values.at[cols].add(
                jnp.einsum(
                    "hqk,qhd->khd",
                    probs.astype(jnp.bfloat16),
                    grad_part,
                    preferred_element_type=jnp.float32,
                )
            )
            grad_query = grad_query.at[rows].add(
                jnp.einsum(
                    "hqk,khd->qhd", grad_scores, keys[cols], preferred_element_type=jnp.float32
                )
                * scale
            )
            grad_keys = grad_keys.at[cols].add(
                jnp.einsum(
                    "hqk,qhd->khd", grad_scores, query[rows], preferred_element_type=jnp.float32
                )
                * scale
            )
    grad_projected = jnp.concatenate(
        [
            grad_query.reshape(length, width).astype(jnp.bfloat16),
            grad_keys.reshape(length, width).astype(jnp.bfloat16),
            grad_values.reshape(length, width).astype(jnp.bfloat16),
        ],
        axis=1,
    )
    qkv_grad = jnp.einsum(
        "td,te->de", normed_one, grad_projected, preferred_element_type=jnp.float32
    )
    query_bias_grad = jnp.sum(grad_projected[:, :width].astype(jnp.float32), axis=0)
    value_bias_grad = jnp.sum(grad_projected[:, 2 * width :].astype(jnp.float32), axis=0)
    grad_normed_one = jnp.einsum(
        "te,de->td", grad_projected, weight_in, preferred_element_type=jnp.float32
    )
    _, norm_back_one = jax.vjp(affine_norm, inputs, gain_one, shift_one)
    grad_resid_one, gain_one_grad, shift_one_grad = norm_back_one(grad_normed_one)
    frames_grad = (grad_two + grad_resid_one).astype(jnp.bfloat16)
    owned = spread_grads(
        (
            gain_one_grad,
            shift_one_grad,
            qkv_grad,
            query_bias_grad,
            value_bias_grad,
            out_grad,
            out_bias_grad,
            gain_two_grad,
            shift_two_grad,
            up_grad,
            up_bias_grad,
            down_grad,
            down_bias_grad,
        )
    )
    return (output, frames_grad) + owned


def solution(mesh):
    placed = (
        P(("dp", "fsdp"), None),
        P(("dp", "fsdp"), None),
        P(("dp", "fsdp"), None),
        P(("dp", "fsdp"), None),
        P(("dp", "fsdp")),
        P(("dp", "fsdp")),
        P("dp", "fsdp"),
        P(("dp", "fsdp")),
        P(("dp", "fsdp")),
        P("dp", "fsdp"),
        P(("dp", "fsdp")),
        P(("dp", "fsdp")),
        P(("dp", "fsdp")),
        P("dp", "fsdp"),
        P(("dp", "fsdp")),
        P("dp", "fsdp"),
        P(("dp", "fsdp")),
    )
    return jax.shard_map(
        body,
        mesh=mesh,
        in_specs=placed,
        out_specs=(
            P(("dp", "fsdp"), None),
            P(("dp", "fsdp"), None),
            P(("dp", "fsdp")),
            P(("dp", "fsdp")),
            P("dp", "fsdp"),
            P(("dp", "fsdp")),
            P(("dp", "fsdp")),
            P("dp", "fsdp"),
            P(("dp", "fsdp")),
            P(("dp", "fsdp")),
            P(("dp", "fsdp")),
            P("dp", "fsdp"),
            P(("dp", "fsdp")),
            P("dp", "fsdp"),
            P(("dp", "fsdp")),
        ),
        check_vma=False,
    )
```

profile of v0, /device:TPU:0, one launch (start us, length us, event | category | flops | bytes accessed | tf_op | source)
XLA Modules:
  0.0 1428.7 jit_solution(7341922572786881008)
XLA Ops:
  8.7 11.8 all_gather.90
  20.5 8.4 all_gather.96
  39.2 7.5 all-reduce.20
  46.7 20.8 %all-gather.19 = bf16[8,1,128]{2,1,0:T(2,128)(2,1)S(1)} all-gather(bf16[1,1,128]{2,1,0:T(2,128)(2,1)S(1)} %bitcast.266), channel_id=5, replica_groups=mesh['dp'=8,'fsdp'=4] {'dp'}, dimensions={0}, use_global_device_ids=true | all-gather | bytes 2304 | tf_op jit(solution)/shard_map/all_gather | solution.py:48
  67.5 17.0 %all-gather.22 = bf16[8,1,128]{2,1,0:T(2,128)(2,1)S(1)} all-gather(bf16[1,1,128]{2,1,0:T(2,128)(2,1)S(1)} %bitcast.265), channel_id=11, replica_groups=mesh['dp'=8,'fsdp'=4] {'dp'}, dimensions={0}, use_global_device_ids=true | all-gather | bytes 2304 | tf_op jit(solution)/shard_map/all_gather | solution.py:53
  84.6 18.5 %all-gather.18 = bf16[8,1,128]{2,1,0:T(2,128)(2,1)S(1)} all-gather(bf16[1,1,128]{2,1,0:T(2,128)(2,1)S(1)} %bitcast.264), channel_id=3, replica_groups=mesh['dp'=8,'fsdp'=4] {'dp'}, dimensions={0}, use_global_device_ids=true | all-gather | bytes 2304 | tf_op jit(solution)/shard_map/all_gather | solution.py:47
  103.1 17.1 %all-gather.20 = bf16[8,1,128]{2,1,0:T(2,128)(2,1)S(1)} all-gather(bf16[1,1,128]{2,1,0:T(2,128)(2,1)S(1)} %bitcast.263), channel_id=7, replica_groups=mesh['dp'=8,'fsdp'=4] {'dp'}, dimensions={0}, use_global_device_ids=true | all-gather | bytes 2304 | tf_op jit(solution)/shard_map/all_gather | solution.py:51
  120.2 18.9 %all-gather.21 = bf16[8,1,128]{2,1,0:T(2,128)(2,1)S(1)} all-gather(bf16[1,1,128]{2,1,0:T(2,128)(2,1)S(1)} %bitcast.262), channel_id=9, replica_groups=mesh['dp'=8,'fsdp'=4] {'dp'}, dimensions={0}, use_global_device_ids=true | all-gather | bytes 2304 | tf_op jit(solution)/shard_map/all_gather | solution.py:50
  139.1 16.5 %all-gather.24 = bf16[8,1,128]{2,1,0:T(2,128)(2,1)S(1)} all-gather(bf16[1,1,128]{2,1,0:T(2,128)(2,1)S(1)} %bitcast.261), channel_id=15, replica_groups=mesh['dp'=8,'fsdp'=4] {'dp'}, dimensions={0}, use_global_device_ids=true | all-gather | bytes 2304 | tf_op jit(solution)/shard_map/all_gather | solution.py:55
  155.6 18.3 %all-gather.23 = bf16[8,1,128]{2,1,0:T(2,128)(2,1)S(1)} all-gather(bf16[1,1,128]{2,1,0:T(2,128)(2,1)S(1)} %bitcast.260), channel_id=13, replica_groups=mesh['dp'=8,'fsdp'=4] {'dp'}, dimensions={0}, use_global_device_ids=true | all-gather | bytes 2304 | tf_op jit(solution)/shard_map/all_gather | solution.py:54
  179.8 26.6 %all-gather.26 = bf16[8,1,512]{2,1,0:T(2,128)(2,1)S(1)} all-gather(bf16[1,1,512]{2,1,0:T(2,128)(2,1)S(1)} %bitcast.240), channel_id=17, replica_groups=mesh['dp'=8,'fsdp'=4] {'dp'}, dimensions={0}, use_global_device_ids=true | all-gather | bytes 9216 | tf_op jit(solution)/shard_map/all_gather | solution.py:57
  213.4 7.3 multiply_sine_fusion
  223.2 7.4 copy.153
  230.6 6.1 reshape.886
  244.0 13.4 fusion.63
  273.5 8.4 fusion.6
  281.9 9.2 exponential_reduce_fusion.2
  291.1 8.7 fusion.7
  299.9 7.3 fusion.8
  307.2 9.2 exponential_reduce_fusion.1
  316.4 9.3 exponential_reduce_fusion
  325.7 9.6 fusion.26
  335.4 8.3 fusion.22
  343.9 5.5 fusion.21
  349.7 6.1 fusion.64
  358.4 17.2 %fusion.49 = f32[1024,4096]{1,0:T(8,128)} fusion(bf16[1024,4096]{1,0:T(8,128)(2,1)} %all-gather.41.cloned.1.call-done, f32[1024,1024]{0,1:T(8,128)} %copy-done.7, f32[1024]{0:T(1024)S(1)} %bitcast.250, f32[1024]{0:T(1024)S(1)} %bitcast.225, f32[1024]{0:T(1024)S(1)} %fusion.31, f32[1024]{0:T(1024)S(1)} %broadcast_multiply_fusion), kind=kOutput, calls=%fused_computation.146 | convolution fusion | flops 8595177472 | bytes 29376512 | tf_op jit(solution)/shard_map/dot_general | solution.py:290
  375.6 73.8 %all-gather.45.cloned.1.call-done = bf16[4096,1024]{1,0:T(8,128)(2,1)} async-done(((bf16[512,1024]{1,0:T(8,128)(2,1)}), bf16[4096,1024]{1,0:T(8,128)(2,1)}) %all-gather.45.cloned.1.call-update) | async-done | bytes 8388624 | tf_op jit(solution)/shard_map/all_gather | solution.py:58
  449.4 51.5 %fusion.50 = (bf16[4096]{0:T(1024)(128)(2,1)}, bf16[1024,4096]{1,0:T(8,128)(2,1)S(1)}, f32[1024,4096]{1,0:T(8,128)}) fusion(f32[1024,4096]{1,0:T(8,128)} %fusion.49, f32[4096]{0:T(1024)S(1)} %bitcast.223, bf16[1024,1024]{1,0:T(8,128)(2,1)S(1)} %copy-done.25, bf16[4096,1024]{1,0:T(8,128)(2,1)} %all-gather.45.cloned.1.call-done), kind=kOutput, calls=%fused_computation.147 | convolution fusion | flops 8900308992 | bytes 52453376 | tf_op jit(solution)/shard_map/td,fd->tf/dot_general | solution.py:318
  500.9 11.4 fusion.66
  517.8 5.4 multiply_reduce_fusion.3
  536.0 9.8 convolution_bitcast_fusion
  545.8 11.9 multiply_reduce_fusion.2
  557.8 12.2 multiply_convert_fusion.2
  576.6 9.6 fusion.67
  586.8 8.3 fusion.18
  598.0 24.3 %multiply_reduce_fusion = (f32[16,512]{1,0:T(8,128)S(1)}, f32[16,512]{1,0:T(8,128)S(1)}, f32[16,512,512]{1,2,0:T(8,128)}) fusion(f32[16,512,512]{1,2,0:T(8,128)} %get-tuple-element.260, f32[16,512]{1,0:T(8,128)S(1)} %copy-done.41, pred[512,512]{0,1:T(8,128)(4,1)S(1)} %copy-done.29, f32[16,512,512]{1,2,0:T(8,128)} %fusion.67, ...), kind=kOutput, calls=%fused_computation.4 | convolution fusion | flops 578797568 | bytes 69828608 | tf_op jit(solution)/shard_map/qhd,khd->hqk/dot_general | solution.py:346
  622.3 27.1 %multiply_convert_fusion = (bf16[16,512,512]{1,2,0:T(8,128)(2,1)S(1)}, bf16[16,512,512]{1,2,0:T(8,128)(2,1)}) fusion(f32[16,512,512]{1,2,0:T(8,128)} %get-tuple-element.267, f32[16,512,512]{1,2,0:T(8,128)} %get-tuple-element.260, f32[16,512]{1,0:T(8,128)S(1)} %add.281, f32[16,512]{1,0:T(8,128)S(1)} %copy-done.41, pred[512,512]{0,1:T(8,128)(4,1)S(1)} %copy-done.29, ...), kind=kLoop, calls=%fused_computation.2 | loop fusion | flops 50331648 | bytes 84475904 | tf_op jit(solution)/shard_map/convert_element_type | solution.py:359
  660.1 5.7 fusion.17
  671.3 10.5 fusion.16
  688.0 13.5 convolution_convert_fusion.2
  701.6 12.9 multiply_convert_fusion.3
  717.8 11.2 convolution_convert_fusion
  729.7 15.8 %convolution_convert_fusion.1 = bf16[1024,4096]{1,0:T(8,128)(2,1)} fusion(bf16[1024,4096]{1,0:T(8,128)(2,1)} %copy-done.80, f32[1024,1024]{0,1:T(8,128)} %copy-done.7, f32[1024]{0:T(1024)S(1)} %bitcast.251, f32[1024]{0:T(1024)S(1)} %bitcast.228, f32[1024]{0:T(1024)S(1)} %copy-done.62, f32[1024]{0:T(1024)S(1)} %copy-done.52), kind=kOutput, calls=%fused_computation.39 | convolution fusion | flops 8599371776 | bytes 20987904 | tf_op jit(solution)/shard_map/td,tf->df/dot_general | solution.py:321
  748.9 12.4 fusion.65
  761.3 5.4 copy.175
  775.1 35.1 %all-reduce.19 = (bf16[8,128]{1,0:T(8,128)(2,1)S(1)}, bf16[8,128]{1,0:T(8,128)(2,1)S(1)}, bf16[8,128]{1,0:T(8,128)(2,1)S(1)}, bf16[8,128]{1,0:T(8,128)(2,1)S(1)}...) all-reduce(bf16[8,128]{1,0:T(8,128)(2,1)S(1)} %bitcast.239, ...), channel_id=20, replica_groups=mesh['dp'=8,'fsdp'=4] {'dp'}, use_global_device_ids=true, to_apply=%region_18.19.clone | all-reduce | flops 12288 | bytes 49152
  824.8 16.8 %all-gather.27 = bf16[8,1,128]{2,1,0:T(2,128)(2,1)S(1)} all-gather(bf16[1,1,128]{2,1,0:T(2,128)(2,1)S(1)} %bitcast.259), channel_id=19, replica_groups=mesh['dp'=8,'fsdp'=4] {'dp'}, dimensions={0}, use_global_device_ids=true | all-gather | bytes 2304 | tf_op jit(solution)/shard_map/all_gather | solution.py:59
  841.6 127.1 %reduce-scatter.48.cloned.1.call-done = bf16[512,1024]{1,0:T(8,128)(2,1)} async-done(((bf16[4096,1024]{1,0:T(8,128)(2,1)}), bf16[512,1024]{1,0:T(8,128)(2,1)}) %reduce-scatter.48.cloned.1.call-update) | async-done | bytes 1048592 | tf_op jit(solution)/shard_map/reduce_scatter | solution.py:103
  968.8 15.7 %add_convert_fusion.2 = bf16[1024,1024]{0,1:T(8,128)(2,1)} fusion(f32[1024,1024]{0,1:T(8,128)} %copy-done.7, f32[1024]{0:T(1024)S(1)} %bitcast.255, bf16[1024,4096]{1,0:T(8,128)(2,1)} %copy-done.24, bf16[4096,1024]{1,0:T(8,128)(2,1)} %all-gather.45.cloned.1.call-done), kind=kOutput, calls=%fused_computation.56 | convolution fusion | flops 8593080320 | bytes 23072768 | tf_op jit(solution)/shard_map/dot_general | solution.py:296
  984.5 134.2 %reduce-scatter.44.cloned.1.call-done = bf16[128,4096]{1,0:T(8,128)(2,1)} async-done(((bf16[1024,4096]{1,0:T(8,128)(2,1)}), bf16[128,4096]{1,0:T(8,128)(2,1)}) %reduce-scatter.44.cloned.1.call-update) | async-done | bytes 1048592 | tf_op jit(solution)/shard_map/reduce_scatter | solution.py:97
  1118.8 6.8 add_convert_fusion.1
  1133.4 6.4 reduce-scatter.68.cloned.1.call-done
  1140.6 21.1 %reduce-scatter.64.cloned.1.call-done = bf16[32,1]{1,0:T(8,128)(2,1)} async-done(((bf16[128,1]{1,0:T(8,128)(2,1)}), bf16[32,1]{1,0:T(8,128)(2,1)}) %reduce-scatter.64.cloned.1.call-update) | async-done | bytes 80
  1162.4 21.2 %reduce-scatter.62.cloned.1.call-done = bf16[32,1]{1,0:T(8,128)(2,1)} async-done(((bf16[128,1]{1,0:T(8,128)(2,1)}), bf16[32,1]{1,0:T(8,128)(2,1)}) %reduce-scatter.62.cloned.1.call-update) | async-done | bytes 80
  1184.4 21.1 %reduce-scatter.60.cloned.1.call-done = bf16[32,1]{1,0:T(8,128)(2,1)} async-done(((bf16[128,1]{1,0:T(8,128)(2,1)}), bf16[32,1]{1,0:T(8,128)(2,1)}) %reduce-scatter.60.cloned.1.call-update) | async-done | bytes 80
  1206.2 21.1 %reduce-scatter.58.cloned.1.call-done = bf16[32,1]{1,0:T(8,128)(2,1)} async-done(((bf16[128,1]{1,0:T(8,128)(2,1)}), bf16[32,1]{1,0:T(8,128)(2,1)}) %reduce-scatter.58.cloned.1.call-update) | async-done | bytes 80
  1228.1 21.6 %reduce-scatter.56.cloned.1.call-done = bf16[32,1]{1,0:T(8,128)(2,1)} async-done(((bf16[128,1]{1,0:T(8,128)(2,1)}), bf16[32,1]{1,0:T(8,128)(2,1)}) %reduce-scatter.56.cloned.1.call-update) | async-done | bytes 80
  1250.5 21.6 %reduce-scatter.54.cloned.1.call-done = bf16[32,1]{1,0:T(8,128)(2,1)} async-done(((bf16[128,1]{1,0:T(8,128)(2,1)}), bf16[32,1]{1,0:T(8,128)(2,1)}) %reduce-scatter.54.cloned.1.call-update) | async-done | bytes 80
  1272.9 21.6 %reduce-scatter.52.cloned.1.call-done = bf16[32,1]{1,0:T(8,128)(2,1)} async-done(((bf16[128,1]{1,0:T(8,128)(2,1)}), bf16[32,1]{1,0:T(8,128)(2,1)}) %reduce-scatter.52.cloned.1.call-update) | async-done | bytes 80
  1299.4 17.8 %reduce-scatter.66.cloned.1.call-done = bf16[128,1]{1,0:T(8,128)(2,1)} async-done(((bf16[512,1]{1,0:T(8,128)(2,1)}), bf16[128,1]{1,0:T(8,128)(2,1)}) %reduce-scatter.66.cloned.1.call-update) | async-done | bytes 272
  1318.6 21.0 %reduce-scatter.42.cloned.1.call-done = bf16[128,256]{1,0:T(8,128)(2,1)} async-done(((bf16[128,1024]{1,0:T(8,128)(2,1)}), bf16[128,256]{1,0:T(8,128)(2,1)}) %reduce-scatter.42.cloned.1.call-update) | async-done | bytes 65552 | tf_op jit(solution)/shard_map/reduce_scatter | solution.py:126
  1341.2 24.3 %reduce-scatter.38.cloned.1.call-done = bf16[128,768]{1,0:T(8,128)(2,1)} async-done(((bf16[128,3072]{1,0:T(8,128)(2,1)}), bf16[128,768]{1,0:T(8,128)(2,1)}) %reduce-scatter.38.cloned.1.call-update) | async-done | bytes 196624 | tf_op jit(solution)/shard_map/reduce_scatter | solution.py:117
  1367.1 25.6 %reduce-scatter.50.cloned.1.call-done = bf16[512,256]{1,0:T(8,128)(2,1)} async-done(((bf16[512,1024]{1,0:T(8,128)(2,1)}), bf16[512,256]{1,0:T(8,128)(2,1)}) %reduce-scatter.50.cloned.1.call-update) | async-done | bytes 262160 | tf_op jit(solution)/shard_map/reduce_scatter | solution.py:144
  1394.5 25.5 %reduce-scatter.46.cloned.1.call-done = bf16[128,1024]{1,0:T(8,128)(2,1)} async-done(((bf16[128,4096]{1,0:T(8,128)(2,1)}), bf16[128,1024]{1,0:T(8,128)(2,1)}) %reduce-scatter.46.cloned.1.call-update) | async-done | bytes 262160 | tf_op jit(solution)/shard_map/reduce_scatter | solution.py:138
  (351 shorter events, 159.9 us)
Async XLA Ops:
  7.2 23.2 %all-gather.39.cloned.1.call-start = ((), (), s32[]{:S(2)}) async-start(), calls=%async_computation.19 | async-start | bytes 1310720 | tf_op jit(solution)/shard_map/all_gather | solution.py:41
  7.9 235.8 %all-gather.43.cloned.1.call-start = ((), (), s32[]{:S(2)}) async-start(), calls=%async_computation.21 | async-start | bytes 1310720 | tf_op jit(solution)/shard_map/all_gather | solution.py:43
  8.7 235.3 %all-gather.35.cloned.1.call-start = ((), (), s32[]{:S(2)}) async-start(), calls=%async_computation.17 | async-start | bytes 7077888 | tf_op jit(solution)/shard_map/all_gather | solution.py:49
  20.5 329.2 %all-gather.37.cloned.1.call-start = ((), (), s32[]{:S(2)}) async-start(), calls=%async_computation.18 | async-start | bytes 2359296 | tf_op jit(solution)/shard_map/all_gather | solution.py:52
  29.0 329.4 %all-gather.41.cloned.1.call-start = ((), (), s32[]{:S(2)}) async-start(), calls=%async_computation.20 | async-start | bytes 9437184 | tf_op jit(solution)/shard_map/all_gather | solution.py:56
  30.4 419.0 %all-gather.45.cloned.1.call-start = ((), (), s32[]{:S(2)}) async-start(), calls=%async_computation.22 | async-start | bytes 9437184 | tf_op jit(solution)/shard_map/all_gather | solution.py:58
  67.5 176.5 %copy-start.74 = (f32[8,1,128]{2,1,0:T(1,128)}, f32[8,1,128]{2,1,0:T(1,128)S(1)}, u32[]{:S(2)}) copy-start(f32[8,1,128]{2,1,0:T(1,128)S(1)} %convert_element_type.377) | copy-start | bytes 12292
  103.1 140.9 %copy-start.46 = (f32[8,1,128]{2,1,0:T(1,128)}, f32[8,1,128]{2,1,0:T(1,128)S(1)}, u32[]{:S(2)}) copy-start(f32[8,1,128]{2,1,0:T(1,128)S(1)} %convert_element_type.376) | copy-start | bytes 12292
  155.6 202.8 %copy-start.72 = (f32[8,1,128]{2,1,0:T(1,128)}, f32[8,1,128]{2,1,0:T(1,128)S(1)}, u32[]{:S(2)}) copy-start(f32[8,1,128]{2,1,0:T(1,128)S(1)} %convert_element_type.382) | copy-start | bytes 12292
  173.9 184.5 %copy-start.57 = (f32[8,1,128]{2,1,0:T(1,128)}, f32[8,1,128]{2,1,0:T(1,128)S(1)}, u32[]{:S(2)}) copy-start(f32[8,1,128]{2,1,0:T(1,128)S(1)} %convert_element_type.381) | copy-start | bytes 12292
  206.4 243.0 %copy-start.48 = (f32[8,1,512]{2,1,0:T(1,128)}, f32[8,1,512]{2,1,0:T(1,128)S(1)}, u32[]{:S(2)}) copy-start(f32[8,1,512]{2,1,0:T(1,128)S(1)} %convert_element_type.383) | copy-start | bytes 49156
  223.2 13.5 copy-start.67
  223.2 13.5 copy-start.71
  239.7 17.7 %copy-start.44 = (f32[1024]{0:T(1024)}, f32[1024]{0:T(1024)S(1)}, u32[]{:S(2)}) copy-start(f32[1024]{0:T(1024)S(1)} %broadcast_multiply_fusion.1) | copy-start | bytes 12292
  242.2 15.3 %copy-start.63 = (f32[1024]{0:T(1024)}, f32[1024]{0:T(1024)S(1)}, u32[]{:S(2)}) copy-start(f32[1024]{0:T(1024)S(1)} %multiply_reduce_fusion.8) | copy-start | bytes 12292
  242.2 15.3 %copy-start.53 = (f32[1024]{0:T(1024)}, f32[1024]{0:T(1024)S(1)}, u32[]{:S(2)}) copy-start(f32[1024]{0:T(1024)S(1)} %fusion.30) | copy-start | bytes 12292
  243.7 100.0 %copy-start.28 = (pred[512,512]{0,1:T(8,128)(4,1)}, pred[512,512]{0,1:T(8,128)(4,1)S(1)}, u32[]{:S(2)}) copy-start(pred[512,512]{0,1:T(8,128)(4,1)S(1)} %get-tuple-element.250) | copy-start | bytes 786436
  243.7 579.8 %reduce-scatter.40.cloned.1.call-start = ((), (), s32[]{:S(2)}) async-start(), calls=%async_computation.25 | async-start | bytes 2359296 | tf_op jit(solution)/shard_map/reduce_scatter | solution.py:85
  258.2 41.7 %copy-start.17 = (bf16[512,1024]{0,1:T(8,128)(2,1)}, bf16[512,1024]{0,1:T(8,128)(2,1)S(1)}, u32[]{:S(2)}) copy-start(bf16[512,1024]{0,1:T(8,128)(2,1)S(1)} %copy.159) | copy-start | bytes 3145732
  258.7 32.4 %copy-start.4 = (bf16[512,1024]{0,1:T(8,128)(2,1)}, bf16[512,1024]{0,1:T(8,128)(2,1)S(1)}, u32[]{:S(2)}) copy-start(bf16[512,1024]{0,1:T(8,128)(2,1)S(1)} %copy.156) | copy-start | bytes 3145732
  268.5 31.3 %copy-start.10 = (bf16[512,1024]{0,1:T(8,128)(2,1)}, bf16[512,1024]{0,1:T(8,128)(2,1)S(1)}, u32[]{:S(2)}) copy-start(bf16[512,1024]{0,1:T(8,128)(2,1)S(1)} %copy.158) | copy-start | bytes 3145732
  291.1 44.3 %copy-start.42 = (f32[16,512]{1,0:T(8,128)}, f32[16,512]{1,0:T(8,128)S(1)}, u32[]{:S(2)}) copy-start(f32[16,512]{1,0:T(8,128)S(1)} %log_add_fusion.1) | copy-start | bytes 98308
  325.7 18.0 %copy-start.40 = (f32[16,512]{1,0:T(8,128)}, f32[16,512]{1,0:T(8,128)S(1)}, u32[]{:S(2)}) copy-start(f32[16,512]{1,0:T(8,128)S(1)} %log_add_fusion) | copy-start | bytes 98308
  325.7 9.7 copy-start.33
  325.7 18.0 %slice-start = ((s8[16777216]{0:T(1024)(128)(4,1)}), s8[4194304]{0:T(1024)(128)(4,1)S(1)}, s32[]{:S(2)}) async-start(s8[16777216]{0:T(1024)(128)(4,1)} %bitcast.175), calls=%async_computation.40 | async-start | bytes 8388608
  325.7 18.0 %slice-start.1 = ((s8[16777216]{0:T(1024)(128)(4,1)}), s8[4194304]{0:T(1024)(128)(4,1)S(1)}, s32[]{:S(2)}) async-start(s8[16777216]{0:T(1024)(128)(4,1)} %bitcast.175), calls=%async_computation.41 | async-start | bytes 8388608
  355.8 19.8 %copy-start.50 = (f32[1024]{0:T(1024)}, f32[1024]{0:T(1024)S(1)}, u32[]{:S(2)}) copy-start(f32[1024]{0:T(1024)S(1)} %broadcast_multiply_fusion) | copy-start | bytes 12292
  358.3 17.3 %copy-start.65 = (f32[1024]{0:T(1024)}, f32[1024]{0:T(1024)S(1)}, u32[]{:S(2)}) copy-start(f32[1024]{0:T(1024)S(1)} %multiply_reduce_fusion.7) | copy-start | bytes 12292
  358.3 17.3 %copy-start.60 = (f32[1024]{0:T(1024)}, f32[1024]{0:T(1024)S(1)}, u32[]{:S(2)}) copy-start(f32[1024]{0:T(1024)S(1)} %fusion.31) | copy-start | bytes 12292
  358.4 91.0 %copy-start.25 = (bf16[1024,1024]{1,0:T(8,128)(2,1)S(1)}, bf16[1024,1024]{1,0:T(8,128)(2,1)}, u32[]{:S(2)}) copy-start(bf16[1024,1024]{1,0:T(8,128)(2,1)} %param.38) | copy-start | bytes 6291460
  449.4 51.5 %copy-start.78 = (bf16[1024,4096]{1,0:T(8,128)(2,1)S(1)}, bf16[1024,4096]{1,0:T(8,128)(2,1)}, u32[]{:S(2)}) copy-start(bf16[1024,4096]{1,0:T(8,128)(2,1)} %all-gather.41.cloned.1.call-done) | copy-start | bytes 25165828
  500.9 11.5 copy-start.80
  512.4 10.8 copy-start.66
  536.0 62.0 %copy-start.19 = (bf16[512,1024]{0,1:T(8,128)(2,1)}, bf16[512,1024]{0,1:T(8,128)(2,1)S(1)}, u32[]{:S(2)}) copy-start(bf16[512,1024]{0,1:T(8,128)(2,1)S(1)} %get-tuple-element.236) | copy-start | bytes 3145732
  536.0 9.8 copy-start.22
  557.8 12.2 copy-start.23
  576.5 247.7 %reduce-scatter.36.cloned.1.call-start = ((), (), s32[]{:S(2)}) async-start(), calls=%async_computation.23 | async-start | bytes 7077888 | tf_op jit(solution)/shard_map/reduce_scatter | solution.py:76
  576.5 10.2 copy-start.32
  576.5 10.2 copy-start.41
  586.7 11.3 copy-start.29
  586.7 11.3 copy-start.36
  595.0 27.3 %copy-start.16 = (f32[1024,16,64]{0,2,1:T(8,128)}, f32[1024,16,64]{0,2,1:T(8,128)S(1)}, u32[]{:S(2)}) copy-start(f32[1024,16,64]{0,2,1:T(8,128)S(1)} %fusion.18) | copy-start | bytes 12582916
  671.3 14.2 copy-start.18
  688.0 13.6 copy-start.49
  701.5 267.2 %reduce-scatter.48.cloned.1.call-start = ((), (), s32[]{:S(2)}) async-start(), calls=%async_computation.29 | async-start | bytes 9437184 | tf_op jit(solution)/shard_map/reduce_scatter | solution.py:103
  701.6 16.2 %copy-start.26 = (bf16[1024,1024]{1,0:T(8,128)(2,1)S(1)}, bf16[1024,1024]{1,0:T(8,128)(2,1)}, u32[]{:S(2)}) copy-start(bf16[1024,1024]{1,0:T(8,128)(2,1)} %param.38) | copy-start | bytes 6291460
  729.1 389.6 %reduce-scatter.44.cloned.1.call-start = ((), (), s32[]{:S(2)}) async-start(), calls=%async_computation.27 | async-start | bytes 9437184 | tf_op jit(solution)/shard_map/reduce_scatter | solution.py:97
  745.5 394.3 %reduce-scatter.68.cloned.1.call-start = ((), (), s32[]{:S(2)}) async-start(), calls=%async_computation.39 | async-start | bytes 40960
  761.3 9.9 copy-start.64
  766.7 58.2 %copy-start.77 = (bf16[128]{0:T(256)(128)(2,1)S(1)}, bf16[128]{0:T(256)(128)(2,1)}, u32[]{:S(2)}) copy-start(bf16[128]{0:T(256)(128)(2,1)} %get-tuple-element.218) | copy-start | bytes 772
  811.7 350.0 %reduce-scatter.64.cloned.1.call-start = ((), (), s32[]{:S(2)}) async-start(), calls=%async_computation.37 | async-start | bytes 40960
  813.1 370.5 %reduce-scatter.62.cloned.1.call-start = ((), (), s32[]{:S(2)}) async-start(), calls=%async_computation.36 | async-start | bytes 40960
  814.6 390.9 %reduce-scatter.60.cloned.1.call-start = ((), (), s32[]{:S(2)}) async-start(), calls=%async_computation.35 | async-start | bytes 40960
  816.1 411.2 %reduce-scatter.58.cloned.1.call-start = ((), (), s32[]{:S(2)}) async-start(), calls=%async_computation.34 | async-start | bytes 40960
  817.5 432.2 %reduce-scatter.56.cloned.1.call-start = ((), (), s32[]{:S(2)}) async-start(), calls=%async_computation.33 | async-start | bytes 40960
  819.0 453.1 %reduce-scatter.54.cloned.1.call-start = ((), (), s32[]{:S(2)}) async-start(), calls=%async_computation.32 | async-start | bytes 40960
  820.4 474.1 %reduce-scatter.52.cloned.1.call-start = ((), (), s32[]{:S(2)}) async-start(), calls=%async_computation.31 | async-start | bytes 40960
  821.9 495.3 %reduce-scatter.66.cloned.1.call-start = ((), (), s32[]{:S(2)}) async-start(), calls=%async_computation.38 | async-start | bytes 163840
  823.5 516.2 %reduce-scatter.42.cloned.1.call-start = ((), (), s32[]{:S(2)}) async-start(), calls=%async_computation.26 | async-start | bytes 327680 | tf_op jit(solution)/shard_map/reduce_scatter | solution.py:126
  824.1 541.4 %reduce-scatter.38.cloned.1.call-start = ((), (), s32[]{:S(2)}) async-start(), calls=%async_computation.24 | async-start | bytes 983040 | tf_op jit(solution)/shard_map/reduce_scatter | solution.py:117
  824.8 568.0 %reduce-scatter.50.cloned.1.call-start = ((), (), s32[]{:S(2)}) async-start(), calls=%async_computation.30 | async-start | bytes 1310720 | tf_op jit(solution)/shard_map/reduce_scatter | solution.py:144
  968.7 451.4 %reduce-scatter.46.cloned.1.call-start = ((), (), s32[]{:S(2)}) async-start(), calls=%async_computation.28 | async-start | bytes 1310720 | tf_op jit(solution)/shard_map/reduce_scatter | solution.py:138
  968.7 150.0 %copy-start.13 = (bf16[1024,1024]{0,1:T(8,128)(2,1)S(1)}, bf16[1024,1024]{0,1:T(8,128)(2,1)}, u32[]{:S(2)}) copy-start(bf16[1024,1024]{0,1:T(8,128)(2,1)} %copy.164) | copy-start | bytes 6291460
  968.8 150.0 %copy-start.56 = (f32[1024]{0:T(1024)S(1)}, f32[1024]{0:T(1024)}, u32[]{:S(2)}) copy-start(f32[1024]{0:T(1024)} %copy-done.55) | copy-start | bytes 12292
  (44 other events, 216.9 us)
Sparse Core Ops, SparseCore 0:
  9.5 20.8 all-gather.38
  32.0 16.9 all-gather.42
  51.1 98.9 all-gather.34
  152.1 47.4 all-gather.36
  201.6 123.1 all-gather.40
  326.7 122.6 all-gather.44
  576.6 66.5 reduce-scatter.39
  701.6 116.4 reduce-scatter.35
  821.7 146.8 reduce-scatter.47
  972.1 146.5 reduce-scatter.43
  1121.1 18.6 reduce-scatter.67
  1142.1 19.5 reduce-scatter.63
  1164.0 19.5 reduce-scatter.61
  1185.9 19.5 reduce-scatter.59
  1207.7 19.5 reduce-scatter.57
  1230.1 19.5 reduce-scatter.55
  1252.5 19.5 reduce-scatter.53
  1275.0 19.5 reduce-scatter.51
  1297.5 19.6 reduce-scatter.65
  1319.5 20.0 reduce-scatter.41
  1342.2 23.1 reduce-scatter.37
  1367.9 24.7 reduce-scatter.49
  1395.3 24.7 reduce-scatter.45
where the time goes:
time: 1430 us
  waiting for transfers between devices  609 us (43%)
  matrix products  322 us (23%)
  blocking collectives  238 us (17%)
  other arithmetic  145 us (10%)
  local copies, waits for them, and re-layouts  96.5 us (7%)
  between operations  16.1 us (1%)
    unnamed x32, waiting for transfers between devices  176 us
    reduce_scatter x1, waiting for transfers between devices, spread_grads(): lax.psum_scatter(pieces[9].astype(jnp.bfloat16), 'dp', scatter_dimension=...  134 us
    reduce_scatter x1, waiting for transfers between devices, spread_grads(): lax.psum_scatter(pieces[11].astype(jnp.bfloat16), 'dp', scatter_dimension...  127 us
    all_gather x1, waiting for transfers between devices, collect(): lax.all_gather(wider[11], 'dp', axis=0, tiled=True)  73.8 us
    unnamed x219, local copies, waits for them, and re-layouts  57.6 us
    dot_general x1, matrix products, body(): jnp.einsum('td,fd->tf', cotangent, weight_down, preferred_element_type=jn...  51.5 us
    unnamed x2, blocking collectives  42.7 us
    convert_element_type x2, other arithmetic, body(): grad_scores = (probs * (grad_probs - delta[..., None])).astype(jnp.bfloat16)  39.3 us
  transfers between devices with their start and end apart: 23, of which 17 were waited for; matrix products, arithmetic and copies ran while one was open for 30% of the time, Pallas kernels for 0%

commit v1 on v0

--- a/solution.py
+++ b/solution.py
@@ -4,7 +4,11 @@
 import jax
 import jax.numpy as jnp
 from jax import lax
+from jax.experimental import pallas as pl
+from jax.experimental.pallas import tpu as pltpu
 from jax.sharding import PartitionSpec as P
+
+MESH = pl.DeviceIdType.MESH
 
 HEADS = 16
 HEAD_DIM = 64
@@ -26,131 +30,238 @@
     return centered * lax.rsqrt(spread + eps) * gain + shift
 
 
+def grid_of(dp_count, fsdp_count):
+    across = 1
+    while across * across * 2 <= dp_count:
+        across *= 2
+    while dp_count % across:
+        across //= 2
+    cores = 2 if fsdp_count % 2 == 0 else 1
+    return dp_count // across, across, fsdp_count // cores, cores
+
+
+def gather_kernel(plan, *refs):
+    dims, chunks, offsets = plan
+    deep, across, down, cores = dims
+    count = len(chunks)
+    names = len(refs) - 9
+    shards = refs[: names // 2]
+    wholes = refs[names // 2 : names]
+    local, z_send, z_recv, a_send, a_recv, b_send, b_recv, s_send, s_recv = refs[names:]
+    outer = lax.axis_index("dp")
+    inner = lax.axis_index("fsdp")
+    z, x, y, c = outer // across, outer % across, inner // cores, inner % cores
+
+    def device(zz, xx, yy, cc):
+        return (zz * across + xx, yy * cores + cc)
+
+    along_z = [device((z + k) % deep, x, y, c) for k in range(1, deep)]
+    along_x = [device(z, (x + k) % across, y, c) for k in range(1, across)]
+    along_y = [device(z, x, (y + k) % down, c) for k in range(1, down)]
+    twin = [device(z, x, y, 1 - c)] if cores == 2 else []
+    barrier = pltpu.get_barrier_semaphore()
+    everyone = along_z + along_x + along_y + twin
+    for peer in everyone:
+        pl.semaphore_signal(barrier, inc=1, device_id=peer, device_id_type=MESH)
+    pl.semaphore_wait(barrier, len(everyone))
+
+    def block(i, zz, xx, yy, cc):
+        which, rows, cols, start, size = chunks[i]
+        return wholes[which].at[
+            pl.ds(pl.multiple_of((zz * across + xx) * rows, 16), rows),
+            pl.ds(pl.multiple_of((yy * cores + cc) * cols + start, 128), size),
+        ]
+
+    def strip(i, yy, cc):
+        which, rows, cols, start, size = chunks[i]
+        return wholes[which].at[
+            :, pl.ds(pl.multiple_of((yy * cores + cc) * cols + start, 128), size)
+        ]
+
+    def own(i):
+        which, rows, cols, start, size = chunks[i]
+        return shards[which].at[:, pl.ds(start, size)]
+
+    def copy(source, target, send, recv, peer):
+        return pltpu.make_async_remote_copy(
+            src_ref=source,
+            dst_ref=target,
+            send_sem=send,
+            recv_sem=recv,
+            device_id=peer,
+            device_id_type=MESH,
+        )
+
+    def first(i):
+        pltpu.make_async_copy(own(i), block(i, z, x, y, c), local.at[i]).start()
+        for k, peer in enumerate(along_z):
+            copy(own(i), block(i, z, x, y, c), z_send.at[i, k], z_recv.at[i, k], peer).start()
+
+    def second(i):
+        pltpu.make_async_copy(own(i), block(i, z, x, y, c), local.at[i]).wait()
+        for k, peer in enumerate(along_z):
+            landed = block(i, (z + deep - k - 1) % deep, x, y, c)
+            copy(own(i), landed, z_send.at[i, k], z_recv.at[i, k], peer).wait()
+
+        @pl.when(c == 0)
+        def _():
+            for k, peer in enumerate(along_x):
+                for zz in range(deep):
+                    piece = block(i, zz, x, y, c)
+                    at = k * deep + zz
+                    copy(piece, piece, a_send.at[i, at], a_recv.at[i, at], peer).start()
+
+        @pl.when(c == 1)
+        def _():
+            for k, peer in enumerate(along_y):
+                for zz in range(deep):
+                    piece = block(i, zz, x, y, c)
+                    at = k * deep + zz
+                    copy(piece, piece, a_send.at[i, at], a_recv.at[i, at], peer).start()
+
+    def third(i):
+        @pl.when(c == 0)
+        def _():
+            for k, peer in enumerate(along_x):
+                for zz in range(deep):
+                    piece = block(i, zz, (x + across - k - 1) % across, y, c)
+                    at = k * deep + zz
+                    copy(piece, piece, a_send.at[i, at], a_recv.at[i, at], peer).wait()
+            mine = strip(i, y, c)
+            for k, peer in enumerate(along_y):
+                copy(mine, mine, b_send.at[i, k], b_recv.at[i, k], peer).start()
+            for peer in twin:
+                copy(mine, mine, s_send.at[i, 0], s_recv.at[i, 0], peer).start()
+
+        @pl.when(c == 1)
+        def _():
+            for k, peer in enumerate(along_y):
+                for zz in range(deep):
+                    piece = block(i, zz, x, (y + down - k - 1) % down, c)
+                    at = k * deep + zz
+                    copy(piece, piece, a_send.at[i, at], a_recv.at[i, at], peer).wait()
+            for k, peer in enumerate(along_x):
+                for zz in range(deep):
+                    for yy in range(down):
+                        piece = block(i, zz, x, yy, c)
+                        at = (k * deep + zz) * down + yy
+                        copy(piece, piece, b_send.at[i, at], b_recv.at[i, at], peer).start()
+
+    def fourth(i):
+        @pl.when(c == 0)
+        def _():
+            for k, peer in enumerate(along_y):
+                landed = strip(i, (y + down - k - 1) % down, c)
+                copy(landed, landed, b_send.at[i, k], b_recv.at[i, k], peer).wait()
+                for other in twin:
+                    copy(
+                        landed, landed, s_send.at[i, k + 1], s_recv.at[i, k + 1], other
+                    ).start()
+
+        @pl.when(c == 1)
+        def _():
+            for k, peer in enumerate(along_x):
+                for zz in range(deep):
+                    for yy in range(down):
+                        piece = block(i, zz, (x + across - k - 1) % across, yy, c)
+                        at = (k * deep + zz) * down + yy
+                        copy(piece, piece, b_send.at[i, at], b_recv.at[i, at], peer).wait()
+            for k in range(down):
+                piece = strip(i, (y + down - k) % down, c)
+                for other in twin:
+                    copy(piece, piece, s_send.at[i, k], s_recv.at[i, k], other).start()
+
+    def fifth(i):
+        for k in range(down):
+            landed = strip(i, (y + down - k) % down, 1 - c)
+            for other in twin:
+                copy(landed, landed, s_send.at[i, k], s_recv.at[i, k], other).wait()
+
+    stages = (first, second, third, fourth, fifth)
+    for step in range(count + offsets[-1]):
+        for at in reversed(range(5)):
+            i = step - offsets[at]
+            if 0 <= i < count:
+                stages[at](i)
+
+
+def gather_weights(shards):
+    dp_count, fsdp_count = lax.axis_size("dp"), lax.axis_size("fsdp")
+    dims = grid_of(dp_count, fsdp_count)
+    deep, across, down, cores = dims
+    chunks = []
+    for which, shard in enumerate(shards):
+        rows, cols = shard.shape
+        size = cols
+        if cols % 256 == 0 and rows * cols > 32768:
+            size = 256 if cols > 256 else 128
+        for start in range(0, cols, size):
+            chunks.append((which, rows, cols, start, size))
+    count = len(chunks)
+    flat = max(deep * max(across, down), 1)
+    return pl.pallas_call(
+        partial(gather_kernel, (dims, tuple(chunks), (0, 2, 4, 6, 8))),
+        out_shape=[
+            jax.ShapeDtypeStruct((s.shape[0] * dp_count, s.shape[1] * fsdp_count), s.dtype)
+            for s in shards
+        ],
+        in_specs=[pl.BlockSpec(memory_space=pl.ANY)] * len(shards),
+        out_specs=[pl.BlockSpec(memory_space=pl.ANY)] * len(shards),
+        scratch_shapes=[
+            pltpu.SemaphoreType.DMA((count,)),
+            pltpu.SemaphoreType.DMA((count, deep)),
+            pltpu.SemaphoreType.DMA((count, deep)),
+            pltpu.SemaphoreType.DMA((count, flat)),
+            pltpu.SemaphoreType.DMA((count, flat)),
+            pltpu.SemaphoreType.DMA((count, deep * across * down)),
+            pltpu.SemaphoreType.DMA((count, deep * across * down)),
+            pltpu.SemaphoreType.DMA((count, down)),
+            pltpu.SemaphoreType.DMA((count, down)),
+        ],
+        compiler_params=pltpu.CompilerParams(collective_id=0, has_side_effects=True),
+    )(*shards)
+
+
 def collect(params):
-    pieces = tuple((item if item.ndim == 2 else item.reshape(1, -1) for item in params))
-    wider = (
-        lax.all_gather(pieces[0], "fsdp", axis=1, tiled=True),
-        lax.all_gather(pieces[1], "fsdp", axis=1, tiled=True),
-        lax.all_gather(pieces[2], "fsdp", axis=1, tiled=True),
-        lax.all_gather(pieces[3], "fsdp", axis=1, tiled=True),
-        lax.all_gather(pieces[4], "fsdp", axis=1, tiled=True),
-        lax.all_gather(pieces[5], "fsdp", axis=1, tiled=True),
-        lax.all_gather(pieces[6], "fsdp", axis=1, tiled=True),
-        lax.all_gather(pieces[7], "fsdp", axis=1, tiled=True),
-        lax.all_gather(pieces[8], "fsdp", axis=1, tiled=True),
-        lax.all_gather(pieces[9], "fsdp", axis=1, tiled=True),
-        lax.all_gather(pieces[10], "fsdp", axis=1, tiled=True),
-        lax.all_gather(pieces[11], "fsdp", axis=1, tiled=True),
-        lax.all_gather(pieces[12], "fsdp", axis=1, tiled=True),
-    )
-    whole = (
-        lax.all_gather(wider[0], "dp", axis=0, tiled=True),
-        lax.all_gather(wider[1], "dp", axis=0, tiled=True),
-        lax.all_gather(wider[2], "dp", axis=0, tiled=True),
-        lax.all_gather(wider[3], "dp", axis=0, tiled=True),
-        lax.all_gather(wider[4], "dp", axis=0, tiled=True),
-        lax.all_gather(wider[5], "dp", axis=0, tiled=True),
-        lax.all_gather(wider[6], "dp", axis=0, tiled=True),
-        lax.all_gather(wider[7], "dp", axis=0, tiled=True),
-        lax.all_gather(wider[8], "dp", axis=0, tiled=True),
-        lax.all_gather(wider[9], "dp", axis=0, tiled=True),
-        lax.all_gather(wider[10], "dp", axis=0, tiled=True),
-        lax.all_gather(wider[11], "dp", axis=0, tiled=True),
-        lax.all_gather(wider[12], "dp", axis=0, tiled=True),
-    )
-    return tuple(
-        (item if source.ndim == 2 else item.reshape(-1) for item, source in zip(whole, params))
-    )
+    vectors = [item for item in params if item.ndim == 1]
+    packed = jnp.concatenate(vectors)
+    spread = lax.all_gather(packed, ("dp", "fsdp"), axis=0, tiled=False)
+    wholes = gather_weights([params[2], params[5], params[9], params[11]])
+    found = []
+    start = 0
+    matrices = iter(wholes)
+    for item in params:
+        if item.ndim == 2:
+            found.append(next(matrices))
+        else:
+            found.append(spread[:, start : start + item.shape[0]].reshape(-1))
+            start += item.shape[0]
+    return tuple(found)
 
 
 def spread_grads(grads):
-    outer_count = lax.axis_size("dp")
-    pieces = tuple((item if item.ndim == 2 else item.reshape(outer_count, -1) for item in grads))
-    reduced = (
-        lax.psum_scatter(
-            pieces[0].astype(jnp.bfloat16), "dp", scatter_dimension=0, tiled=True
-        ).astype(jnp.float32),
-        lax.psum_scatter(
-            pieces[1].astype(jnp.bfloat16), "dp", scatter_dimension=0, tiled=True
-        ).astype(jnp.float32),
-        lax.psum_scatter(
-            pieces[2].astype(jnp.bfloat16), "dp", scatter_dimension=0, tiled=True
-        ).astype(jnp.float32),
-        lax.psum_scatter(
-            pieces[3].astype(jnp.bfloat16), "dp", scatter_dimension=0, tiled=True
-        ).astype(jnp.float32),
-        lax.psum_scatter(
-            pieces[4].astype(jnp.bfloat16), "dp", scatter_dimension=0, tiled=True
-        ).astype(jnp.float32),
-        lax.psum_scatter(
-            pieces[5].astype(jnp.bfloat16), "dp", scatter_dimension=0, tiled=True
-        ).astype(jnp.float32),
-        lax.psum_scatter(
-            pieces[6].astype(jnp.bfloat16), "dp", scatter_dimension=0, tiled=True
-        ).astype(jnp.float32),
-        lax.psum_scatter(
-            pieces[7].astype(jnp.bfloat16), "dp", scatter_dimension=0, tiled=True
-        ).astype(jnp.float32),
-        lax.psum_scatter(
-            pieces[8].astype(jnp.bfloat16), "dp", scatter_dimension=0, tiled=True
-        ).astype(jnp.float32),
-        lax.psum_scatter(
-            pieces[9].astype(jnp.bfloat16), "dp", scatter_dimension=0, tiled=True
-        ).astype(jnp.float32),
-        lax.psum_scatter(
-            pieces[10].astype(jnp.bfloat16), "dp", scatter_dimension=0, tiled=True
-        ).astype(jnp.float32),
-        lax.psum_scatter(
-            pieces[11].astype(jnp.bfloat16), "dp", scatter_dimension=0, tiled=True
-        ).astype(jnp.float32),
-        lax.psum_scatter(
-            pieces[12].astype(jnp.bfloat16), "dp", scatter_dimension=0, tiled=True
-        ).astype(jnp.float32),
-    )
-    owned = (
-        lax.psum_scatter(
-            reduced[0].astype(jnp.bfloat16), "fsdp", scatter_dimension=1, tiled=True
-        ).astype(jnp.float32),
-        lax.psum_scatter(
-            reduced[1].astype(jnp.bfloat16), "fsdp", scatter_dimension=1, tiled=True
-        ).astype(jnp.float32),
-        lax.psum_scatter(
-            reduced[2].astype(jnp.bfloat16), "fsdp", scatter_dimension=1, tiled=True
-        ).astype(jnp.float32),
-        lax.psum_scatter(
-            reduced[3].astype(jnp.bfloat16), "fsdp", scatter_dimension=1, tiled=True
-        ).astype(jnp.float32),
-        lax.psum_scatter(
-            reduced[4].astype(jnp.bfloat16), "fsdp", scatter_dimension=1, tiled=True
-        ).astype(jnp.float32),
-        lax.psum_scatter(
-            reduced[5].astype(jnp.bfloat16), "fsdp", scatter_dimension=1, tiled=True
-        ).astype(jnp.float32),
-        lax.psum_scatter(
-            reduced[6].astype(jnp.bfloat16), "fsdp", scatter_dimension=1, tiled=True
-        ).astype(jnp.float32),
-        lax.psum_scatter(
-            reduced[7].astype(jnp.bfloat16), "fsdp", scatter_dimension=1, tiled=True
-        ).astype(jnp.float32),
-        lax.psum_scatter(
-            reduced[8].astype(jnp.bfloat16), "fsdp", scatter_dimension=1, tiled=True
-        ).astype(jnp.float32),
-        lax.psum_scatter(
-            reduced[9].astype(jnp.bfloat16), "fsdp", scatter_dimension=1, tiled=True
-        ).astype(jnp.float32),
-        lax.psum_scatter(
-            reduced[10].astype(jnp.bfloat16), "fsdp", scatter_dimension=1, tiled=True
-        ).astype(jnp.float32),
-        lax.psum_scatter(
-            reduced[11].astype(jnp.bfloat16), "fsdp", scatter_dimension=1, tiled=True
-        ).astype(jnp.float32),
-        lax.psum_scatter(
-            reduced[12].astype(jnp.bfloat16), "fsdp", scatter_dimension=1, tiled=True
-        ).astype(jnp.float32),
-    )
-    return tuple(
-        (item if source.ndim == 2 else item.reshape(-1) for item, source in zip(owned, grads))
-    )
+    dp_count, fsdp_count = lax.axis_size("dp"), lax.axis_size("fsdp")
+    devices = dp_count * fsdp_count
+    vectors = [item.reshape(devices, -1) for item in grads if item.ndim == 1]
+    widths = [item.shape[1] for item in vectors]
+    packed = jnp.concatenate(vectors, axis=1)
+    summed = lax.psum_scatter(packed, ("dp", "fsdp"), scatter_dimension=0, tiled=False)
+    found = []
+    start = 0
+    for item in grads:
+        if item.ndim == 2:
+            rows, cols = item.shape[0] // dp_count, item.shape[1] // fsdp_count
+            pieces = item.astype(jnp.bfloat16).reshape(dp_count, rows, fsdp_count, cols)
+            pieces = pieces.transpose(0, 2, 1, 3).reshape(devices, rows, cols)
+            owned = lax.psum_scatter(
+                pieces, ("dp", "fsdp"), scatter_dimension=0, tiled=False
+            )
+            found.append(owned.astype(jnp.float32))
+        else:
+            width = item.shape[0] // devices
+            found.append(summed[start : start + width])
+            start += width
+    return tuple(found)
 
 
 def block_scores(query_part, key_part, segment_query, segment_key, place_query, place_key):
@@ -297,21 +408,6 @@
         + bias_down.astype(jnp.float32)
     )
     output = result.astype(jnp.bfloat16)
-    (
-        gain_first,
-        shift_first,
-        weight_in,
-        bias_query,
-        bias_value,
-        weight_out,
-        bias_out,
-        gain_second,
-        shift_second,
-        weight_up,
-        bias_up,
-        weight_down,
-        bias_down,
-    ) = collect(params)
     grad_out = cotangent.astype(jnp.float32)
     down_grad = jnp.einsum("tf,td->fd", activated, cotangent, preferred_element_type=jnp.float32)
     down_bias_grad = jnp.sum(cotangent.astype(jnp.float32), axis=0)

time: 1430 us -> 1080 us (0.76)
  waiting for transfers between devices: 609 us -> 235 us
  blocking collectives: 238 us -> 88.7 us
  Pallas kernels: 0 us -> 131 us
  local copies, waits for them, and re-layouts: 96.5 us -> 146 us
  other arithmetic: 145 us -> 124 us
    unnamed x32 -> x4, waiting for transfers between devices: 176 us -> 0.07 us
    all_gather x12 -> x1, blocking collectives: 196 us -> 43.4 us  [collect(): spread = lax.all_gather(packed, ('dp', 'fsdp'), axis=0, tiled=False)]
    pallas_call x0 -> x1, Pallas kernels: none -> 131 us  [gather_weights(): pl.pallas_call(partial(gather_kernel, (dims, tuple(chunks), (0, 2, 4, 6,...]
    reduce_scatter x8 -> x4, waiting for transfers between devices: 358 us -> 235 us  [spread_grads(): lax.psum_scatter(pieces, ('dp', 'fsdp'), scatter_dimension=0, tiled=False)]
    all_gather x6 -> x0, waiting for transfers between devices: 75.3 us -> none  [the longest x1 73.8 us: collect(): lax.all_gather(wider[11], 'dp', axis=0, tiled=True)]
    reshape x0 -> x12, local copies, waits for them, and re-layouts: none -> 45.5 us  [the longest x4 44.9 us: spread_grads(): pieces = item.astype(jnp.bfloat16).reshape(dp_count, rows, fsdp_count, cols)]
    unnamed x219 -> x172, local copies, waits for them, and re-layouts: 57.6 us -> 25 us
    dot_general x1, matrix products: 17.2 us -> 46.4 us  [body(): jnp.dot(normed_two, weight_up, preferred_element_type=jnp.float32)]
  transfers between devices with their start and end apart: 23 -> 4, of which waited for: 17 -> 2; matrix products, arithmetic and copies ran while one was open for 30% -> 30% of each run, Pallas kernels for 0% -> 0%
where the time goes in v1:
time: 1080 us; the launch traced here: 1070 us
  matrix products  328 us (30%)
  waiting for transfers between devices  235 us (22%)
  local copies, waits for them, and re-layouts  146 us (14%)
  Pallas kernels  131 us (12%)
  other arithmetic  124 us (11%)
  blocking collectives  88.7 us (8%)
  between operations  15 us (1%)
    reduce_scatter x4, waiting for transfers between devices, spread_grads(): lax.psum_scatter(pieces, ('dp', 'fsdp'), scatter_dimension=0, tiled=False)  235 us
    pallas_call x1, Pallas kernels, gather_weights(): pl.pallas_call(partial(gather_kernel, (dims, tuple(chunks), (0, 2, 4, 6,...  131 us
    dot_general x1, matrix products, body(): jnp.dot(normed_two, weight_up, preferred_element_type=jnp.float32)  46.4 us
    unnamed x1, blocking collectives  45.3 us
    reshape x4, local copies, waits for them, and re-layouts, spread_grads(): pieces = item.astype(jnp.bfloat16).reshape(dp_count, rows, fsdp_count, cols)  44.9 us
    all_gather x1, blocking collectives, collect(): spread = lax.all_gather(packed, ('dp', 'fsdp'), axis=0, tiled=False)  43.4 us
    convert_element_type x2, other arithmetic, body(): grad_scores = (probs * (grad_probs - delta[..., None])).astype(jnp.bfloat16)  39.3 us
    reduce_sum x3, other arithmetic, body(): jnp.sum(jnp.exp(scores - new_peak[..., None]), axis=-1)  27.6 us
  transfers between devices with their start and end apart: 4, of which 2 were waited for; matrix products, arithmetic and copies ran while one was open for 30% of the time, Pallas kernels for 0%

profile of v1, /device:TPU:0, one launch (start us, length us, event | category | flops | bytes accessed | tf_op | source)
XLA Modules:
  0.0 1067.9 jit_solution(10848989970017128847)
XLA Ops:
  8.6 6.1 concatenate.32
  14.7 43.4 %all-gather.1 = bf16[32,1,384]{2,1,0:T(2,128)(2,1)S(1)} all-gather(bf16[1,1,384]{2,1,0:T(2,128)(2,1)S(1)} %reshape.887), channel_id=2, replica_groups=mesh['dp'=8,'fsdp'=4] {'dp','fsdp'}, dimensions={0}, use_global_device_ids=true | all-gather | bytes 25344 | tf_op jit(solution)/shard_map/all_gather | solution.py:228
  60.1 3.9 copy.180
  64.0 2.9 copy.168
  66.9 7.3 multiply_sine_fusion
  76.7 7.4 copy.169
  84.1 6.1 reshape.855
  90.2 3.0 fusion.61
  95.7 131.2 %shard_map.280 = (bf16[1024,3072]{1,0:T(8,128)(2,1)}, bf16[1024,1024]{1,0:T(8,128)(2,1)}, bf16[1024,4096]{1,0:T(8,128)(2,1)}, bf16[4096,1024]{1,0:T(8,128)(2,1)}) custom-call(bf16[128,768]{1,0:T(8,128)(2,1)} %refs_0_.1, bf16[128,256]{1,0:T(8,128)(2,1)} %refs_1_.1, bf16[128,1024]{1,0:T(8,128)(2,1)} %refs_2_.1, bf16[512,256]{1,0:T(8,128)(2,1)} %refs_3_.1), custom_call_target="tpu_custom_call" | custom-call | tf_op jit(solution)/shard_map/pallas_call | solution.py:202
  226.9 13.4 %fusion.68 = (bf16[1024,3072]{1,0:T(8,128)(2,1)S(1)}, f32[1024,3072]{1,0:T(8,128)}) fusion(bf16[1024,3072]{1,0:T(8,128)(2,1)} %get-tuple-element.127, f32[1024,1024]{0,1:T(8,128)} %copy-done.1, f32[1024]{0:T(1024)S(1)} %reshape.874, f32[1024]{0:T(1024)S(1)} %reshape.873, f32[1024]{0:T(1024)S(1)} %fusion.38, f32[1024]{0:T(1024)S(1)} %broadcast_multiply_fusion.1), kind=kOutput, calls=%fused_computation.170 | convolution fusion | flops 6450839552 | bytes 29376512 | tf_op jit(solution)/shard_map/dot_general | solution.py:340
  241.6 5.1 fusion.19
  251.3 2.7 copy.170
  257.6 8.6 fusion.13
  266.2 9.2 exponential_reduce_fusion.2
  275.5 8.3 fusion.14
  283.8 7.8 fusion.15
  291.6 9.2 exponential_reduce_fusion.1
  300.8 9.3 exponential_reduce_fusion
  310.2 9.5 fusion.33
  319.6 9.2 fusion.29
  328.9 6.6 fusion.28
  337.3 5.0 fusion.69
  344.6 46.4 %multiply_convert_fusion.3 = (bf16[1024,4096]{1,0:T(8,128)(2,1)}, f32[1024,4096]{1,0:T(8,128)}, f32[1024,4096]{1,0:T(8,128)}) fusion(f32[4096]{0:T(1024)S(1)} %fusion.37, bf16[1024,4096]{1,0:T(8,128)(2,1)S(1)} %bitcast.214, bf16[1024,1024]{0,1:T(8,128)(2,1)S(1)} %add_convert_fusion.8.clone.4), kind=kOutput, calls=%fused_computation.18 | convolution fusion | flops 8866758656 | bytes 52445184 | tf_op jit(solution)/shard_map/dot_general | solution.py:401
  391.0 24.3 %convert_reduce_fusion = (f32[4096]{0:T(1024)}, bf16[1024,4096]{1,0:T(8,128)(2,1)}) fusion(f32[1024,4096]{1,0:T(8,128)} %get-tuple-element.219, bf16[4096,1024]{1,0:T(8,128)(2,1)} %get-tuple-element.130, bf16[1024,1024]{1,0:T(8,128)(2,1)S(1)} %copy-done.39, f32[1024,4096]{1,0:T(8,128)} %get-tuple-element.273, f32[4096]{0:T(1024)S(1)} %fusion.37), kind=kOutput, calls=%fused_computation.11 | convolution fusion | flops 8661233664 | bytes 52461568 | tf_op jit(solution)/shard_map/td,fd->tf/dot_general | solution.py:414
  415.3 15.7 %fusion.71 = (f32[1024]{0:T(1024)}, f32[1024,1024]{1,0:T(8,128)}) fusion(bf16[1024,4096]{1,0:T(8,128)(2,1)} %get-tuple-element.282, bf16[1024,4096]{1,0:T(8,128)(2,1)} %get-tuple-element.129), kind=kOutput, calls=%fused_computation.173 | convolution fusion | flops 8590982144 | bytes 20975616 | tf_op jit(solution)/shard_map/tf,df->td/dot_general | solution.py:419
  431.0 5.6 copy.181
  436.7 5.4 multiply_reduce_fusion.3
  448.3 3.7 convolution_convert_fusion.4
  452.0 3.3 reshape.867
  457.1 4.6 convolution_convert_fusion.3
  461.9 8.5 convolution_bitcast_fusion
  470.4 11.8 %multiply_reduce_fusion.2 = (f32[16,512]{1,0:T(8,128)S(1)}, f32[16,512,512]{1,2,0:T(8,128)}) fusion(f32[16,512,512]{1,2,0:T(8,128)} %get-tuple-element.270, f32[16,512]{1,0:T(8,128)S(1)} %copy-done.46, pred[512,512]{0,1:T(8,128)(4,1)S(1)} %copy-done.35, bf16[512,16,64]{0,2,1:T(8,128)(2,1)S(1)} %bitcast.198, bf16[512,16,64]{0,2,1:T(8,128)(2,1)S(1)} %bitcast.187), kind=kOutput, calls=%fused_computation.17 | convolution fusion | flops 557834240 | bytes 35979264 | tf_op jit(solution)/shard_map/qhd,khd->hqk/dot_general | solution.py:452
  482.3 12.4 %multiply_convert_fusion.2 = bf16[16,512,512]{1,2,0:T(8,128)(2,1)S(1)} fusion(f32[16,512,512]{1,2,0:T(8,128)} %get-tuple-element.275, f32[16,512,512]{1,2,0:T(8,128)} %get-tuple-element.270, f32[16,512]{1,0:T(8,128)S(1)} %get-tuple-element.274, f32[16,512]{1,0:T(8,128)S(1)} %copy-done.46, pred[512,512]{0,1:T(8,128)(4,1)S(1)} %copy-done.35), kind=kLoop, calls=%fused_computation.16 | loop fusion | flops 25165824 | bytes 42270720 | tf_op jit(solution)/shard_map/convert_element_type | solution.py:455
  494.7 2.6 multiply_bitcast_fusion
  499.8 8.1 fusion.72
  508.5 8.1 fusion.25
  516.6 2.8 scatter-add.30
  519.5 23.5 %multiply_reduce_fusion = (f32[16,512]{1,0:T(8,128)S(1)}, f32[16,512]{1,0:T(8,128)S(1)}, f32[16,512,512]{1,2,0:T(8,128)}) fusion(f32[16,512,512]{1,2,0:T(8,128)} %get-tuple-element.268, f32[16,512]{1,0:T(8,128)S(1)} %copy-done.44, pred[512,512]{0,1:T(8,128)(4,1)S(1)} %copy-done.29, f32[16,512,512]{1,2,0:T(8,128)} %fusion.72, ...), kind=kOutput, calls=%fused_computation.14 | convolution fusion | flops 578797568 | bytes 69828608 | tf_op jit(solution)/shard_map/qhd,khd->hqk/dot_general | solution.py:442
  543.0 26.9 %multiply_convert_fusion = (bf16[16,512,512]{1,2,0:T(8,128)(2,1)S(1)}, bf16[16,512,512]{1,2,0:T(8,128)(2,1)}) fusion(f32[16,512,512]{1,2,0:T(8,128)} %get-tuple-element.276, f32[16,512,512]{1,2,0:T(8,128)} %get-tuple-element.268, f32[16,512]{1,0:T(8,128)S(1)} %add.239, f32[16,512]{1,0:T(8,128)S(1)} %copy-done.44, pred[512,512]{0,1:T(8,128)(4,1)S(1)} %copy-done.29, ...), kind=kLoop, calls=%fused_computation.12 | loop fusion | flops 50331648 | bytes 84475904 | tf_op jit(solution)/shard_map/convert_element_type | solution.py:455
  569.9 5.0 multiply_bitcast_fusion.1
  576.7 4.1 fusion.26
  580.7 5.7 fusion.24
  588.2 3.9 convert_element_type.273
  592.0 10.5 fusion.23
  602.6 3.8 convert_reduce_fusion.3
  608.9 13.5 %convolution_convert_fusion.2 = bf16[1024,3072]{1,0:T(8,128)(2,1)} fusion(bf16[1024,1024]{0,1:T(8,128)(2,1)} %bitcast.201, bf16[1024,1024]{0,1:T(8,128)(2,1)} %bitcast.199, bf16[1024,1024]{0,1:T(8,128)(2,1)} %bitcast.192, f32[1024,1024]{0,1:T(8,128)} %copy-done.1, f32[1024]{0:T(1024)S(1)} %copy-done.75, f32[1024]{0:T(1024)S(1)} %copy-done.53, ...), kind=kOutput, calls=%fused_computation.52 | convolution fusion | flops 6469713920 | bytes 16793600 | tf_op jit(solution)/shard_map/td,te->de/dot_general | solution.py:484
  622.4 12.3 %reshape.865 = bf16[8,128,4,768]{3,2,1,0:T(4,128)(2,1)} reshape(bf16[1024,3072]{1,0:T(8,128)(2,1)} %convolution_convert_fusion.2) | data formatting | bytes 12582912 | tf_op jit(solution)/shard_map/reshape | solution.py:254
  634.7 6.8 copy.194
  641.7 14.7 %convolution_convert_fusion = bf16[4096,1024]{1,0:T(8,128)(2,1)} fusion(bf16[1024,4096]{1,0:T(8,128)(2,1)} %get-tuple-element.218, bf16[1024,1024]{1,0:T(8,128)(2,1)S(1)} %copy-done.40), kind=kOutput, calls=%fused_computation.47 | convolution fusion | flops 8594128896 | bytes 18874368 | tf_op jit(solution)/shard_map/tf,td->fd/dot_general | solution.py:412
  656.4 14.7 %reshape.871 = bf16[8,512,4,256]{3,2,1,0:T(4,128)(2,1)} reshape(bf16[4096,1024]{1,0:T(8,128)(2,1)} %convolution_convert_fusion) | data formatting | bytes 16777216 | tf_op jit(solution)/shard_map/reshape | solution.py:254
  671.1 8.5 copy.197
  680.3 15.8 %convolution_convert_fusion.1 = bf16[1024,4096]{1,0:T(8,128)(2,1)} fusion(bf16[1024,4096]{1,0:T(8,128)(2,1)} %get-tuple-element.282, f32[1024,1024]{0,1:T(8,128)} %copy-done.5, f32[1024]{0:T(1024)S(1)} %copy-done.71, f32[1024]{0:T(1024)S(1)} %copy-done.56, f32[1024]{0:T(1024)S(1)} %copy-done.59, f32[1024]{0:T(1024)S(1)} %copy-done.51), kind=kOutput, calls=%fused_computation.48 | convolution fusion | flops 8599371776 | bytes 20987904 | tf_op jit(solution)/shard_map/td,tf->df/dot_general | solution.py:417
  696.1 14.5 %reshape.869 = bf16[8,128,4,1024]{3,2,1,0:T(4,128)(2,1)} reshape(bf16[1024,4096]{1,0:T(8,128)(2,1)} %convolution_convert_fusion.1) | data formatting | bytes 16777216 | tf_op jit(solution)/shard_map/reshape | solution.py:254
  710.6 9.9 copy.196
  721.3 15.9 %add_convert_fusion.1 = bf16[1024,1024]{0,1:T(8,128)(2,1)} fusion(f32[1024,1024]{0,1:T(8,128)} %copy-done.5, f32[1024]{0:T(1024)S(1)} %reshape.881, bf16[1024,4096]{1,0:T(8,128)(2,1)} %get-tuple-element.218, bf16[4096,1024]{1,0:T(8,128)(2,1)} %get-tuple-element.130), kind=kOutput, calls=%fused_computation.69 | convolution fusion | flops 8593080320 | bytes 23072768 | tf_op jit(solution)/shard_map/dot_general | solution.py:407
  737.2 4.0 copy.198
  741.9 12.0 %fusion.70 = (f32[1024]{0:T(1024)S(1)}, f32[1024,1024]{1,0:T(8,128)}) fusion(bf16[1024,3072]{1,0:T(8,128)(2,1)} %get-tuple-element.127, bf16[1024,1024]{0,1:T(8,128)(2,1)} %bitcast.202, bf16[1024,1024]{0,1:T(8,128)(2,1)} %bitcast.200, bf16[1024,1024]{0,1:T(8,128)(2,1)S(1)} %bitcast.193), kind=kOutput, calls=%fused_computation.172 | convolution fusion | flops 6462372864 | bytes 16781312 | tf_op jit(solution)/shard_map/te,de->td/dot_general | solution.py:489
  753.9 5.4 copy.191
  759.3 4.2 multiply_reduce_fusion.5
  767.4 2.6 convert_reduce_fusion.1
  770.2 2.5 copy.199
  772.8 45.3 %all-reduce.2 = f32[32,384]{1,0:T(8,128)S(1)} all-reduce(f32[32,384]{1,0:T(8,128)S(1)} %concatenate.35), channel_id=3, replica_groups=mesh['dp'=8,'fsdp'=4] {'dp','fsdp'}, use_global_device_ids=true, to_apply=%region_26.27.clone | all-reduce | flops 12288 | bytes 98304
  822.5 88.5 %reduce-scatter.11.cloned.1.call-done = bf16[1,512,256]{2,1,0:T(8,128)(2,1)} async-done(((bf16[32,512,256]{2,1,0:T(8,128)(2,1)}), bf16[1,512,256]{2,1,0:T(8,128)(2,1)}) %reduce-scatter.11.cloned.1.call-update) | async-done | bytes 262160 | tf_op jit(solution)/shard_map/reduce_scatter | solution.py:256
  912.9 146.5 %reduce-scatter.9.cloned.1.call-done = bf16[1,128,1024]{2,1,0:T(8,128)(2,1)} async-done(((bf16[32,128,1024]{2,1,0:T(8,128)(2,1)}), bf16[1,128,1024]{2,1,0:T(8,128)(2,1)}) %reduce-scatter.9.cloned.1.call-update) | async-done | bytes 262160 | tf_op jit(solution)/shard_map/reduce_scatter | solution.py:256
  (245 shorter events, 53.4 us)
Async XLA Ops:
  7.2 812.1 %reduce-scatter.7.cloned.1.call-start = ((), (), s32[]{:S(2)}) async-start(), calls=%async_computation.5 | async-start | bytes 2162688 | tf_op jit(solution)/shard_map/reduce_scatter | solution.py:256
  59.6 284.2 %copy-start.54 = (f32[1024]{0:T(1024)}, f32[1024]{0:T(1024)S(1)}, u32[]{:S(2)}) copy-start(f32[1024]{0:T(1024)S(1)} %reshape.878) | copy-start | bytes 12292
  59.7 167.2 %copy-start.52 = (f32[1024]{0:T(1024)}, f32[1024]{0:T(1024)S(1)}, u32[]{:S(2)}) copy-start(f32[1024]{0:T(1024)S(1)} %reshape.873) | copy-start | bytes 12292
  59.8 284.1 %copy-start.70 = (f32[1024]{0:T(1024)}, f32[1024]{0:T(1024)S(1)}, u32[]{:S(2)}) copy-start(f32[1024]{0:T(1024)S(1)} %reshape.879) | copy-start | bytes 12292
  59.9 167.0 %copy-start.74 = (f32[1024]{0:T(1024)}, f32[1024]{0:T(1024)S(1)}, u32[]{:S(2)}) copy-start(f32[1024]{0:T(1024)S(1)} %reshape.874) | copy-start | bytes 12292
  93.2 147.0 %copy-start.47 = (f32[1024]{0:T(1024)}, f32[1024]{0:T(1024)S(1)}, u32[]{:S(2)}) copy-start(f32[1024]{0:T(1024)S(1)} %broadcast_multiply_fusion.1) | copy-start | bytes 12292
  95.7 144.6 %copy-start.65 = (f32[1024]{0:T(1024)}, f32[1024]{0:T(1024)S(1)}, u32[]{:S(2)}) copy-start(f32[1024]{0:T(1024)S(1)} %multiply_reduce_fusion.8) | copy-start | bytes 12292
  95.7 144.6 %copy-start.61 = (f32[1024]{0:T(1024)}, f32[1024]{0:T(1024)S(1)}, u32[]{:S(2)}) copy-start(f32[1024]{0:T(1024)S(1)} %fusion.38) | copy-start | bytes 12292
  241.0 42.7 %copy-start.19 = (bf16[512,1024]{0,1:T(8,128)(2,1)}, bf16[512,1024]{0,1:T(8,128)(2,1)S(1)}, u32[]{:S(2)}) copy-start(bf16[512,1024]{0,1:T(8,128)(2,1)S(1)} %copy.175) | copy-start | bytes 3145732
  241.6 33.9 %copy-start.7 = (bf16[512,1024]{0,1:T(8,128)(2,1)}, bf16[512,1024]{0,1:T(8,128)(2,1)S(1)}, u32[]{:S(2)}) copy-start(bf16[512,1024]{0,1:T(8,128)(2,1)S(1)} %copy.172) | copy-start | bytes 3145732
  251.3 32.5 %copy-start.12 = (bf16[512,1024]{0,1:T(8,128)(2,1)}, bf16[512,1024]{0,1:T(8,128)(2,1)S(1)}, u32[]{:S(2)}) copy-start(bf16[512,1024]{0,1:T(8,128)(2,1)S(1)} %copy.174) | copy-start | bytes 3145732
  257.6 8.6 copy-start.33
  257.6 71.2 %copy-start.28 = (pred[512,512]{0,1:T(8,128)(4,1)}, pred[512,512]{0,1:T(8,128)(4,1)S(1)}, u32[]{:S(2)}) copy-start(pred[512,512]{0,1:T(8,128)(4,1)S(1)} %get-tuple-element.258) | copy-start | bytes 786436
  275.4 44.2 %copy-start.45 = (f32[16,512]{1,0:T(8,128)}, f32[16,512]{1,0:T(8,128)S(1)}, u32[]{:S(2)}) copy-start(f32[16,512]{1,0:T(8,128)S(1)} %log_add_fusion.1) | copy-start | bytes 98308
  283.8 7.8 copy-start.30
  300.8 9.3 copy-start.23
  300.8 9.3 copy-start.31
  310.1 18.8 %copy-start.43 = (f32[16,512]{1,0:T(8,128)}, f32[16,512]{1,0:T(8,128)S(1)}, u32[]{:S(2)}) copy-start(f32[16,512]{1,0:T(8,128)S(1)} %log_add_fusion) | copy-start | bytes 98308
  310.1 9.5 copy-start.34
  310.1 18.7 %slice-start = ((s8[16777216]{0:T(1024)(128)(4,1)}), s8[4194304]{0:T(1024)(128)(4,1)S(1)}, s32[]{:S(2)}) async-start(s8[16777216]{0:T(1024)(128)(4,1)} %bitcast.163), calls=%async_computation.8 | async-start | bytes 8388608
  310.1 18.7 %slice-start.1 = ((s8[16777216]{0:T(1024)(128)(4,1)}), s8[4194304]{0:T(1024)(128)(4,1)S(1)}, s32[]{:S(2)}) async-start(s8[16777216]{0:T(1024)(128)(4,1)} %bitcast.163), calls=%async_computation.9 | async-start | bytes 8388608
  319.6 9.2 slice-start.2
  319.6 9.2 slice-start.3
  319.6 9.2 copy-start.36
  328.9 8.4 copy-start.2
  337.3 7.2 slice-start.4
  337.3 7.2 slice-start.5
  342.4 48.6 %copy-start.5 = (f32[1024,1024]{0,1:T(8,128)}, f32[1024,1024]{0,1:T(8,128)S(1)}, u32[]{:S(2)}) copy-start(f32[1024,1024]{0,1:T(8,128)S(1)} %get-tuple-element.272) | copy-start | bytes 12582916
  342.4 48.6 %copy-start.49 = (f32[1024]{0:T(1024)}, f32[1024]{0:T(1024)S(1)}, u32[]{:S(2)}) copy-start(f32[1024]{0:T(1024)S(1)} %broadcast_multiply_fusion) | copy-start | bytes 12292
  343.9 47.1 %copy-start.57 = (f32[1024]{0:T(1024)}, f32[1024]{0:T(1024)S(1)}, u32[]{:S(2)}) copy-start(f32[1024]{0:T(1024)S(1)} %fusion.39) | copy-start | bytes 12292
  344.6 46.4 %copy-start.39 = (bf16[1024,1024]{1,0:T(8,128)(2,1)S(1)}, bf16[1024,1024]{1,0:T(8,128)(2,1)}, u32[]{:S(2)}) copy-start(bf16[1024,1024]{1,0:T(8,128)(2,1)} %param.38) | copy-start | bytes 6291460
  431.0 5.6 copy-start.50
  431.0 5.6 copy-start.55
  431.0 5.6 copy-start.58
  431.0 11.1 %copy-start.68 = (f32[1024]{0:T(1024)S(1)}, f32[1024]{0:T(1024)}, u32[]{:S(2)}) copy-start(f32[1024]{0:T(1024)} %copy-done.67) | copy-start | bytes 12292
  436.7 5.9 copy-start.11
  442.6 5.7 copy-start.42
  457.1 363.7 %reduce-scatter.5.cloned.1.call-start = ((), (), s32[]{:S(2)}) async-start(), calls=%async_computation.4 | async-start | bytes 6488064 | tf_op jit(solution)/shard_map/reduce_scatter | solution.py:256
  461.9 57.6 %copy-start.21 = (bf16[512,1024]{0,1:T(8,128)(2,1)}, bf16[512,1024]{0,1:T(8,128)(2,1)S(1)}, u32[]{:S(2)}) copy-start(bf16[512,1024]{0,1:T(8,128)(2,1)S(1)} %get-tuple-element.228) | copy-start | bytes 3145732
  461.9 8.5 copy-start.24
  482.3 12.4 %copy-start.25 = (bf16[512,1024]{0,1:T(8,128)(2,1)S(1)}, bf16[512,1024]{0,1:T(8,128)(2,1)}, u32[]{:S(2)}) copy-start(bf16[512,1024]{0,1:T(8,128)(2,1)} %copy.171) | copy-start | bytes 3145732
  497.3 19.3 %copy-start.16 = (f32[512,16,64]{0,2,1:T(8,128)}, f32[512,16,64]{0,2,1:T(8,128)S(1)}, u32[]{:S(2)}) copy-start(f32[512,16,64]{0,2,1:T(8,128)S(1)} %multiply_bitcast_fusion) | copy-start | bytes 6291460
  499.8 8.7 copy-start.32
  499.8 8.7 copy-start.44
  508.5 11.0 %copy-start.29 = (pred[512,512]{0,1:T(8,128)(4,1)S(1)}, pred[512,512]{0,1:T(8,128)(4,1)}, u32[]{:S(2)}) copy-start(pred[512,512]{0,1:T(8,128)(4,1)} %copy-done.28) | copy-start | bytes 786436
  508.5 11.0 %copy-start.37 = (bf16[512,1024]{0,1:T(8,128)(2,1)S(1)}, bf16[512,1024]{0,1:T(8,128)(2,1)}, u32[]{:S(2)}) copy-start(bf16[512,1024]{0,1:T(8,128)(2,1)} %copy.177) | copy-start | bytes 3145732
  516.6 26.4 %copy-start.18 = (f32[1024,16,64]{0,2,1:T(8,128)}, f32[1024,16,64]{0,2,1:T(8,128)S(1)}, u32[]{:S(2)}) copy-start(f32[1024,16,64]{0,2,1:T(8,128)S(1)} %fusion.25) | copy-start | bytes 12582916
  569.9 5.8 copy-start
  569.9 6.1 copy-start.13
  569.9 6.7 copy-start.17
  580.7 5.7 copy-start.27
  592.0 14.3 %copy-start.20 = (bf16[512,1024]{0,1:T(8,128)(2,1)S(1)}, bf16[512,1024]{0,1:T(8,128)(2,1)}, u32[]{:S(2)}) copy-start(bf16[512,1024]{0,1:T(8,128)(2,1)} %copy-done.19) | copy-start | bytes 3145732
  634.7 6.9 copy-start.40
  641.6 269.5 %reduce-scatter.11.cloned.1.call-start = ((), (), s32[]{:S(2)}) async-start(), calls=%async_computation.7 | async-start | bytes 8650752 | tf_op jit(solution)/shard_map/reduce_scatter | solution.py:256
  679.7 379.7 %reduce-scatter.9.cloned.1.call-start = ((), (), s32[]{:S(2)}) async-start(), calls=%async_computation.6 | async-start | bytes 8650752 | tf_op jit(solution)/shard_map/reduce_scatter | solution.py:256
  721.3 19.8 %copy-start.76 = (f32[1024]{0:T(1024)S(1)}, f32[1024]{0:T(1024)}, u32[]{:S(2)}) copy-start(f32[1024]{0:T(1024)} %get-tuple-element.279) | copy-start | bytes 12292
  721.3 19.9 %copy-start.72 = (f32[1024]{0:T(1024)S(1)}, f32[1024]{0:T(1024)}, u32[]{:S(2)}) copy-start(f32[1024]{0:T(1024)} %get-tuple-element.208) | copy-start | bytes 12292
  721.3 20.0 %copy-start.69 = (f32[1024]{0:T(1024)S(1)}, f32[1024]{0:T(1024)}, u32[]{:S(2)}) copy-start(f32[1024]{0:T(1024)} %get-tuple-element.212) | copy-start | bytes 12292
  721.3 20.1 %copy-start.26 = (bf16[1024,16,64]{0,2,1:T(8,128)(2,1)S(1)}, bf16[1024,16,64]{0,2,1:T(8,128)(2,1)}, u32[]{:S(2)}) copy-start(bf16[1024,16,64]{0,2,1:T(8,128)(2,1)} %fusion.27) | copy-start | bytes 6291460
  753.9 9.7 copy-start.66
  759.3 5.9 copy-start.4
  759.3 8.0 copy-start.10
  759.3 8.0 copy-start.15
  759.3 8.0 copy-start.64
  (23 other events, 65.1 us)
Sparse Core Ops, SparseCore 0:
  457.2 140.9 reduce-scatter.6
  641.7 117.5 reduce-scatter.4
  761.7 149.3 reduce-scatter.10
  913.2 146.0 reduce-scatter.8

commit v2 on v1

--- a/solution.py
+++ b/solution.py
@@ -10,7 +10,6 @@
 
 MESH = pl.DeviceIdType.MESH
 
-HEADS = 16
 HEAD_DIM = 64
 
 
@@ -24,15 +23,16 @@
     return jnp.stack([jnp.sin(angles), jnp.cos(angles)], axis=-1).reshape(places.shape + (width,))
 
 
-def affine_norm(values, gain, shift):
+def standardize(values):
     centered = values - jnp.mean(values, axis=-1, keepdims=True)
     spread = jnp.mean(centered * centered, axis=-1, keepdims=True)
-    return centered * lax.rsqrt(spread + eps) * gain + shift
+    rate = lax.rsqrt(spread + eps)
+    return centered * rate, rate
 
 
 def grid_of(dp_count, fsdp_count):
     across = 1
-    while across * across * 2 <= dp_count:
+    while across * across * 8 <= dp_count:
         across *= 2
     while dp_count % across:
         across //= 2
@@ -239,40 +239,558 @@
     return tuple(found)
 
 
-def spread_grads(grads):
+def attend(query, keys, values, start):
+    length = query.shape[0]
+    block = min(256, length)
+    lane = lax.broadcasted_iota(jnp.int32, (block, 2 * HEAD_DIM), 1)
+    factor = math.log2(math.e) / math.sqrt(HEAD_DIM)
+    parts = []
+    for at in range(length // block):
+        rows = slice(at * block, (at + 1) * block)
+        span = (at + 1) * block
+        asked = query[rows, :]
+        seen = keys[:span, :]
+        held = values[:span, :]
+        row = at * block + lax.broadcasted_iota(jnp.int32, (block, span), 0)
+        col = lax.broadcasted_iota(jnp.int32, (block, span), 1)
+        allowed = (col <= row) & (col >= start[rows, :])
+        found = []
+        for side in range(2):
+            mine = jnp.where((lane // HEAD_DIM) == side, asked, jnp.zeros_like(asked))
+            scores = lax.dot_general(
+                mine, seen, (((1,), (1,)), ((), ())), preferred_element_type=jnp.float32
+            )
+            scores = jnp.where(allowed, scores * factor, -1e30)
+            weight = jnp.exp2(scores - jnp.max(scores, axis=1, keepdims=True))
+            total = jnp.sum(weight, axis=1, keepdims=True)
+            mixed = jnp.dot(
+                weight.astype(jnp.bfloat16), held, preferred_element_type=jnp.float32
+            )
+            found.append(mixed / total)
+        parts.append(jnp.where(lane < HEAD_DIM, found[0], found[1]).astype(jnp.bfloat16))
+    return parts
+
+
+def attention_kernel(query, keys, values, start, mixed):
+    block = min(256, query.shape[0])
+    for at, part in enumerate(attend(query, keys, values, start)):
+        mixed[at * block : (at + 1) * block, :] = part
+
+
+def attention(projected, start):
+    length, triple = projected.shape
+    width = triple // 3
+    pairs = width // (2 * HEAD_DIM)
+    return pl.pallas_call(
+        attention_kernel,
+        grid=(pairs,),
+        out_shape=jax.ShapeDtypeStruct((length, width), jnp.bfloat16),
+        in_specs=[
+            pl.BlockSpec((length, 2 * HEAD_DIM), lambda h: (0, h)),
+            pl.BlockSpec((length, 2 * HEAD_DIM), lambda h: (0, pairs + h)),
+            pl.BlockSpec((length, 2 * HEAD_DIM), lambda h: (0, 2 * pairs + h)),
+            pl.BlockSpec((length, 1), lambda h: (0, 0)),
+        ],
+        out_specs=pl.BlockSpec((length, 2 * HEAD_DIM), lambda h: (0, h)),
+        name="attention",
+    )(projected, projected, projected, start)
+
+
+def matmul(left, right, contract):
+    return lax.dot_general(
+        left, right, ((contract[:1], contract[1:]), ((), ())), preferred_element_type=jnp.float32
+    )
+
+
+def backward_kernel(dims, *refs):
+    (
+        place, cot_hbm, act_hbm, slope_hbm, two_hbm, unit_two, rate_two, mixed_hbm, qkv_hbm,
+        one_hbm, unit_one, rate_one, gains, in_hbm, out_hbm, up_hbm, down_hbm,
+        result, owned, sums,
+        grads, twin_in, a_in, b_in, z_in,
+        v_own, v_hold, v_twin, v_a, v_b, v_z,
+        cot, left, right, unit, wide, total, second, branch,
+        load, t_send, t_recv, a_send, a_recv, b_send, b_recv, z_send, z_recv,
+        v_send, v_recv,
+    ) = refs
+    deep, across, down, cores = dims
+    side = across
+    length, width = cot.shape
+    hidden = wide.shape[1]
+    piece, gw = owned.shape[1], owned.shape[2]
+    fsdp = down * cores
+    rows_each = 2 * piece
+    outer = lax.axis_index("dp")
+    inner = lax.axis_index("fsdp")
+    z, x, y, c = outer // across, outer % across, inner // cores, inner % cores
+    a = (1 - c) * x + c * y
+    b = (1 - c) * y + c * x
+    block = min(256, length)
+    steps = length // block
+
+    def device(zz, xx, yy, cc):
+        return (zz * across + xx, yy * cores + cc)
+
+    twin = device(z, x, y, 1 - c)
+
+    def a_peer(k):
+        to = (a + k) % side
+        return device(z, (1 - c) * to + c * x, (1 - c) * y + c * to, c)
+
+    def b_peer(k):
+        to = (b + k) % side
+        return device(z, (1 - c) * x + c * to, (1 - c) * to + c * y, c)
+
+    def z_peer(k):
+        return device((z + k) % deep, x, y, c)
+
+    barrier = pltpu.get_barrier_semaphore()
+    everyone = [twin]
+    everyone += [a_peer(k) for k in range(1, side)] + [b_peer(k) for k in range(1, side)]
+    everyone += [z_peer(k) for k in range(1, deep)]
+    for peer in everyone:
+        pl.semaphore_signal(barrier, inc=1, device_id=peer, device_id_type=MESH)
+    pl.semaphore_wait(barrier, len(everyone))
+
+    def copy(source, target, send, recv, peer):
+        return pltpu.make_async_remote_copy(
+            src_ref=source, dst_ref=target, send_sem=send, recv_sem=recv,
+            device_id=peer, device_id_type=MESH,
+        )
+
+    def t_copy(i):
+        return copy(
+            grads.at[(i // 2) % 2, i % 2, 1 - c], twin_in.at[i], t_send.at[i], t_recv.at[i], twin
+        )
+
+    def a_copy(i, k):
+        return copy(
+            twin_in.at[i, (a + k) % side], a_in.at[i, k - 1],
+            a_send.at[i, k - 1], a_recv.at[i, k - 1], a_peer(k),
+        )
+
+    def b_copy(i, k):
+        return copy(
+            a_in.at[i, 0, (b + k) % side], b_in.at[i, k - 1],
+            b_send.at[i, k - 1], b_recv.at[i, k - 1], b_peer(k),
+        )
+
+    def z_copy(i, k):
+        return copy(
+            b_in.at[i, 0, (z + k) % deep], z_in.at[i, k - 1],
+            z_send.at[i, k - 1], z_recv.at[i, k - 1], z_peer(k),
+        )
+
+    def first(i):
+        t_copy(i).start()
+
+    def second_stage(i):
+        t_copy(i).wait()
+        twin_in[i] = twin_in[i] + grads[(i // 2) % 2, i % 2, c]
+        for k in range(1, side):
+            a_copy(i, k).start()
+
+    def third(i):
+        for k in range(1, side):
+            a_copy(i, k).wait()
+        found = twin_in[i, a]
+        for k in range(1, side):
+            found = found + a_in[i, k - 1]
+        a_in[i, 0] = found
+        for k in range(1, side):
+            b_copy(i, k).start()
+
+    def fourth(i):
+        for k in range(1, side):
+            b_copy(i, k).wait()
+        found = a_in[i, 0, b]
+        for k in range(1, side):
+            found = found + b_in[i, k - 1]
+        b_in[i, 0] = found
+        for k in range(1, deep):
+            z_copy(i, k).start()
+
+    def fifth(i):
+        for k in range(1, deep):
+            z_copy(i, k).wait()
+        found = b_in[i, 0, z].astype(jnp.float32)
+        for k in range(1, deep):
+            found = found + z_in[i, k - 1].astype(jnp.float32)
+        owned[i] = found
+
+    stages = (first, second_stage, third, fourth, fifth)
+
+    def advance(step, low, high):
+        for at in reversed(range(5)):
+            i = step - at
+            if isinstance(step, int):
+                if low <= i < high:
+                    stages[at](i)
+            else:
+                @pl.when((i >= low) & (i < high))
+                def _(i=i, at=at):
+                    stages[at](i)
+
+    def fetch(source, target, at):
+        return pltpu.make_async_copy(source, target, load.at[at])
+
+    def tile(ref, j):
+        return ref.at[:, pl.ds(pl.multiple_of(j * width, width), width)]
+
+    def band(ref, j):
+        return ref.at[pl.ds(pl.multiple_of(j * width, width), width), :]
+
+    def rows_at(m):
+        return pl.ds(pl.multiple_of(m * block, block), block)
+
+    def make_unit(slot, source, strip):
+        @pl.loop(0, width // block)
+        def _(m):
+            lhs = left[rows_at(m), :]
+            for f in range(fsdp):
+                yy, cc = f // cores, f % cores
+                found = matmul(lhs, source[:, pl.ds(strip(f), gw)], (1, 0)).astype(jnp.bfloat16)
+                for q in range(block // piece):
+                    owner = m * (block // rows_each) + q // 2
+                    zz, xx = owner // across, owner % across
+                    part = found[q * piece : (q + 1) * piece, :]
+                    if cc == 0:
+                        grads[slot, q % 2, 0, xx, yy, zz] = part
+                    else:
+                        grads[slot, q % 2, 1, yy, xx, zz] = part
+
+    def columns(value):
+        return jnp.sum(value, axis=0, keepdims=True)
+
+    fetch(cot_hbm, cot, 0).start()
+    fetch(band(act_hbm, 0), left, 1).start()
+    fetch(band(down_hbm, 0), right, 2).start()
+    fetch(slope_hbm, wide, 3).start()
+    fetch(unit_two, unit, 4).start()
+    v_own[...] = jnp.zeros_like(v_own)
+    total[...] = jnp.zeros_like(total)
+    fetch(cot_hbm, cot, 0).wait()
+
+    @pl.loop(0, 4)
+    def _(j):
+        fetch(band(act_hbm, j), left, 1).wait()
+        make_unit(j % 2, cot, lambda f: f * gw)
+
+        @pl.when(j < 3)
+        def _():
+            fetch(band(act_hbm, (j + 1) % 4), left, 1).start()
+
+        @pl.when(j == 3)
+        def _():
+            fetch(two_hbm, left, 1).start()
+
+        advance(2 * j, 0, 18)
+        fetch(band(down_hbm, j), right, 2).wait()
+
+        @pl.when(j == 0)
+        def _():
+            fetch(slope_hbm, wide, 3).wait()
+
+        span = pl.ds(pl.multiple_of(j * width, width), width)
+
+        @pl.loop(0, steps)
+        def _(m):
+            found = matmul(cot[rows_at(m), :], right[...], (1, 1))
+            found = (found * wide[rows_at(m), span].astype(jnp.float32)).astype(jnp.bfloat16)
+            wide[rows_at(m), span] = found
+            v_own[pl.ds(8 + j, 1), :] += columns(found.astype(jnp.float32))
+
+        @pl.when(j < 3)
+        def _():
+            fetch(band(down_hbm, (j + 1) % 4), right, 2).start()
+
+        @pl.when(j == 3)
+        def _():
+            fetch(tile(up_hbm, 0), right, 2).start()
+
+        advance(2 * j + 1, 0, 18)
+
+    fetch(two_hbm, left, 1).wait()
+    each_up = hidden // fsdp
+
+    @pl.loop(0, 4)
+    def _(j):
+        make_unit(j % 2, wide, lambda f: pl.multiple_of(f * each_up + j * gw, 128))
+        advance(8 + 2 * j, 0, 18)
+        fetch(tile(up_hbm, j), right, 2).wait()
+        span = pl.ds(pl.multiple_of(j * width, width), width)
+
+        @pl.loop(0, steps)
+        def _(m):
+            total[rows_at(m), :] += matmul(wide[rows_at(m), span], right[...], (1, 1))
+
+        @pl.when(j < 3)
+        def _():
+            fetch(tile(up_hbm, (j + 1) % 4), right, 2).start()
+
+        @pl.when(j == 3)
+        def _():
+            fetch(out_hbm, right, 2).start()
+
+        advance(9 + 2 * j, 0, 18)
+
+    triple = qkv_hbm.shape[1]
+    packed = wide.at[:, pl.ds(0, triple)]
+    fetch(mixed_hbm, left, 1).start()
+    fetch(qkv_hbm, packed, 3).start()
+    fetch(unit_two, unit, 4).wait()
+
+    def norm_back(rate, gain, finish):
+        @pl.loop(0, steps)
+        def _(m):
+            grad = total[rows_at(m), :]
+            normal = unit[rows_at(m), :].astype(jnp.float32)
+            scaled = grad * gain
+            mean = jnp.mean(scaled, axis=1, keepdims=True)
+            tilt = jnp.mean(scaled * normal, axis=1, keepdims=True)
+            finish(m, grad, normal, rate[rows_at(m), :] * (scaled - mean - normal * tilt))
+
+    def finish_two(m, grad, normal, moved):
+        incoming = cot[rows_at(m), :].astype(jnp.float32)
+        found = incoming + moved
+        second[rows_at(m), :] = found
+        low = found.astype(jnp.bfloat16)
+        branch[rows_at(m), :] = low
+        v_own[4:5, :] += columns(low.astype(jnp.float32))
+        v_own[5:6, :] += columns(grad * normal)
+        v_own[6:7, :] += columns(grad)
+        v_own[7:8, :] += columns(incoming)
+
+    norm_back(rate_two, gains[1:2, :], finish_two)
+    fetch(unit_one, unit, 4).start()
+    fetch(mixed_hbm, left, 1).wait()
+    make_unit(0, branch, lambda f: f * gw)
+    fetch(one_hbm, left, 1).start()
+    advance(16, 0, 18)
+    fetch(out_hbm, right, 2).wait()
+
+    @pl.loop(0, steps)
+    def _(m):
+        found = matmul(branch[rows_at(m), :], right[...], (1, 1))
+        branch[rows_at(m), :] = found.astype(jnp.bfloat16)
+
+    fetch(tile(in_hbm, 0), right, 2).start()
+    advance(17, 0, 18)
+    fetch(qkv_hbm, packed, 3).wait()
+    pairs = width // (2 * HEAD_DIM)
+    scale = 1.0 / math.sqrt(HEAD_DIM)
+    factor = scale * math.log2(math.e)
+    lane = lax.broadcasted_iota(jnp.int32, (block, 2 * HEAD_DIM), 1)
+
+    @pl.loop(0, pairs)
+    def _(j):
+        pair = 2 * HEAD_DIM
+        at_q = pl.ds(pl.multiple_of(j * pair, pair), pair)
+        at_k = pl.ds(pl.multiple_of(width + j * pair, pair), pair)
+        at_v = pl.ds(pl.multiple_of(2 * width + j * pair, pair), pair)
+        sum_q = jnp.zeros((1, pair), jnp.float32)
+        for at in range(steps):
+            rows = pl.ds(at * block, block)
+            span = (at + 1) * block
+            asked = wide[rows, at_q]
+            given = branch[rows, at_q]
+            seen = wide[pl.ds(0, span), at_k]
+            held = wide[pl.ds(0, span), at_v]
+            col = at * block + lax.broadcasted_iota(jnp.int32, (span, block), 1)
+            row = lax.broadcasted_iota(jnp.int32, (span, block), 0)
+            begin = at * block + lax.broadcasted_iota(jnp.int32, (1, block), 1)
+            begin = begin - place[:, pl.ds(at * block, block)]
+            allowed = (row <= col) & (row >= begin)
+            grad_q = []
+            grad_k = None
+            grad_v = None
+            for half in range(2):
+                keep = (lane // HEAD_DIM) == half
+                mine = jnp.where(keep, asked, jnp.zeros_like(asked))
+                ours = jnp.where(keep, given, jnp.zeros_like(given))
+                scores = matmul(seen, mine, (1, 1))
+                scores = jnp.where(allowed, scores * factor, -1e30)
+                probs = jnp.exp2(scores - jnp.max(scores, axis=0, keepdims=True))
+                probs = probs * (1.0 / columns(probs))
+                grad_p = matmul(held, ours, (1, 1))
+                delta = columns(probs * grad_p)
+                grad_s = (probs * (grad_p - delta)).astype(jnp.bfloat16)
+                part_v = matmul(probs.astype(jnp.bfloat16), ours, (1, 0))
+                part_k = matmul(grad_s, mine, (1, 0))
+                grad_q.append(matmul(grad_s, seen, (0, 0)))
+                grad_v = part_v if grad_v is None else grad_v + part_v
+                grad_k = part_k if grad_k is None else grad_k + part_k
+            found = jnp.where(lane < HEAD_DIM, grad_q[0], grad_q[1]) * scale
+            found = found.astype(jnp.bfloat16)
+            wide[rows, at_q] = found
+            sum_q = sum_q + columns(found.astype(jnp.float32))
+            if at:
+                old = pl.ds(0, at * block)
+                total[old, 0:pair] += grad_k[: at * block, :]
+                total[old, pair : 2 * pair] += grad_v[: at * block, :]
+            total[rows, 0:pair] = grad_k[at * block :, :]
+            total[rows, pair : 2 * pair] = grad_v[at * block :, :]
+        wide[:, at_k] = (total[:, 0:pair] * scale).astype(jnp.bfloat16)
+        low = total[:, pair : 2 * pair].astype(jnp.bfloat16)
+        wide[:, at_v] = low
+        v_own[2:3, at_q] = sum_q
+        v_own[3:4, at_q] = columns(low.astype(jnp.float32))
+        advance(18 + j, 0, 18)
+
+    total[...] = jnp.zeros_like(total)
+    each_in = triple // fsdp
+    fetch(one_hbm, left, 1).wait()
+    for j in range(3):
+        make_unit((9 + j) % 2, wide, lambda f: f * each_in + j * gw)
+        advance(18 + 2 * j, 18, 24)
+        if j:
+            advance(18 + 2 * j + 1, 18, 24)
+        else:
+            advance(19, 18, 24)
+    fetch(unit_one, unit, 4).wait()
+    for j in range(3):
+        fetch(tile(in_hbm, j), right, 2).wait()
+        span = pl.ds(j * width, width)
+
+        @pl.loop(0, steps)
+        def _(m):
+            total[rows_at(m), :] += matmul(wide[rows_at(m), span], right[...], (1, 1))
+
+        if j < 2:
+            fetch(tile(in_hbm, j + 1), right, 2).start()
+        advance(24 + j, 18, 24)
+
+    def finish_one(m, grad, normal, moved):
+        branch[rows_at(m), :] = (second[rows_at(m), :] + moved).astype(jnp.bfloat16)
+        v_own[0:1, :] += columns(grad * normal)
+        v_own[1:2, :] += columns(grad)
+
+    norm_back(rate_one, gains[0:1, :], finish_one)
+    fetch(branch, result, 0).start()
+
+    def small(source, target, at, peer):
+        return copy(source, target, v_send.at[at], v_recv.at[at], peer)
+
+    hops = [
+        [(v_own, v_twin, 0, twin)],
+        [(v_hold.at[0], v_a.at[k - 1], k, a_peer(k)) for k in range(1, side)],
+        [(v_hold.at[1], v_b.at[k - 1], side + k - 1, b_peer(k)) for k in range(1, side)],
+        [(v_hold.at[2], v_z.at[k - 1], 2 * side + k - 2, z_peer(k)) for k in range(1, deep)],
+    ]
+    lands = [
+        lambda: [v_own[...], v_twin[...]],
+        lambda: [v_hold[0]] + [v_a[k] for k in range(side - 1)],
+        lambda: [v_hold[1]] + [v_b[k] for k in range(side - 1)],
+        lambda: [v_hold[2]] + [v_z[k] for k in range(deep - 1)],
+    ]
+    for at in range(4):
+        for hop in hops[at]:
+            small(*hop).start()
+        if at < 1:
+            advance(27, 18, 24)
+        for hop in hops[at]:
+            small(*hop).wait()
+        found = lands[at]()
+        whole = found[0]
+        for item in found[1:]:
+            whole = whole + item
+        if at < 3:
+            v_hold[at] = whole
+        else:
+            sums[...] = whole
+    fetch(branch, result, 0).wait()
+
+
+def backward(place, cot, act, slope, two, unit_two, rate_two, mixed, qkv, one, unit_one,
+             rate_one, gains, weights):
+    dp_count, fsdp_count = lax.axis_size("dp"), lax.axis_size("fsdp")
+    dims = grid_of(dp_count, fsdp_count)
+    deep, across, down, cores = dims
+    assert across == down and cores == 2
+    length, width = cot.shape
+    hidden = slope.shape[1]
+    piece = width // dp_count // 2
+    gw = width // fsdp_count
+    count = 2 * (2 * (hidden // width) + 1 + qkv.shape[1] // width)
+    any_ = pl.BlockSpec(memory_space=pl.ANY)
+    vmem = pl.BlockSpec(memory_space=pltpu.VMEM)
+    bf16, f32 = jnp.bfloat16, jnp.float32
+    hops = 2 * side_of(dims) + deep
+    return pl.pallas_call(
+        partial(backward_kernel, dims),
+        out_shape=[
+            jax.ShapeDtypeStruct((length, width), bf16),
+            jax.ShapeDtypeStruct((count, piece, gw), f32),
+            jax.ShapeDtypeStruct((16, width), f32),
+        ],
+        in_specs=[vmem, any_, any_, any_, any_, any_, vmem, any_, any_, any_, any_, vmem, vmem]
+        + [any_] * 4,
+        out_specs=[any_, vmem, vmem],
+        scratch_shapes=[
+            pltpu.VMEM((2, 2, 2, across, down, deep, piece, gw), bf16),
+            pltpu.VMEM((count, across, down, deep, piece, gw), bf16),
+            pltpu.VMEM((count, across - 1, down, deep, piece, gw), bf16),
+            pltpu.VMEM((count, down - 1, deep, piece, gw), bf16),
+            pltpu.VMEM((count, deep - 1, piece, gw), bf16),
+            pltpu.VMEM((16, width), f32),
+            pltpu.VMEM((3, 16, width), f32),
+            pltpu.VMEM((16, width), f32),
+            pltpu.VMEM((across - 1, 16, width), f32),
+            pltpu.VMEM((down - 1, 16, width), f32),
+            pltpu.VMEM((deep - 1, 16, width), f32),
+            pltpu.VMEM((length, width), bf16),
+            pltpu.VMEM((width, width), bf16),
+            pltpu.VMEM((width, width), bf16),
+            pltpu.VMEM((length, width), bf16),
+            pltpu.VMEM((length, hidden), bf16),
+            pltpu.VMEM((length, width), f32),
+            pltpu.VMEM((length, width), f32),
+            pltpu.VMEM((length, width), bf16),
+            pltpu.SemaphoreType.DMA((5,)),
+            pltpu.SemaphoreType.DMA((count,)),
+            pltpu.SemaphoreType.DMA((count,)),
+            pltpu.SemaphoreType.DMA((count, across - 1)),
+            pltpu.SemaphoreType.DMA((count, across - 1)),
+            pltpu.SemaphoreType.DMA((count, down - 1)),
+            pltpu.SemaphoreType.DMA((count, down - 1)),
+            pltpu.SemaphoreType.DMA((count, deep - 1)),
+            pltpu.SemaphoreType.DMA((count, deep - 1)),
+            pltpu.SemaphoreType.DMA((hops,)),
+            pltpu.SemaphoreType.DMA((hops,)),
+        ],
+        compiler_params=pltpu.CompilerParams(
+            collective_id=1, has_side_effects=True, vmem_limit_bytes=67043328
+        ),
+        name="backward",
+    )(place, cot, act, slope, two, unit_two, rate_two, mixed, qkv, one, unit_one, rate_one, gains,
+      *weights)
+
+
+def side_of(dims):
+    return dims[1]
+
+
+def pick_grads(owned, sums, width, hidden):
     dp_count, fsdp_count = lax.axis_size("dp"), lax.axis_size("fsdp")
     devices = dp_count * fsdp_count
-    vectors = [item.reshape(devices, -1) for item in grads if item.ndim == 1]
-    widths = [item.shape[1] for item in vectors]
-    packed = jnp.concatenate(vectors, axis=1)
-    summed = lax.psum_scatter(packed, ("dp", "fsdp"), scatter_dimension=0, tiled=False)
-    found = []
-    start = 0
-    for item in grads:
-        if item.ndim == 2:
-            rows, cols = item.shape[0] // dp_count, item.shape[1] // fsdp_count
-            pieces = item.astype(jnp.bfloat16).reshape(dp_count, rows, fsdp_count, cols)
-            pieces = pieces.transpose(0, 2, 1, 3).reshape(devices, rows, cols)
-            owned = lax.psum_scatter(
-                pieces, ("dp", "fsdp"), scatter_dimension=0, tiled=False
-            )
-            found.append(owned.astype(jnp.float32))
-        else:
-            width = item.shape[0] // devices
-            found.append(summed[start : start + width])
-            start += width
-    return tuple(found)
-
-
-def block_scores(query_part, key_part, segment_query, segment_key, place_query, place_key):
-    scale = 1.0 / math.sqrt(HEAD_DIM)
-    raw = (
-        jnp.einsum("qhd,khd->hqk", query_part, key_part, preferred_element_type=jnp.float32) * scale
-    )
-    allowed = (segment_query[:, None] == segment_key[None, :]) & (
-        place_key[None, :] <= place_query[:, None]
-    )
-    return jnp.where(allowed[None], raw, -1e30)
+    at = lax.axis_index("dp") * fsdp_count + lax.axis_index("fsdp")
+    count, piece, gw = owned.shape
+    bands = hidden // width
+
+    def beside(part):
+        groups = part.shape[0] // 2
+        part = part.reshape(groups, 2 * piece, gw).transpose(1, 0, 2)
+        return part.reshape(2 * piece, groups * gw)
+
+    down = owned[: 2 * bands].reshape(bands * 2 * piece, gw)
+    up = beside(owned[2 * bands : 4 * bands])
+    out = owned[4 * bands : 4 * bands + 2].reshape(2 * piece, gw)
+    qkv = beside(owned[4 * bands + 2 :])
+    each = width // devices
+    small = lax.dynamic_slice(sums[:8], (0, at * each), (8, each))
+    tall = sums[8 : 8 + bands].reshape(hidden)
+    tall = lax.dynamic_slice(tall, (at * (hidden // devices),), (hidden // devices,))
+    return small, tall, qkv, out, up, down
 
 
 def body(
@@ -310,11 +828,6 @@
         down_bias,
     )
     length, width = frames.shape
-    heads = HEADS
-    scale = 1.0 / math.sqrt(HEAD_DIM)
-    block = min(512, length)
-    blocks = length // block
-    segment_row = segment_ids[0]
     place_row = positions[0]
     (
         gain_first,
@@ -336,180 +849,72 @@
     gain_two = gain_second.astype(jnp.float32)
     shift_two = shift_second.astype(jnp.float32)
     inputs = frames.astype(jnp.float32) + sinusoid(place_row, width)
-    normed_one = affine_norm(inputs, gain_one, shift_one).astype(jnp.bfloat16)
+    unit_one, rate_one = standardize(inputs)
+    normed_one = (unit_one * gain_one + shift_one).astype(jnp.bfloat16)
     projected = jnp.dot(normed_one, weight_in, preferred_element_type=jnp.float32)
-    query = (
-        (projected[:, :width] + bias_query.astype(jnp.float32))
-        .astype(jnp.bfloat16)
-        .reshape(length, heads, HEAD_DIM)
-    )
-    keys = projected[:, width : 2 * width].astype(jnp.bfloat16).reshape(length, heads, HEAD_DIM)
-    values = (
-        (projected[:, 2 * width :] + bias_value.astype(jnp.float32))
-        .astype(jnp.bfloat16)
-        .reshape(length, heads, HEAD_DIM)
-    )
-
-    def rows_of(index):
-        return slice(index * block, (index + 1) * block)
-
-    def scores_for(row_block, col_block):
-        rows = rows_of(row_block)
-        cols = rows_of(col_block)
-        return block_scores(
-            query[rows],
-            keys[cols],
-            segment_row[rows],
-            segment_row[cols],
-            place_row[rows],
-            place_row[cols],
-        )
-
-    log_totals = []
-    attended_all = []
-    for row_block in range(blocks):
-        peak = jnp.full((heads, block), -1e30, jnp.float32)
-        total = jnp.zeros((heads, block), jnp.float32)
-        for col_block in range(row_block + 1):
-            scores = scores_for(row_block, col_block)
-            new_peak = jnp.maximum(peak, jnp.max(scores, axis=-1))
-            total = total * jnp.exp(peak - new_peak) + jnp.sum(
-                jnp.exp(scores - new_peak[..., None]), axis=-1
-            )
-            peak = new_peak
-        log_total = peak + jnp.log(total)
-        attended = jnp.zeros((block, heads, HEAD_DIM), jnp.float32)
-        for col_block in range(row_block + 1):
-            probs = jnp.exp(scores_for(row_block, col_block) - log_total[..., None]).astype(
-                jnp.bfloat16
-            )
-            attended = attended + jnp.einsum(
-                "hqk,khd->qhd",
-                probs,
-                values[rows_of(col_block)],
-                preferred_element_type=jnp.float32,
-            )
-        log_totals.append(log_total)
-        attended_all.append(attended)
-    mixed = jnp.concatenate(attended_all, axis=0).reshape(length, width).astype(jnp.bfloat16)
+    bias_all = jnp.concatenate([bias_query, jnp.zeros_like(bias_query), bias_value])
+    projected = (projected + bias_all.astype(jnp.float32)).astype(jnp.bfloat16)
+
+    start = jnp.arange(length, dtype=jnp.int32) - place_row
+    mixed = attention(projected, start[:, None])
     resid_two = (
         inputs
         + jnp.dot(mixed, weight_out, preferred_element_type=jnp.float32)
         + bias_out.astype(jnp.float32)
     )
-    normed_two = affine_norm(resid_two, gain_two, shift_two).astype(jnp.bfloat16)
+    unit_two, rate_two = standardize(resid_two)
+    normed_two = (unit_two * gain_two + shift_two).astype(jnp.bfloat16)
     hidden = jnp.dot(normed_two, weight_up, preferred_element_type=jnp.float32) + bias_up.astype(
         jnp.float32
     )
-    activated = jax.nn.gelu(hidden, approximate=False).astype(jnp.bfloat16)
+    half = 0.5 + 0.5 * lax.erf(hidden * math.sqrt(0.5))
+    activated = (hidden * half).astype(jnp.bfloat16)
+    slope = half + hidden * jnp.exp(-0.5 * hidden * hidden) * (1.0 / math.sqrt(2.0 * math.pi))
+    slope = slope.astype(jnp.bfloat16)
     result = (
         resid_two
         + jnp.dot(activated, weight_down, preferred_element_type=jnp.float32)
         + bias_down.astype(jnp.float32)
     )
     output = result.astype(jnp.bfloat16)
-    grad_out = cotangent.astype(jnp.float32)
-    down_grad = jnp.einsum("tf,td->fd", activated, cotangent, preferred_element_type=jnp.float32)
-    down_bias_grad = jnp.sum(cotangent.astype(jnp.float32), axis=0)
-    grad_act = jnp.einsum("td,fd->tf", cotangent, weight_down, preferred_element_type=jnp.float32)
-    _, gelu_back = jax.vjp(partial(jax.nn.gelu, approximate=False), hidden)
-    grad_hidden = gelu_back(grad_act)[0].astype(jnp.bfloat16)
-    up_grad = jnp.einsum("td,tf->df", normed_two, grad_hidden, preferred_element_type=jnp.float32)
-    up_bias_grad = jnp.sum(grad_hidden.astype(jnp.float32), axis=0)
-    grad_normed_two = jnp.einsum(
-        "tf,df->td", grad_hidden, weight_up, preferred_element_type=jnp.float32
+    many = hidden.shape[1]
+    dp_count = lax.axis_size("dp")
+    act = activated.T.reshape(dp_count, many // width, width // dp_count, length)
+    act = act.transpose(1, 0, 2, 3).reshape(many, length)
+    frames_grad, owned, sums = backward(
+        positions,
+        cotangent,
+        act,
+        slope,
+        normed_two.T,
+        unit_two.astype(jnp.bfloat16),
+        rate_two,
+        mixed.T,
+        projected,
+        normed_one.T,
+        unit_one.astype(jnp.bfloat16),
+        rate_one,
+        jnp.stack([gain_one, gain_two]),
+        (weight_in, weight_out, weight_up, weight_down),
     )
-    _, norm_back_two = jax.vjp(affine_norm, resid_two, gain_two, shift_two)
-    grad_resid_two, gain_two_grad, shift_two_grad = norm_back_two(grad_normed_two)
-    grad_two = grad_out + grad_resid_two
-    grad_branch = grad_two.astype(jnp.bfloat16)
-    out_grad = jnp.einsum("to,td->od", mixed, grad_branch, preferred_element_type=jnp.float32)
-    out_bias_grad = jnp.sum(grad_branch.astype(jnp.float32), axis=0)
-    grad_mixed = jnp.einsum(
-        "td,od->to", grad_branch, weight_out, preferred_element_type=jnp.float32
+    small, tall, qkv_grad, out_grad, up_grad, down_grad = pick_grads(owned, sums, width, many)
+    return (
+        output,
+        frames_grad,
+        small[0],
+        small[1],
+        qkv_grad,
+        small[2],
+        small[3],
+        out_grad,
+        small[4],
+        small[5],
+        small[6],
+        up_grad,
+        tall,
+        down_grad,
+        small[7],
     )
-    grad_mixed = grad_mixed.astype(jnp.bfloat16).reshape(length, heads, HEAD_DIM)
-    grad_query = jnp.zeros((length, heads, HEAD_DIM), jnp.float32)
-    grad_keys = jnp.zeros((length, heads, HEAD_DIM), jnp.float32)
-    grad_values = jnp.zeros((length, heads, HEAD_DIM), jnp.float32)
-    for row_block in range(blocks):
-        rows = rows_of(row_block)
-        grad_part = grad_mixed[rows]
-        log_total = log_totals[row_block]
-        delta = jnp.zeros((heads, block), jnp.float32)
-        for col_block in range(row_block + 1):
-            probs = jnp.exp(scores_for(row_block, col_block) - log_total[..., None])
-            grad_probs = jnp.einsum(
-                "qhd,khd->hqk",
-                grad_part,
-                values[rows_of(col_block)],
-                preferred_element_type=jnp.float32,
-            )
-            delta = delta + jnp.sum(probs * grad_probs, axis=-1)
-        for col_block in range(row_block + 1):
-            cols = rows_of(col_block)
-            probs = jnp.exp(scores_for(row_block, col_block) - log_total[..., None])
-            grad_probs = jnp.einsum(
-                "qhd,khd->hqk", grad_part, values[cols], preferred_element_type=jnp.float32
-            )
-            grad_scores = (probs * (grad_probs - delta[..., None])).astype(jnp.bfloat16)
-            grad_values = grad_values.at[cols].add(
-                jnp.einsum(
-                    "hqk,qhd->khd",
-                    probs.astype(jnp.bfloat16),
-                    grad_part,
-                    preferred_element_type=jnp.float32,
-                )
-            )
-            grad_query = grad_query.at[rows].add(
-                jnp.einsum(
-                    "hqk,khd->qhd", grad_scores, keys[cols], preferred_element_type=jnp.float32
-                )
-                * scale
-            )
-            grad_keys = grad_keys.at[cols].add(
-                jnp.einsum(
-                    "hqk,qhd->khd", grad_scores, query[rows], preferred_element_type=jnp.float32
-                )
-                * scale
-            )
-    grad_projected = jnp.concatenate(
-        [
-            grad_query.reshape(length, width).astype(jnp.bfloat16),
-            grad_keys.reshape(length, width).astype(jnp.bfloat16),
-            grad_values.reshape(length, width).astype(jnp.bfloat16),
-        ],
-        axis=1,
-    )
-    qkv_grad = jnp.einsum(
-        "td,te->de", normed_one, grad_projected, preferred_element_type=jnp.float32
-    )
-    query_bias_grad = jnp.sum(grad_projected[:, :width].astype(jnp.float32), axis=0)
-    value_bias_grad = jnp.sum(grad_projected[:, 2 * width :].astype(jnp.float32), axis=0)
-    grad_normed_one = jnp.einsum(
-        "te,de->td", grad_projected, weight_in, preferred_element_type=jnp.float32
-    )
-    _, norm_back_one = jax.vjp(affine_norm, inputs, gain_one, shift_one)
-    grad_resid_one, gain_one_grad, shift_one_grad = norm_back_one(grad_normed_one)
-    frames_grad = (grad_two + grad_resid_one).astype(jnp.bfloat16)
-    owned = spread_grads(
-        (
-            gain_one_grad,
-            shift_one_grad,
-            qkv_grad,
-            query_bias_grad,
-            value_bias_grad,
-            out_grad,
-            out_bias_grad,
-            gain_two_grad,
-            shift_two_grad,
-            up_grad,
-            up_bias_grad,
-            down_grad,
-            down_bias_grad,
-        )
-    )
-    return (output, frames_grad) + owned
 
 
 def solution(mesh):

time: 1080 us -> 606 us (0.56)
  matrix products: 328 us -> 46 us
  Pallas kernels: 131 us -> 389 us
  waiting for transfers between devices: 235 us -> 0 us
  other arithmetic: 124 us -> 38.8 us
  local copies, waits for them, and re-layouts: 146 us -> 79.1 us
  blocking collectives: 88.7 us -> 43.4 us
  between operations: 15 us -> 1.22 us
    pallas_call x0 -> x2, Pallas kernels: none -> 267 us  [the longest x1 235 us: backward(): pl.pallas_call(partial(backward_kernel, dims), out_shape=[jax.ShapeDtypeS...]
    dot_general x26 -> x0, matrix products: 247 us -> none  [the longest x3 27.1 us: body(): jnp.einsum('hqk,qhd->khd', probs.astype(jnp.bfloat16), grad_part, preferr...]
    reduce_scatter x4 -> x0, waiting for transfers between devices: 235 us -> none  [spread_grads(): lax.psum_scatter(pieces, ('dp', 'fsdp'), scatter_dimension=0, tiled=False)]
    reduce_sum x14 -> x3, other arithmetic: 52.3 us -> 6.51 us  [the longest x2 3.69 us: standardize(): spread = jnp.mean(centered * centered, axis=-1, keepdims=True)]
    unnamed x1 -> x0, blocking collectives: 45.3 us -> none
    convert_element_type x10 -> x4, other arithmetic: 56.4 us -> 20.2 us  [the longest x1 13.2 us: body(): slope = slope.astype(jnp.bfloat16)]
    dot_general x1, matrix products: 46.4 us -> 15.9 us  [body(): jnp.dot(normed_two, weight_up, preferred_element_type=jnp.float32)]
    reshape x12 -> x3, local copies, waits for them, and re-layouts: 45.5 us -> 15.3 us  [the longest x1 14.2 us: body(): activated.T.reshape(dp_count, many // width, width // dp_count, length)]
  transfers between devices with their start and end apart: 4 -> 0, of which waited for: 2 -> 0; matrix products, arithmetic and copies ran while one was open for 30% -> 0% of each run, Pallas kernels for 0% -> 0%
where the time goes in v2:
time: 606 us; the launch traced here: 598 us
  Pallas kernels  389 us (64%)
  local copies, waits for them, and re-layouts  79.1 us (13%)
  matrix products  46 us (8%)
  blocking collectives  43.4 us (7%)
  other arithmetic  38.8 us (6%)
    pallas_call x1, Pallas kernels, backward(): pl.pallas_call(partial(backward_kernel, dims), out_shape=[jax.ShapeDtypeS...  235 us
    pallas_call x1, Pallas kernels, gather_weights(): pl.pallas_call(partial(gather_kernel, (dims, tuple(chunks), (0, 2, 4, 6,...  123 us
    all_gather x1, blocking collectives, collect(): spread = lax.all_gather(packed, ('dp', 'fsdp'), axis=0, tiled=False)  43.4 us
    pallas_call x1, Pallas kernels, attention(): pl.pallas_call(attention_kernel, grid=(pairs,), out_shape=jax.ShapeDtypeS...  31.4 us
    dot_general x1, matrix products, body(): jnp.dot(normed_two, weight_up, preferred_element_type=jnp.float32)  15.9 us
    reshape x1, local copies, waits for them, and re-layouts, body(): activated.T.reshape(dp_count, many // width, width // dp_count, length)  14.2 us
    transpose x1, local copies, waits for them, and re-layouts, body(): act = act.transpose(1, 0, 2, 3).reshape(many, length)  13.7 us
    convert_element_type x1, other arithmetic, body(): slope = slope.astype(jnp.bfloat16)  13.2 us

profile of v2, /device:TPU:0, one launch (start us, length us, event | category | flops | bytes accessed | tf_op | source)
XLA Modules:
  0.0 597.8 jit_solution(9535100577568252248)
XLA Ops:
  0.6 6.1 %concatenate.14 = bf16[384]{0:T(512)(128)(2,1)S(1)} concatenate(bf16[32]{0:T(256)(128)(2,1)} %param.20, bf16[32]{0:T(256)(128)(2,1)} %param.21, bf16[32]{0:T(256)(128)(2,1)} %param.23, bf16[32]{0:T(256)(128)(2,1)} %param.24, bf16[32]{0:T(256)(128)(2,1)} %param.26, bf16[32]{0:T(256)(128)(2,1)} %param.27, bf16[32]{0:T(256)(128)(2,1)} %param.28, bf16[128]{0:T(256)(128)(2,1)} %param.30, ...), dimensions={0} | concatenate | bytes 1536 | tf_op jit(solution)/shard_map/concatenate | solution.py:227
  6.8 43.4 %all-gather.1 = bf16[32,1,384]{2,1,0:T(2,128)(2,1)S(1)} all-gather(bf16[1,1,384]{2,1,0:T(2,128)(2,1)S(1)} %reshape.337), channel_id=2, replica_groups=mesh['dp'=8,'fsdp'=4] {'dp','fsdp'}, dimensions={0}, use_global_device_ids=true | all-gather | bytes 25344 | tf_op jit(solution)/shard_map/all_gather | solution.py:228
  50.1 0.1 fusion.16
  50.2 0.1 reshape.331
  50.3 0.1 concatenate.16
  50.4 0.1 concatenate.15
  50.5 0.7 convert_element_type.132
  51.2 7.3 %multiply_sine_fusion = (f32[1024,512,1]{1,0,2:T(8,128)S(1)}, f32[1024,512,1]{1,0,2:T(8,128)S(1)}) fusion(f32[512]{0:T(512)S(1)} %multiply_exponential_fusion, f32[1024]{0:T(1024)S(1)} %bitcast.90), kind=kLoop, calls=%fused_computation.28 | loop fusion | flops 524288 | bytes 4200448 | tf_op jit(solution)/shard_map/sin | solution.py:23
  58.5 2.4 pad_maximum_fusion
  61.0 7.8 %copy.74 = f32[1024,512,2]{0,2,1:T(2,128)} copy(f32[1024,512,2]{1,0,2:T(8,128)} %pad_maximum_fusion) | data formatting | bytes 8388608 | tf_op jit(solution)/shard_map/stack | solution.py:23
  68.7 6.1 %reshape.319 = f32[1024,1024]{0,1:T(8,128)} reshape(f32[1024,512,2]{0,2,1:T(2,128)} %copy.74) | data formatting | bytes 8388608 | tf_op jit(solution)/shard_map/reshape | solution.py:23
  74.8 5.5 copy.75
  80.3 0.0 copy-done.1
  80.3 2.8 fusion.12
  83.2 0.6 copy-done
  83.8 0.8 multiply_reduce_fusion.1
  84.6 0.1 reshape.330
  84.7 0.1 reshape.329
  84.7 4.2 multiply_convert_fusion.3
  89.0 122.6 %shard_map.271 = (bf16[1024,3072]{1,0:T(8,128)(2,1)}, bf16[1024,1024]{1,0:T(8,128)(2,1)}, bf16[1024,4096]{1,0:T(8,128)(2,1)}, bf16[4096,1024]{1,0:T(8,128)(2,1)}) custom-call(bf16[128,768]{1,0:T(8,128)(2,1)} %refs_0_.2, bf16[128,256]{1,0:T(8,128)(2,1)} %refs_1_.2, bf16[128,1024]{1,0:T(8,128)(2,1)} %refs_2_.1, bf16[512,256]{1,0:T(8,128)(2,1)} %refs_3_.1), custom_call_target="tpu_custom_call" | custom-call | tf_op jit(solution)/shard_map/pallas_call | solution.py:202
  211.6 0.0 copy-start.7
  211.6 11.3 %add_convert_fusion.query.keys.values.refs_8_ = bf16[1024,3072]{1,0:T(8,128)(2,1)} fusion(f32[3072]{0:T(1024)S(1)} %maximum_convert_fusion, bf16[1024,1024]{1,0:T(8,128)(2,1)} %get-tuple-element.90, bf16[1024,3072]{1,0:T(8,128)(2,1)} %get-tuple-element.22.refs_13_), kind=kOutput, calls=%fused_computation.14 | convolution fusion | flops 6448742400 | bytes 14692352 | tf_op jit(solution)/shard_map/dot_general | solution.py:854
  222.9 0.0 copy-done.7
  222.9 0.2 copy.76
  223.2 0.8 iota_subtract_fusion.start
  224.0 31.4 %attention.1 = bf16[1024,1024]{1,0:T(8,128)(2,1)} custom-call(bf16[1024,3072]{1,0:T(8,128)(2,1)} %add_convert_fusion.query.keys.values.refs_8_, bf16[1024,3072]{1,0:T(8,128)(2,1)} %add_convert_fusion.query.keys.values.refs_8_, bf16[1024,3072]{1,0:T(8,128)(2,1)} %add_convert_fusion.query.keys.values.refs_8_, s32[1024,1]{1,0:T(8,128)} %iota_subtract_fusion.start), custom_call_target="tpu_custom_call" | custom-call | tf_op jit(solution)/shard_map/attention/pallas_call | solution.py:284
  255.4 8.0 %fusion.17 = (f32[1024]{0:T(1024)S(1)}, f32[1024,1024]{1,0:T(8,128)}) fusion(f32[1024]{0:T(1024)S(1)} %reshape.331, bf16[1024,1024]{1,0:T(8,128)(2,1)} %attention.1, bf16[1024,1024]{1,0:T(8,128)(2,1)} %get-tuple-element.23.refs_14_, f32[1024,1024]{1,0:T(8,128)} %copy.75, bf16[1024,1024]{1,0:T(8,128)(2,1)S(1)} %copy-done.1), kind=kOutput, calls=%fused_computation.62 | convolution fusion | flops 2152725504 | bytes 14688256 | tf_op jit(solution)/shard_map/dot_general | solution.py:862
  263.4 0.1 reshape.335
  263.5 0.1 fusion.11
  263.5 0.1 reshape.333
  263.6 0.1 reshape.332
  263.7 2.9 multiply_reduce_fusion
  266.6 0.5 copy-done.3
  267.1 15.9 %fusion.8 = (bf16[4096,1024]{0,1:T(8,128)(2,1)}, f32[1024,4096]{1,0:T(8,128)S(1)}) fusion(f32[4096]{0:T(1024)S(1)} %fusion.11, bf16[1024,4096]{1,0:T(8,128)(2,1)} %get-tuple-element.24.refs_15_, f32[1024,1024]{1,0:T(8,128)S(1)} %copy-done.3, f32[1024]{0:T(1024)S(1)} %reshape.333, f32[1024]{0:T(1024)S(1)} %reshape.332, f32[1024]{0:T(1024)S(1)} %add_rsqrt_fusion, ...), kind=kOutput, calls=%fused_computation.13 | convolution fusion | flops 8620343296 | bytes 37781504 | tf_op jit(solution)/shard_map/dot_general | solution.py:867
  283.0 0.0 slice-done
  283.0 0.0 slice-done.1
  283.0 10.9 %add_convert_fusion.1 = bf16[1024,1024]{1,0:T(8,128)(2,1)} fusion(f32[1024,1024]{1,0:T(8,128)S(1)} %copy-done.3, f32[1024]{0:T(1024)S(1)} %reshape.335, bf16[4096,1024]{1,0:T(8,128)(2,1)S(1)} %bitcast.78, f32[1024,4096]{1,0:T(8,128)S(1)} %get-tuple-element.118, f32[4096]{0:T(1024)S(1)} %fusion.11), kind=kOutput, calls=%fused_computation.18 | convolution fusion | flops 8618246144 | bytes 31477760 | tf_op jit(solution)/shard_map/dot_general | solution.py:876
  293.9 0.0 copy-done.2
  293.9 14.2 %reshape.320 = bf16[8,4,128,1024]{2,1,0,3:T(4,128)(2,1)} reshape(bf16[4096,1024]{0,1:T(8,128)(2,1)} %get-tuple-element.117) | data formatting | bytes 16777216 | tf_op jit(solution)/shard_map/reshape | solution.py:882
  308.1 13.7 %copy.78 = bf16[4,8,128,1024]{3,2,1,0:T(8,128)(2,1)} copy(bf16[4,8,128,1024]{2,0,1,3:T(4,128)(2,1)} %bitcast.73) | data formatting | bytes 16777216 | tf_op jit(solution)/shard_map/transpose | solution.py:883
  321.8 13.2 %fusion.4.refs_3_ = bf16[1024,4096]{1,0:T(8,128)(2,1)} fusion(f32[1024,4096]{1,0:T(8,128)} %copy-done.2, f32[4096]{0:T(1024)S(1)} %fusion.11), kind=kLoop, calls=%fused_computation.5 | loop fusion | flops 41943040 | bytes 25182208 | tf_op jit(solution)/shard_map/convert_element_type | solution.py:873
  335.1 0.0 copy-done.4
  335.1 2.8 multiply_convert_fusion.2
  337.8 4.1 copy.80.refs_4_
  341.9 1.0 copy.81.refs_6_
  343.0 3.9 copy.79
  346.9 2.5 copy.82.refs_9_
  349.4 1.0 copy.83.refs_11_
  350.5 0.1 convert_element_type.159
  350.5 0.1 convert_element_type.158
  350.6 0.6 maximum_convert_fusion.1.refs_12_
  351.2 235.3 %backward.1 = (bf16[1024,1024]{1,0:T(8,128)(2,1)}, f32[24,64,256]{2,1,0:T(8,128)}, f32[16,1024]{1,0:T(8,128)}) custom-call(s32[1,1024]{1,0:T(1,128)} %refs_0_.3, bf16[1024,1024]{1,0:T(8,128)(2,1)} %refs_1_.3, bf16[4096,1024]{1,0:T(8,128)(2,1)} %bitcast.74, bf16[1024,4096]{1,0:T(8,128)(2,1)} %fusion.4.refs_3_, bf16[1024,1024]{1,0:T(8,128)(2,1)} %copy.80.refs_4_, ...), custom_call_target="tpu_custom_call" | custom-call | tf_op jit(solution)/shard_map/backward/pallas_call | solution.py:719
  586.6 0.9 slice.78
  587.5 0.1 constant_dynamic-slice_fusion
  587.6 0.5 slice_bitcast_fusion.2
  588.1 1.0 slice.81
  589.1 0.2 copy.84
  589.3 0.9 copy.86
  590.2 1.6 slice.84
  591.8 2.1 fusion.15
  593.9 0.8 copy.89
  594.7 0.8 slice_bitcast_fusion
  595.5 0.6 dynamic_slice.7
  596.1 1.3 copy.96
  (22 shorter events, 0.1 us)
Async XLA Ops:
  74.8 5.5 copy-start.1
  80.3 3.4 copy-start
  211.6 11.3 %copy-start.7 = (s32[1,1024]{1,0:T(1,128)S(1)}, s32[1,1024]{1,0:T(1,128)}, u32[]{:S(2)}) copy-start(s32[1,1024]{1,0:T(1,128)} %refs_0_.3) | copy-start | bytes 12292
  263.7 3.5 copy-start.3
  263.7 19.3 %slice-start = ((s8[8388608]{0:T(1024)(128)(4,1)}), s8[4194304]{0:T(1024)(128)(4,1)S(1)}, s32[]{:S(2)}) async-start(s8[8388608]{0:T(1024)(128)(4,1)} %bitcast.77), calls=%async_computation | async-start | bytes 8388608
  267.1 15.9 %slice-start.1 = ((s8[8388608]{0:T(1024)(128)(4,1)}), s8[4194304]{0:T(1024)(128)(4,1)S(1)}, s32[]{:S(2)}) async-start(s8[8388608]{0:T(1024)(128)(4,1)} %bitcast.77), calls=%async_computation.1 | async-start | bytes 8388608
  283.0 10.9 %copy-start.2 = (f32[1024,4096]{1,0:T(8,128)}, f32[1024,4096]{1,0:T(8,128)S(1)}, u32[]{:S(2)}) copy-start(f32[1024,4096]{1,0:T(8,128)S(1)} %get-tuple-element.118) | copy-start | bytes 50331652
  321.8 13.2 %copy-start.4 = (f32[1024,1024]{1,0:T(8,128)S(1)}, f32[1024,1024]{1,0:T(8,128)}, u32[]{:S(2)}) copy-start(f32[1024,1024]{1,0:T(8,128)} %get-tuple-element.116) | copy-start | bytes 12582916
  337.8 9.1 %copy-start.5 = (bf16[1024,1024]{1,0:T(8,128)(2,1)S(1)}, bf16[1024,1024]{1,0:T(8,128)(2,1)}, u32[]{:S(2)}) copy-start(bf16[1024,1024]{1,0:T(8,128)(2,1)} %get-tuple-element.90) | copy-start | bytes 6291460
  586.6 9.5 %copy-start.6 = (bf16[1024,1024]{1,0:T(8,128)(2,1)S(1)}, bf16[1024,1024]{1,0:T(8,128)(2,1)}, u32[]{:S(2)}) copy-start(bf16[1024,1024]{1,0:T(8,128)(2,1)} %get-tuple-element.135) | copy-start | bytes 6291460

commit v3 on v2

--- a/solution.py
+++ b/solution.py
@@ -14,20 +14,6 @@
 
 
 eps = 1e-05
-
-
-def sinusoid(places, width):
-    halves = jnp.arange(width // 2, dtype=jnp.float32)
-    rates = jnp.exp(halves * (-2.0 * math.log(10000.0) / width))
-    angles = places.astype(jnp.float32)[..., None] * rates
-    return jnp.stack([jnp.sin(angles), jnp.cos(angles)], axis=-1).reshape(places.shape + (width,))
-
-
-def standardize(values):
-    centered = values - jnp.mean(values, axis=-1, keepdims=True)
-    spread = jnp.mean(centered * centered, axis=-1, keepdims=True)
-    rate = lax.rsqrt(spread + eps)
-    return centered * rate, rate
 
 
 def grid_of(dp_count, fsdp_count):
@@ -40,260 +26,495 @@
     return dp_count // across, across, fsdp_count // cores, cores
 
 
-def gather_kernel(plan, *refs):
-    dims, chunks, offsets = plan
+def forward_kernel(dims, *refs):
+    (
+        place, frames, vector_shard, in_shard, out_shard, up_shard, down_shard,
+        result, weights, act_hbm, slope_hbm, two_hbm, unit_two, rate_two, mixed_hbm, qkv_hbm,
+        one_hbm, unit_one, rate_one, vectors,
+        spread, tall, stream, normed, unit, qkv, mixed, act, slope, turned, loaded,
+        load, save, local, z_send, z_recv, a_send, a_recv, b_send, b_recv, s_send, s_recv,
+    ) = refs
     deep, across, down, cores = dims
-    count = len(chunks)
-    names = len(refs) - 9
-    shards = refs[: names // 2]
-    wholes = refs[names // 2 : names]
-    local, z_send, z_recv, a_send, a_recv, b_send, b_recv, s_send, s_recv = refs[names:]
+    side = across
+    fsdp = down * cores
+    dp_count = deep * across
+    devices = dp_count * fsdp
+    length, width = stream.shape
+    hidden = act.shape[1]
+    triple = qkv.shape[1]
+    piece = weights.shape[4]
+    rows_each = 2 * piece
+    gw = width // fsdp
+    each_in, each_up = triple // fsdp, hidden // fsdp
+    groups_in, groups_up = triple // width, hidden // width
+    units = weights.shape[0]
+    count = 2 * units
+    extra = count
+    first_up = groups_in + 1
+    first_down = first_up + groups_up
+    block = min(256, length)
+    steps = length // block
     outer = lax.axis_index("dp")
     inner = lax.axis_index("fsdp")
     z, x, y, c = outer // across, outer % across, inner // cores, inner % cores
+    a = (1 - c) * x + c * y
+    b = (1 - c) * y + c * x
 
     def device(zz, xx, yy, cc):
         return (zz * across + xx, yy * cores + cc)
 
-    along_z = [device((z + k) % deep, x, y, c) for k in range(1, deep)]
-    along_x = [device(z, (x + k) % across, y, c) for k in range(1, across)]
-    along_y = [device(z, x, (y + k) % down, c) for k in range(1, down)]
-    twin = [device(z, x, y, 1 - c)] if cores == 2 else []
+    twin = device(z, x, y, 1 - c)
+
+    def a_peer(k):
+        to = (a + k) % side
+        return device(z, (1 - c) * to + c * x, (1 - c) * y + c * to, c)
+
+    def b_peer(k):
+        to = (b + k) % side
+        return device(z, (1 - c) * x + c * to, (1 - c) * to + c * y, c)
+
+    def z_peer(k):
+        return device((z + k) % deep, x, y, c)
+
     barrier = pltpu.get_barrier_semaphore()
-    everyone = along_z + along_x + along_y + twin
+    everyone = [twin]
+    everyone += [a_peer(k) for k in range(1, side)] + [b_peer(k) for k in range(1, side)]
+    everyone += [z_peer(k) for k in range(1, deep)]
     for peer in everyone:
         pl.semaphore_signal(barrier, inc=1, device_id=peer, device_id_type=MESH)
     pl.semaphore_wait(barrier, len(everyone))
 
-    def block(i, zz, xx, yy, cc):
-        which, rows, cols, start, size = chunks[i]
-        return wholes[which].at[
-            pl.ds(pl.multiple_of((zz * across + xx) * rows, 16), rows),
-            pl.ds(pl.multiple_of((yy * cores + cc) * cols + start, 128), size),
-        ]
-
-    def strip(i, yy, cc):
-        which, rows, cols, start, size = chunks[i]
-        return wholes[which].at[
-            :, pl.ds(pl.multiple_of((yy * cores + cc) * cols + start, 128), size)
-        ]
-
-    def own(i):
-        which, rows, cols, start, size = chunks[i]
-        return shards[which].at[:, pl.ds(start, size)]
-
     def copy(source, target, send, recv, peer):
         return pltpu.make_async_remote_copy(
-            src_ref=source,
-            dst_ref=target,
-            send_sem=send,
-            recv_sem=recv,
-            device_id=peer,
-            device_id_type=MESH,
+            src_ref=source, dst_ref=target, send_sem=send, recv_sem=recv,
+            device_id=peer, device_id_type=MESH,
         )
 
+    every = slice(None)
+
+    def view(i, zz, xx, yy, cc):
+        lane = yy * cores + cc
+        if isinstance(i, int) and i == extra:
+            return spread.at[zz, xx, :, pl.ds(pl.multiple_of(lane * 128, 128), 128)]
+        return weights.at[
+            i // 2, zz, xx, i % 2, :, pl.ds(pl.multiple_of(lane * gw, 128), gw)
+        ]
+
+    def own(i):
+        if i == extra:
+            return vector_shard
+        unit_at, half = i // 2, i % 2
+        rows = pl.ds(half * piece, piece)
+        if unit_at < groups_in:
+            return in_shard.at[rows, pl.ds(unit_at * gw, gw)]
+        if unit_at < first_up:
+            return out_shard.at[rows, :]
+        if unit_at < first_down:
+            return up_shard.at[rows, pl.ds((unit_at - first_up) * gw, gw)]
+        return down_shard.at[pl.ds((unit_at - first_down) * rows_each + half * piece, piece), :]
+
+    def begin(i):
+        mine = view(i, z, x, y, c)
+        pltpu.make_async_copy(own(i), mine, local.at[i]).start()
+        for k in range(1, deep):
+            copy(own(i), mine, z_send.at[i, k - 1], z_recv.at[i, k - 1], z_peer(k)).start()
+
     def first(i):
-        pltpu.make_async_copy(own(i), block(i, z, x, y, c), local.at[i]).start()
-        for k, peer in enumerate(along_z):
-            copy(own(i), block(i, z, x, y, c), z_send.at[i, k], z_recv.at[i, k], peer).start()
+        mine = view(i, z, x, y, c)
+        pltpu.make_async_copy(mine, mine, local.at[i]).wait()
+        for k in range(1, deep):
+            landed = view(i, (z + deep - k) % deep, x, y, c)
+            copy(mine, landed, z_send.at[i, k - 1], z_recv.at[i, k - 1], z_peer(k)).wait()
+        line = view(i, every, x, y, c)
+        for k in range(1, side):
+            copy(line, line, a_send.at[i, k - 1], a_recv.at[i, k - 1], a_peer(k)).start()
 
     def second(i):
-        pltpu.make_async_copy(own(i), block(i, z, x, y, c), local.at[i]).wait()
-        for k, peer in enumerate(along_z):
-            landed = block(i, (z + deep - k - 1) % deep, x, y, c)
-            copy(own(i), landed, z_send.at[i, k], z_recv.at[i, k], peer).wait()
-
-        @pl.when(c == 0)
+        for k in range(1, side):
+            xs = (1 - c) * ((x + side - k) % side) + c * x
+            ys = (1 - c) * y + c * ((y + side - k) % side)
+            landed = view(i, every, xs, ys, c)
+            copy(landed, landed, a_send.at[i, k - 1], a_recv.at[i, k - 1], a_peer(k)).wait()
+        for k in range(1, side):
+            for s in range(side):
+                line = view(i, every, (1 - c) * s + c * x, (1 - c) * y + c * s, c)
+                at = (k - 1) * side + s
+                copy(line, line, b_send.at[i, at], b_recv.at[i, at], b_peer(k)).start()
+
+    def third(i):
+        for k in range(1, side):
+            for s in range(side):
+                xs = (1 - c) * s + c * ((x + side - k) % side)
+                ys = (1 - c) * ((y + side - k) % side) + c * s
+                landed = view(i, every, xs, ys, c)
+                at = (k - 1) * side + s
+                copy(landed, landed, b_send.at[i, at], b_recv.at[i, at], b_peer(k)).wait()
+        for s in range(side):
+            sheet = view(i, every, every, s, c)
+            copy(sheet, sheet, s_send.at[i, s], s_recv.at[i, s], twin).start()
+
+    def fourth(i):
+        for s in range(side):
+            sheet = view(i, every, every, s, 1 - c)
+            copy(sheet, sheet, s_send.at[i, s], s_recv.at[i, s], twin).wait()
+
+    stages = (first, second, third, fourth)
+
+    def advance(step):
+        for at in reversed(range(4)):
+            i = step - at
+            if isinstance(step, int):
+                if 0 <= i < count:
+                    stages[at](i)
+            else:
+                @pl.when((i >= 0) & (i < count))
+                def _(i=i, at=at):
+                    stages[at](i)
+
+    def rows_at(m):
+        return pl.ds(pl.multiple_of(m * block, block), block)
+
+    def lanes(start, size):
+        return pl.ds(start if isinstance(start, int) else pl.multiple_of(start, 128), size)
+
+    def unit_load(at, slot):
+        return pltpu.make_async_copy(weights.at[at], loaded.at[slot], load.at[slot])
+
+    def matrix(slot):
+        return loaded[slot].reshape(width, width)
+
+    begin(extra)
+    for i in range(count):
+        begin(i)
+
+    even = lax.broadcasted_iota(jnp.int32, (1, width), 1)
+    speed = jnp.exp((even // 2).astype(jnp.float32) * (-2.0 * math.log(10000.0) / width))
+    phase = (even % 2).astype(jnp.float32) * (0.5 * math.pi)
+    small = min(64, block)
+    for at in range(4):
+        @pl.loop(0, length // 4 // small)
+        def _(s):
+            rows = pl.ds(pl.multiple_of(at * (length // 4) + s * small, small), small)
+            angle = place[rows, :].astype(jnp.float32) * speed + phase
+            stream[rows, :] = frames[rows, :].astype(jnp.float32) + jnp.sin(angle)
+
+        stages[at](extra)
+        advance(at)
+
+    group = 128 // (width // devices)
+    for tile in range(width // 128):
+        found = None
+        for owner in range(tile * group, (tile + 1) * group):
+            dp_at, f = owner // fsdp, owner % fsdp
+            part = spread[dp_at // across, dp_at % across, 0:8, f * 128 : (f + 1) * 128]
+            found = part if found is None else found + part
+        vectors[:, tile * 128 : (tile + 1) * 128] = found
+    group = 128 // (hidden // devices)
+    for tile in range(hidden // 128):
+        found = None
+        for owner in range(tile * group, (tile + 1) * group):
+            dp_at, f = owner // fsdp, owner % fsdp
+            part = spread[dp_at // across, dp_at % across, 8:16, f * 128 : (f + 1) * 128]
+            found = part if found is None else found + part
+        tall[:, tile * 128 : (tile + 1) * 128] = found
+
+    def normalize(m, value, row, rate_ref):
+        mean = jnp.mean(value, axis=1, keepdims=True)
+        centered = value - mean
+        rate = lax.rsqrt(jnp.mean(centered * centered, axis=1, keepdims=True) + eps)
+        normal = centered * rate
+        rate_ref[rows_at(m), :] = jnp.broadcast_to(rate, (block, 128))
+        unit[rows_at(m), :] = normal.astype(jnp.bfloat16)
+        found = (normal * vectors[row : row + 1, :] + vectors[row + 1 : row + 2, :])
+        found = found.astype(jnp.bfloat16)
+        normed[rows_at(m), :] = found
+        return found
+
+    @pl.loop(0, steps)
+    def _(m):
+        found = normalize(m, stream[rows_at(m), :], 0, rate_one)
+        turned[0, :, rows_at(m)] = found.T
+
+    def keep(source, target, at):
+        return pltpu.make_async_copy(source, target, save.at[at])
+
+    keep(unit, unit_one, 0).start()
+    keep(turned.at[0], one_hbm, 1).start()
+    advance(4)
+    for g in range(groups_in):
+        if g:
+            advance(3 + 2 * g)
+            advance(4 + 2 * g)
+        unit_load(g, g % 2).start()
+        unit_load(g, g % 2).wait()
+
+        @pl.loop(0, steps)
+        def _(m):
+            found = jnp.dot(
+                normed[rows_at(m), :], matrix(g % 2), preferred_element_type=jnp.float32
+            )
+            for f in range(fsdp):
+                start = f * each_in + g * gw
+                part = found[:, f * gw : (f + 1) * gw]
+                if start < width:
+                    part = part + vectors[2:3, start : start + gw]
+                elif start >= 2 * width:
+                    at = start - 2 * width
+                    part = part + vectors[3:4, at : at + gw]
+                qkv[rows_at(m), start : start + gw] = part.astype(jnp.bfloat16)
+
+    keep(qkv, qkv_hbm, 2).start()
+    pairs = width // (2 * HEAD_DIM)
+    base = 2 * (groups_in - 1) + 5
+    factor = math.log2(math.e) / math.sqrt(HEAD_DIM)
+    lane = lax.broadcasted_iota(jnp.int32, (block, 2 * HEAD_DIM), 1)
+
+    @pl.loop(0, pairs)
+    def _(j):
+        pair = 2 * HEAD_DIM
+        at_q = lanes(j * pair, pair)
+        at_k = lanes(width + j * pair, pair)
+        at_v = lanes(2 * width + j * pair, pair)
+        for at in range(steps):
+            rows = pl.ds(at * block, block)
+            span = (at + 1) * block
+            asked = qkv[rows, at_q]
+            seen = qkv[pl.ds(0, span), at_k]
+            held = qkv[pl.ds(0, span), at_v]
+            row = at * block + lax.broadcasted_iota(jnp.int32, (block, span), 0)
+            col = lax.broadcasted_iota(jnp.int32, (block, span), 1)
+            start = at * block + lax.broadcasted_iota(jnp.int32, (block, 1), 0) - place[rows, :]
+            allowed = (col <= row) & (col >= start)
+            found = []
+            for half in range(2):
+                mine = jnp.where((lane // HEAD_DIM) == half, asked, jnp.zeros_like(asked))
+                scores = matmul(mine, seen, (1, 1))
+                scores = jnp.where(allowed, scores * factor, -1e30)
+                weight = jnp.exp2(scores - jnp.max(scores, axis=1, keepdims=True))
+                whole = jnp.sum(weight, axis=1, keepdims=True)
+                found.append(matmul(weight.astype(jnp.bfloat16), held, (1, 0)) / whole)
+            part = jnp.where(lane < HEAD_DIM, found[0], found[1]).astype(jnp.bfloat16)
+            mixed[rows, at_q] = part
+            turned[1, lanes(j * pair, pair), rows] = part.T
+        advance(base + j)
+
+    keep(turned.at[1], mixed_hbm, 3).start()
+    unit_load(groups_in, 0).start()
+    base = base + pairs
+    advance(base)
+    keep(unit, unit_one, 0).wait()
+    keep(turned.at[0], one_hbm, 1).wait()
+    unit_load(groups_in, 0).wait()
+
+    @pl.loop(0, steps)
+    def _(m):
+        found = jnp.dot(mixed[rows_at(m), :], matrix(0), preferred_element_type=jnp.float32)
+        found = stream[rows_at(m), :] + found + vectors[4:5, :]
+        stream[rows_at(m), :] = found
+        found = normalize(m, found, 5, rate_two)
+        turned[0, :, rows_at(m)] = found.T
+
+    keep(unit, unit_two, 0).start()
+    keep(turned.at[0], two_hbm, 1).start()
+    advance(base + 1)
+    base = base + 2
+
+    def turned_rows(slot, g):
+        moves = []
+        for q in range(width // rows_each):
+            f, rest = q * rows_each // gw, q * rows_each % gw
+            at = f * each_up + g * gw + rest
+            owner, band = at // (groups_up * rows_each), (at // rows_each) % groups_up
+            target = pl.multiple_of(band * width + owner * rows_each, 16)
+            moves.append(
+                pltpu.make_async_copy(
+                    turned.at[slot, pl.ds(q * rows_each, rows_each), :],
+                    act_hbm.at[pl.ds(target, rows_each), :],
+                    save.at[4 + slot],
+                )
+            )
+        return moves
+
+    def turned_done(slot):
+        return pltpu.make_async_copy(
+            turned.at[slot], act_hbm.at[pl.ds(0, width), :], save.at[4 + slot]
+        )
+
+    unit_load(first_up, 0).start()
+
+    @pl.loop(0, groups_up)
+    def _(g):
+        slot = g % 2
+        unit_load(first_up + g, slot).wait()
+
+        @pl.when(g < groups_up - 1)
         def _():
-            for k, peer in enumerate(along_x):
-                for zz in range(deep):
-                    piece = block(i, zz, x, y, c)
-                    at = k * deep + zz
-                    copy(piece, piece, a_send.at[i, at], a_recv.at[i, at], peer).start()
-
-        @pl.when(c == 1)
+            unit_load(first_up + g + 1, 1 - slot).start()
+
+        @pl.when(g == 0)
         def _():
-            for k, peer in enumerate(along_y):
-                for zz in range(deep):
-                    piece = block(i, zz, x, y, c)
-                    at = k * deep + zz
-                    copy(piece, piece, a_send.at[i, at], a_recv.at[i, at], peer).start()
-
-    def third(i):
-        @pl.when(c == 0)
+            keep(turned.at[0], two_hbm, 1).wait()
+
+        @pl.when(g == 1)
         def _():
-            for k, peer in enumerate(along_x):
-                for zz in range(deep):
-                    piece = block(i, zz, (x + across - k - 1) % across, y, c)
-                    at = k * deep + zz
-                    copy(piece, piece, a_send.at[i, at], a_recv.at[i, at], peer).wait()
-            mine = strip(i, y, c)
-            for k, peer in enumerate(along_y):
-                copy(mine, mine, b_send.at[i, k], b_recv.at[i, k], peer).start()
-            for peer in twin:
-                copy(mine, mine, s_send.at[i, 0], s_recv.at[i, 0], peer).start()
-
-        @pl.when(c == 1)
+            keep(turned.at[1], mixed_hbm, 3).wait()
+
+        @pl.when(g >= 2)
         def _():
-            for k, peer in enumerate(along_y):
-                for zz in range(deep):
-                    piece = block(i, zz, x, (y + down - k - 1) % down, c)
-                    at = k * deep + zz
-                    copy(piece, piece, a_send.at[i, at], a_recv.at[i, at], peer).wait()
-            for k, peer in enumerate(along_x):
-                for zz in range(deep):
-                    for yy in range(down):
-                        piece = block(i, zz, x, yy, c)
-                        at = (k * deep + zz) * down + yy
-                        copy(piece, piece, b_send.at[i, at], b_recv.at[i, at], peer).start()
-
-    def fourth(i):
-        @pl.when(c == 0)
+            turned_done(slot).wait()
+
+        @pl.loop(0, steps)
+        def _(m):
+            found = jnp.dot(
+                normed[rows_at(m), :], matrix(slot), preferred_element_type=jnp.float32
+            )
+            for f in range(fsdp):
+                at = lanes(f * each_up + g * gw, gw)
+                pre = found[:, f * gw : (f + 1) * gw] + tall[0:1, at]
+                half = 0.5 + 0.5 * lax.erf(pre * math.sqrt(0.5))
+                low = (pre * half).astype(jnp.bfloat16)
+                act[rows_at(m), at] = low
+                bend = half + pre * jnp.exp(-0.5 * pre * pre) * (1.0 / math.sqrt(2.0 * math.pi))
+                slope[rows_at(m), at] = bend.astype(jnp.bfloat16)
+                turned[slot, pl.ds(f * gw, gw), rows_at(m)] = low.T
+
+        for move in turned_rows(slot, g):
+            move.start()
+        advance(base + 2 * g)
+        advance(base + 1 + 2 * g)
+
+    keep(slope, slope_hbm, 6).start()
+    for step in range(base + 2 * groups_up, count + 3):
+        advance(step)
+
+    def band_load(k, slot):
+        moves = []
+        for q in range(dp_count):
+            owner, at = k * (dp_count // groups_up) + q // groups_up, q % groups_up
+            moves.append(
+                pltpu.make_async_copy(
+                    weights.at[first_down + at, owner // across, owner % across],
+                    loaded.at[slot, q // across, q % across],
+                    load.at[slot],
+                )
+            )
+        return moves
+
+    for move in band_load(0, 0):
+        move.start()
+
+    @pl.loop(0, groups_up)
+    def _(k):
+        slot = k % 2
+        unit_load(0, slot).wait()
+
+        @pl.when(k < groups_up - 1)
         def _():
-            for k, peer in enumerate(along_y):
-                landed = strip(i, (y + down - k - 1) % down, c)
-                copy(landed, landed, b_send.at[i, k], b_recv.at[i, k], peer).wait()
-                for other in twin:
-                    copy(
-                        landed, landed, s_send.at[i, k + 1], s_recv.at[i, k + 1], other
-                    ).start()
-
-        @pl.when(c == 1)
-        def _():
-            for k, peer in enumerate(along_x):
-                for zz in range(deep):
-                    for yy in range(down):
-                        piece = block(i, zz, (x + across - k - 1) % across, yy, c)
-                        at = (k * deep + zz) * down + yy
-                        copy(piece, piece, b_send.at[i, at], b_recv.at[i, at], peer).wait()
-            for k in range(down):
-                piece = strip(i, (y + down - k) % down, c)
-                for other in twin:
-                    copy(piece, piece, s_send.at[i, k], s_recv.at[i, k], other).start()
-
-    def fifth(i):
-        for k in range(down):
-            landed = strip(i, (y + down - k) % down, 1 - c)
-            for other in twin:
-                copy(landed, landed, s_send.at[i, k], s_recv.at[i, k], other).wait()
-
-    stages = (first, second, third, fourth, fifth)
-    for step in range(count + offsets[-1]):
-        for at in reversed(range(5)):
-            i = step - offsets[at]
-            if 0 <= i < count:
-                stages[at](i)
-
-
-def gather_weights(shards):
+            for move in band_load(k + 1, 1 - slot):
+                move.start()
+
+        @pl.loop(0, steps)
+        def _(m):
+            stream[rows_at(m), :] += jnp.dot(
+                act[rows_at(m), lanes(k * width, width)], matrix(slot),
+                preferred_element_type=jnp.float32,
+            )
+
+    @pl.loop(0, steps)
+    def _(m):
+        normed[rows_at(m), :] = (stream[rows_at(m), :] + vectors[7:8, :]).astype(jnp.bfloat16)
+
+    keep(normed, result, 7).start()
+    keep(unit, unit_two, 0).wait()
+    keep(qkv, qkv_hbm, 2).wait()
+    for slot in range(2):
+        turned_done(slot).wait()
+    keep(slope, slope_hbm, 6).wait()
+    keep(normed, result, 7).wait()
+
+
+def forward(place, frames, vectors, shards):
     dp_count, fsdp_count = lax.axis_size("dp"), lax.axis_size("fsdp")
     dims = grid_of(dp_count, fsdp_count)
     deep, across, down, cores = dims
-    chunks = []
-    for which, shard in enumerate(shards):
-        rows, cols = shard.shape
-        size = cols
-        if cols % 256 == 0 and rows * cols > 32768:
-            size = 256 if cols > 256 else 128
-        for start in range(0, cols, size):
-            chunks.append((which, rows, cols, start, size))
-    count = len(chunks)
-    flat = max(deep * max(across, down), 1)
+    assert across == down and cores == 2
+    length, width = frames.shape
+    triple = shards[0].shape[1] * fsdp_count
+    hidden = shards[2].shape[1] * fsdp_count
+    piece = width // dp_count // 2
+    units = 2 * (hidden // width) + 1 + triple // width
+    count = 2 * units
+    any_ = pl.BlockSpec(memory_space=pl.ANY)
+    vmem = pl.BlockSpec(memory_space=pltpu.VMEM)
+    bf16, f32 = jnp.bfloat16, jnp.float32
+
+    def shape(*sizes, kind=bf16):
+        return jax.ShapeDtypeStruct(sizes, kind)
+
     return pl.pallas_call(
-        partial(gather_kernel, (dims, tuple(chunks), (0, 2, 4, 6, 8))),
+        partial(forward_kernel, dims),
         out_shape=[
-            jax.ShapeDtypeStruct((s.shape[0] * dp_count, s.shape[1] * fsdp_count), s.dtype)
-            for s in shards
+            shape(length, width),
+            shape(units, deep, across, 2, piece, width),
+            shape(hidden, length),
+            shape(length, hidden),
+            shape(width, length),
+            shape(length, width),
+            shape(length, 128, kind=f32),
+            shape(width, length),
+            shape(length, triple),
+            shape(width, length),
+            shape(length, width),
+            shape(length, 128, kind=f32),
+            shape(8, width, kind=f32),
         ],
-        in_specs=[pl.BlockSpec(memory_space=pl.ANY)] * len(shards),
-        out_specs=[pl.BlockSpec(memory_space=pl.ANY)] * len(shards),
+        in_specs=[vmem] * 7,
+        out_specs=[any_] * 6 + [vmem] + [any_] * 4 + [vmem] * 2,
         scratch_shapes=[
-            pltpu.SemaphoreType.DMA((count,)),
-            pltpu.SemaphoreType.DMA((count, deep)),
-            pltpu.SemaphoreType.DMA((count, deep)),
-            pltpu.SemaphoreType.DMA((count, flat)),
-            pltpu.SemaphoreType.DMA((count, flat)),
-            pltpu.SemaphoreType.DMA((count, deep * across * down)),
-            pltpu.SemaphoreType.DMA((count, deep * across * down)),
-            pltpu.SemaphoreType.DMA((count, down)),
-            pltpu.SemaphoreType.DMA((count, down)),
+            pltpu.VMEM((deep, across, 16, fsdp_count * 128), f32),
+            pltpu.VMEM((8, hidden), f32),
+            pltpu.VMEM((length, width), f32),
+            pltpu.VMEM((length, width), bf16),
+            pltpu.VMEM((length, width), bf16),
+            pltpu.VMEM((length, triple), bf16),
+            pltpu.VMEM((length, width), bf16),
+            pltpu.VMEM((length, hidden), bf16),
+            pltpu.VMEM((length, hidden), bf16),
+            pltpu.VMEM((2, width, length), bf16),
+            pltpu.VMEM((2, deep, across, 2, piece, width), bf16),
+            pltpu.SemaphoreType.DMA((2,)),
+            pltpu.SemaphoreType.DMA((8,)),
+            pltpu.SemaphoreType.DMA((count + 1,)),
+            pltpu.SemaphoreType.DMA((count + 1, deep - 1)),
+            pltpu.SemaphoreType.DMA((count + 1, deep - 1)),
+            pltpu.SemaphoreType.DMA((count + 1, across - 1)),
+            pltpu.SemaphoreType.DMA((count + 1, across - 1)),
+            pltpu.SemaphoreType.DMA((count + 1, (across - 1) * across)),
+            pltpu.SemaphoreType.DMA((count + 1, (across - 1) * across)),
+            pltpu.SemaphoreType.DMA((count + 1, down)),
+            pltpu.SemaphoreType.DMA((count + 1, down)),
         ],
-        compiler_params=pltpu.CompilerParams(collective_id=0, has_side_effects=True),
-    )(*shards)
-
-
-def collect(params):
-    vectors = [item for item in params if item.ndim == 1]
-    packed = jnp.concatenate(vectors)
-    spread = lax.all_gather(packed, ("dp", "fsdp"), axis=0, tiled=False)
-    wholes = gather_weights([params[2], params[5], params[9], params[11]])
-    found = []
-    start = 0
-    matrices = iter(wholes)
-    for item in params:
-        if item.ndim == 2:
-            found.append(next(matrices))
-        else:
-            found.append(spread[:, start : start + item.shape[0]].reshape(-1))
-            start += item.shape[0]
-    return tuple(found)
-
-
-def attend(query, keys, values, start):
-    length = query.shape[0]
-    block = min(256, length)
-    lane = lax.broadcasted_iota(jnp.int32, (block, 2 * HEAD_DIM), 1)
-    factor = math.log2(math.e) / math.sqrt(HEAD_DIM)
-    parts = []
-    for at in range(length // block):
-        rows = slice(at * block, (at + 1) * block)
-        span = (at + 1) * block
-        asked = query[rows, :]
-        seen = keys[:span, :]
-        held = values[:span, :]
-        row = at * block + lax.broadcasted_iota(jnp.int32, (block, span), 0)
-        col = lax.broadcasted_iota(jnp.int32, (block, span), 1)
-        allowed = (col <= row) & (col >= start[rows, :])
-        found = []
-        for side in range(2):
-            mine = jnp.where((lane // HEAD_DIM) == side, asked, jnp.zeros_like(asked))
-            scores = lax.dot_general(
-                mine, seen, (((1,), (1,)), ((), ())), preferred_element_type=jnp.float32
-            )
-            scores = jnp.where(allowed, scores * factor, -1e30)
-            weight = jnp.exp2(scores - jnp.max(scores, axis=1, keepdims=True))
-            total = jnp.sum(weight, axis=1, keepdims=True)
-            mixed = jnp.dot(
-                weight.astype(jnp.bfloat16), held, preferred_element_type=jnp.float32
-            )
-            found.append(mixed / total)
-        parts.append(jnp.where(lane < HEAD_DIM, found[0], found[1]).astype(jnp.bfloat16))
-    return parts
-
-
-def attention_kernel(query, keys, values, start, mixed):
-    block = min(256, query.shape[0])
-    for at, part in enumerate(attend(query, keys, values, start)):
-        mixed[at * block : (at + 1) * block, :] = part
-
-
-def attention(projected, start):
-    length, triple = projected.shape
-    width = triple // 3
-    pairs = width // (2 * HEAD_DIM)
-    return pl.pallas_call(
-        attention_kernel,
-        grid=(pairs,),
-        out_shape=jax.ShapeDtypeStruct((length, width), jnp.bfloat16),
-        in_specs=[
-            pl.BlockSpec((length, 2 * HEAD_DIM), lambda h: (0, h)),
-            pl.BlockSpec((length, 2 * HEAD_DIM), lambda h: (0, pairs + h)),
-            pl.BlockSpec((length, 2 * HEAD_DIM), lambda h: (0, 2 * pairs + h)),
-            pl.BlockSpec((length, 1), lambda h: (0, 0)),
-        ],
-        out_specs=pl.BlockSpec((length, 2 * HEAD_DIM), lambda h: (0, h)),
-        name="attention",
-    )(projected, projected, projected, start)
+        compiler_params=pltpu.CompilerParams(
+            collective_id=0, has_side_effects=True, vmem_limit_bytes=67043328
+        ),
+        name="forward",
+    )(place, frames, vectors, *shards)
+
+
+def place_vectors(items, up_bias):
+    devices = lax.axis_size("dp") * lax.axis_size("fsdp")
+    at = lax.axis_index("dp") * lax.axis_size("fsdp") + lax.axis_index("fsdp")
+    lane = jnp.arange(128)
+
+    def placed(rows):
+        size = rows.shape[1]
+        repeated = jnp.tile(rows.astype(jnp.float32), (1, 128 // size))
+        return jnp.where((lane // size == at % (128 // size))[None], repeated, 0.0)
+
+    packed = jnp.stack(items)
+    return jnp.concatenate(
+        [placed(packed), placed(up_bias[None]), jnp.zeros((7, 128), jnp.float32)]
+    )
 
 
 def matmul(left, right, contract):
@@ -305,7 +526,7 @@
 def backward_kernel(dims, *refs):
     (
         place, cot_hbm, act_hbm, slope_hbm, two_hbm, unit_two, rate_two, mixed_hbm, qkv_hbm,
-        one_hbm, unit_one, rate_one, gains, in_hbm, out_hbm, up_hbm, down_hbm,
+        one_hbm, unit_one, rate_one, gains, weights,
         result, owned, sums,
         grads, twin_in, a_in, b_in, z_in,
         v_own, v_hold, v_twin, v_a, v_b, v_z,
@@ -434,8 +655,32 @@
     def fetch(source, target, at):
         return pltpu.make_async_copy(source, target, load.at[at])
 
-    def tile(ref, j):
-        return ref.at[:, pl.ds(pl.multiple_of(j * width, width), width)]
+    groups_up = hidden // width
+    groups_in = qkv_hbm.shape[1] // width
+    first_up = groups_in + 1
+    first_down = first_up + groups_up
+    dp_count = deep * across
+
+    def down_load(j):
+        moves = []
+        for q in range(dp_count):
+            owner, at = j * (dp_count // groups_up) + q // groups_up, q % groups_up
+            moves.append(
+                fetch(weights.at[first_down + at, pl.ds(2 * owner, 2)], right.at[pl.ds(2 * q, 2)], 2)
+            )
+        return moves
+
+    def matrix():
+        return right[...].reshape(width, width)
+
+    def strips(rows, each, g):
+        parts = []
+        for f in range(fsdp):
+            start = f * each + g * gw
+            if not isinstance(start, int):
+                start = pl.multiple_of(start, 128)
+            parts.append(wide[rows, pl.ds(start, gw)])
+        return jnp.concatenate(parts, axis=1)
 
     def band(ref, j):
         return ref.at[pl.ds(pl.multiple_of(j * width, width), width), :]
@@ -464,7 +709,8 @@
 
     fetch(cot_hbm, cot, 0).start()
     fetch(band(act_hbm, 0), left, 1).start()
-    fetch(band(down_hbm, 0), right, 2).start()
+    for move in down_load(0):
+        move.start()
     fetch(slope_hbm, wide, 3).start()
     fetch(unit_two, unit, 4).start()
     v_own[...] = jnp.zeros_like(v_own)
@@ -485,7 +731,7 @@
             fetch(two_hbm, left, 1).start()
 
         advance(2 * j, 0, 18)
-        fetch(band(down_hbm, j), right, 2).wait()
+        fetch(weights.at[0], right, 2).wait()
 
         @pl.when(j == 0)
         def _():
@@ -495,18 +741,19 @@
 
         @pl.loop(0, steps)
         def _(m):
-            found = matmul(cot[rows_at(m), :], right[...], (1, 1))
+            found = matmul(cot[rows_at(m), :], matrix(), (1, 1))
             found = (found * wide[rows_at(m), span].astype(jnp.float32)).astype(jnp.bfloat16)
             wide[rows_at(m), span] = found
             v_own[pl.ds(8 + j, 1), :] += columns(found.astype(jnp.float32))
 
         @pl.when(j < 3)
         def _():
-            fetch(band(down_hbm, (j + 1) % 4), right, 2).start()
+            for move in down_load((j + 1) % 4):
+                move.start()
 
         @pl.when(j == 3)
         def _():
-            fetch(tile(up_hbm, 0), right, 2).start()
+            fetch(weights.at[first_up], right, 2).start()
 
         advance(2 * j + 1, 0, 18)
 
@@ -517,20 +764,19 @@
     def _(j):
         make_unit(j % 2, wide, lambda f: pl.multiple_of(f * each_up + j * gw, 128))
         advance(8 + 2 * j, 0, 18)
-        fetch(tile(up_hbm, j), right, 2).wait()
-        span = pl.ds(pl.multiple_of(j * width, width), width)
+        fetch(weights.at[first_up + j], right, 2).wait()
 
         @pl.loop(0, steps)
         def _(m):
-            total[rows_at(m), :] += matmul(wide[rows_at(m), span], right[...], (1, 1))
+            total[rows_at(m), :] += matmul(strips(rows_at(m), each_up, j), matrix(), (1, 1))
 
         @pl.when(j < 3)
         def _():
-            fetch(tile(up_hbm, (j + 1) % 4), right, 2).start()
+            fetch(weights.at[first_up + (j + 1) % 4], right, 2).start()
 
         @pl.when(j == 3)
         def _():
-            fetch(out_hbm, right, 2).start()
+            fetch(weights.at[groups_in], right, 2).start()
 
         advance(9 + 2 * j, 0, 18)
 
@@ -548,7 +794,7 @@
             scaled = grad * gain
             mean = jnp.mean(scaled, axis=1, keepdims=True)
             tilt = jnp.mean(scaled * normal, axis=1, keepdims=True)
-            finish(m, grad, normal, rate[rows_at(m), :] * (scaled - mean - normal * tilt))
+            finish(m, grad, normal, rate[rows_at(m), 0:1] * (scaled - mean - normal * tilt))
 
     def finish_two(m, grad, normal, moved):
         incoming = cot[rows_at(m), :].astype(jnp.float32)
@@ -561,20 +807,20 @@
         v_own[6:7, :] += columns(grad)
         v_own[7:8, :] += columns(incoming)
 
-    norm_back(rate_two, gains[1:2, :], finish_two)
+    norm_back(rate_two, gains[5:6, :], finish_two)
     fetch(unit_one, unit, 4).start()
     fetch(mixed_hbm, left, 1).wait()
     make_unit(0, branch, lambda f: f * gw)
     fetch(one_hbm, left, 1).start()
     advance(16, 0, 18)
-    fetch(out_hbm, right, 2).wait()
+    fetch(weights.at[groups_in], right, 2).wait()
 
     @pl.loop(0, steps)
     def _(m):
-        found = matmul(branch[rows_at(m), :], right[...], (1, 1))
+        found = matmul(branch[rows_at(m), :], matrix(), (1, 1))
         branch[rows_at(m), :] = found.astype(jnp.bfloat16)
 
-    fetch(tile(in_hbm, 0), right, 2).start()
+    fetch(weights.at[0], right, 2).start()
     advance(17, 0, 18)
     fetch(qkv_hbm, packed, 3).wait()
     pairs = width // (2 * HEAD_DIM)
@@ -649,15 +895,14 @@
             advance(19, 18, 24)
     fetch(unit_one, unit, 4).wait()
     for j in range(3):
-        fetch(tile(in_hbm, j), right, 2).wait()
-        span = pl.ds(j * width, width)
+        fetch(weights.at[j], right, 2).wait()
 
         @pl.loop(0, steps)
         def _(m):
-            total[rows_at(m), :] += matmul(wide[rows_at(m), span], right[...], (1, 1))
+            total[rows_at(m), :] += matmul(strips(rows_at(m), each_in, j), matrix(), (1, 1))
 
         if j < 2:
-            fetch(tile(in_hbm, j + 1), right, 2).start()
+            fetch(weights.at[j + 1], right, 2).start()
         advance(24 + j, 18, 24)
 
     def finish_one(m, grad, normal, moved):
@@ -724,7 +969,7 @@
             jax.ShapeDtypeStruct((16, width), f32),
         ],
         in_specs=[vmem, any_, any_, any_, any_, any_, vmem, any_, any_, any_, any_, vmem, vmem]
-        + [any_] * 4,
+        + [any_],
         out_specs=[any_, vmem, vmem],
         scratch_shapes=[
             pltpu.VMEM((2, 2, 2, across, down, deep, piece, gw), bf16),
@@ -740,7 +985,7 @@
             pltpu.VMEM((deep - 1, 16, width), f32),
             pltpu.VMEM((length, width), bf16),
             pltpu.VMEM((width, width), bf16),
-            pltpu.VMEM((width, width), bf16),
+            pltpu.VMEM((2 * dp_count, piece, width), bf16),
             pltpu.VMEM((length, width), bf16),
             pltpu.VMEM((length, hidden), bf16),
             pltpu.VMEM((length, width), f32),
@@ -763,7 +1008,7 @@
         ),
         name="backward",
     )(place, cot, act, slope, two, unit_two, rate_two, mixed, qkv, one, unit_one, rate_one, gains,
-      *weights)
+      weights)
 
 
 def side_of(dims):
@@ -812,90 +1057,32 @@
     down_weight,
     down_bias,
 ):
-    params = (
-        norm1_gain,
-        norm1_shift,
-        qkv_weight,
-        query_bias,
-        value_bias,
-        out_weight,
-        out_bias,
-        norm2_gain,
-        norm2_shift,
-        up_weight,
+    length, width = frames.shape
+    many = up_weight.shape[1] * lax.axis_size("fsdp")
+    vectors = place_vectors(
+        [
+            norm1_gain,
+            norm1_shift,
+            query_bias,
+            value_bias,
+            out_bias,
+            norm2_gain,
+            norm2_shift,
+            down_bias,
+        ],
         up_bias,
-        down_weight,
-        down_bias,
     )
-    length, width = frames.shape
-    place_row = positions[0]
     (
-        gain_first,
-        shift_first,
-        weight_in,
-        bias_query,
-        bias_value,
-        weight_out,
-        bias_out,
-        gain_second,
-        shift_second,
-        weight_up,
-        bias_up,
-        weight_down,
-        bias_down,
-    ) = collect(params)
-    gain_one = gain_first.astype(jnp.float32)
-    shift_one = shift_first.astype(jnp.float32)
-    gain_two = gain_second.astype(jnp.float32)
-    shift_two = shift_second.astype(jnp.float32)
-    inputs = frames.astype(jnp.float32) + sinusoid(place_row, width)
-    unit_one, rate_one = standardize(inputs)
-    normed_one = (unit_one * gain_one + shift_one).astype(jnp.bfloat16)
-    projected = jnp.dot(normed_one, weight_in, preferred_element_type=jnp.float32)
-    bias_all = jnp.concatenate([bias_query, jnp.zeros_like(bias_query), bias_value])
-    projected = (projected + bias_all.astype(jnp.float32)).astype(jnp.bfloat16)
-
-    start = jnp.arange(length, dtype=jnp.int32) - place_row
-    mixed = attention(projected, start[:, None])
-    resid_two = (
-        inputs
-        + jnp.dot(mixed, weight_out, preferred_element_type=jnp.float32)
-        + bias_out.astype(jnp.float32)
+        output, weights, act, slope, two, unit_two, rate_two, mixed, qkv, one, unit_one, rate_one,
+        gains,
+    ) = forward(
+        positions[0][:, None], frames, vectors, (qkv_weight, out_weight, up_weight, down_weight)
     )
-    unit_two, rate_two = standardize(resid_two)
-    normed_two = (unit_two * gain_two + shift_two).astype(jnp.bfloat16)
-    hidden = jnp.dot(normed_two, weight_up, preferred_element_type=jnp.float32) + bias_up.astype(
-        jnp.float32
-    )
-    half = 0.5 + 0.5 * lax.erf(hidden * math.sqrt(0.5))
-    activated = (hidden * half).astype(jnp.bfloat16)
-    slope = half + hidden * jnp.exp(-0.5 * hidden * hidden) * (1.0 / math.sqrt(2.0 * math.pi))
-    slope = slope.astype(jnp.bfloat16)
-    result = (
-        resid_two
-        + jnp.dot(activated, weight_down, preferred_element_type=jnp.float32)
-        + bias_down.astype(jnp.float32)
-    )
-    output = result.astype(jnp.bfloat16)
-    many = hidden.shape[1]
-    dp_count = lax.axis_size("dp")
-    act = activated.T.reshape(dp_count, many // width, width // dp_count, length)
-    act = act.transpose(1, 0, 2, 3).reshape(many, length)
+    units, deep, across, halves, piece, _ = weights.shape
+    weights = weights.reshape(units, deep * across * halves, piece, width)
     frames_grad, owned, sums = backward(
-        positions,
-        cotangent,
-        act,
-        slope,
-        normed_two.T,
-        unit_two.astype(jnp.bfloat16),
-        rate_two,
-        mixed.T,
-        projected,
-        normed_one.T,
-        unit_one.astype(jnp.bfloat16),
-        rate_one,
-        jnp.stack([gain_one, gain_two]),
-        (weight_in, weight_out, weight_up, weight_down),
+        positions, cotangent, act, slope, two, unit_two, rate_two, mixed, qkv, one, unit_one,
+        rate_one, gains, weights,
     )
     small, tall, qkv_grad, out_grad, up_grad, down_grad = pick_grads(owned, sums, width, many)
     return (

time: 606 us -> 458 us (0.76); the launches traced: 598 us -> 458 us
  local copies, waits for them, and re-layouts: 79.1 us -> 15.7 us
  Pallas kernels: 389 us -> 440 us
  matrix products: 46 us -> 0 us
  blocking collectives: 43.4 us -> 0 us
  other arithmetic: 38.8 us -> 1.35 us
    dot_general x4 -> x0, matrix products: 46 us -> none  [the longest x1 15.9 us: body(): jnp.dot(normed_two, weight_up, preferred_element_type=jnp.float32)]
    all_gather x1 -> x0, blocking collectives: 43.4 us -> none  [collect(): spread = lax.all_gather(packed, ('dp', 'fsdp'), axis=0, tiled=False)]
    pallas_call x2 -> x1, Pallas kernels: 154 us -> 191 us  [forward(): pl.pallas_call(partial(forward_kernel, dims), out_shape=[shape(length, wi...]
    reshape x3 -> x0, local copies, waits for them, and re-layouts: 25.8 us -> none  [the longest x1 14.2 us: body(): activated.T.reshape(dp_count, many // width, width // dp_count, length)]
    convert_element_type x6 -> x0, other arithmetic: 21 us -> none  [the longest x1 13.2 us: body(): slope = slope.astype(jnp.bfloat16)]
    transpose x3 -> x0, local copies, waits for them, and re-layouts: 20.3 us -> none  [the longest x1 13.7 us: body(): act = act.transpose(1, 0, 2, 3).reshape(many, length)]
    pallas_call x1, Pallas kernels: 235 us -> 249 us  [backward(): pl.pallas_call(partial(backward_kernel, dims), out_shape=[jax.ShapeDtypeS...]
    sin x1 -> x0, other arithmetic: 7.34 us -> none  [sinusoid(): jnp.sin(angles)]
where the time goes in v3:
time: 458 us
  Pallas kernels  440 us (96%)
  local copies, waits for them, and re-layouts  15.7 us (3%)
    pallas_call x1, Pallas kernels, backward(): pl.pallas_call(partial(backward_kernel, dims), out_shape=[jax.ShapeDtypeS...  249 us
    pallas_call x1, Pallas kernels, forward(): pl.pallas_call(partial(forward_kernel, dims), out_shape=[shape(length, wi...  191 us

profile of v3, /device:TPU:0, one launch (start us, length us, event | category | flops | bytes accessed | tf_op | source)
XLA Modules:
  0.0 457.8 jit_solution(13427081733377489183)
XLA Ops:
  0.6 1.7 copy.33.refs_0_
  2.4 0.7 fusion.1
  3.0 0.8 stack.35
  3.8 0.1 tile.10
  3.9 0.1 pad.2.clone
  4.0 0.7 maximum_maximum_fusion.refs_2_
  4.7 191.3 %forward.1 = (bf16[1024,1024]{1,0:T(8,128)(2,1)}, bf16[12,4,2,2,64,1024]{5,4,3,2,1,0:T(8,128)(2,1)}, bf16[4096,1024]{1,0:T(8,128)(2,1)}, bf16[1024,4096]{1,0:T(8...) custom-call(s32[1024,1]{1,0:T(8,128)} %copy.33.refs_0_, ...), custom_call_target="tpu_custom_call" | custom-call | tf_op jit(solution)/shard_map/forward/pallas_call | solution.py:454
  196.0 248.8 %backward.1 = (bf16[1024,1024]{1,0:T(8,128)(2,1)}, f32[24,64,256]{2,1,0:T(8,128)}, f32[16,1024]{1,0:T(8,128)}) custom-call(s32[1,1024]{1,0:T(1,128)} %refs_0_.1, bf16[1024,1024]{1,0:T(8,128)(2,1)} %refs_1_.3, bf16[4096,1024]{1,0:T(8,128)(2,1)} %get-tuple-element.32.refs_2_, bf16[1024,4096]{1,0:T(8,128)(2,1)} %get-tuple-element.33.refs_3_, ...), custom_call_target="tpu_custom_call" | custom-call | tf_op jit(solution)/shard_map/backward/pallas_call | solution.py:964
  444.8 0.8 slice.42
  445.6 0.1 constant_dynamic-slice_fusion
  445.7 0.5 slice_bitcast_fusion.1
  446.2 1.0 slice.45
  447.2 0.2 copy.34
  447.4 0.0 copy-start
  447.4 0.9 copy.36
  448.3 1.6 slice.48
  449.9 2.1 fusion.2
  452.0 0.8 copy.37
  452.8 0.8 slice_bitcast_fusion
  453.6 0.6 dynamic_slice.7
  454.2 0.0 copy-done
  454.2 0.0 copy-start.1
  454.2 1.3 copy.43
  455.5 1.0 copy-done.1
  456.5 1.3 copy.44
  (5 shorter events, 0.0 us)
Async XLA Ops:
  447.4 6.8 %copy-start = (bf16[1024,1024]{1,0:T(8,128)(2,1)S(1)}, bf16[1024,1024]{1,0:T(8,128)(2,1)}, u32[]{:S(2)}) copy-start(bf16[1024,1024]{1,0:T(8,128)(2,1)} %get-tuple-element.87) | copy-start | bytes 6291460
  454.2 2.3 copy-start.1

commit v4 on v3

--- a/solution.py
+++ b/solution.py
@@ -159,10 +159,12 @@
             copy(sheet, sheet, s_send.at[i, s], s_recv.at[i, s], twin).wait()
 
     stages = (first, second, third, fourth)
+    lag = 2
+    last = 3 * lag
 
     def advance(step):
         for at in reversed(range(4)):
-            i = step - at
+            i = step - lag * at
             if isinstance(step, int):
                 if 0 <= i < count:
                     stages[at](i)
@@ -240,11 +242,11 @@
 
     keep(unit, unit_one, 0).start()
     keep(turned.at[0], one_hbm, 1).start()
-    advance(4)
+    done = 4
     for g in range(groups_in):
-        if g:
-            advance(3 + 2 * g)
-            advance(4 + 2 * g)
+        while done < 2 * g + 2 + last:
+            advance(done)
+            done += 1
         unit_load(g, g % 2).start()
         unit_load(g, g % 2).wait()
 
@@ -265,7 +267,7 @@
 
     keep(qkv, qkv_hbm, 2).start()
     pairs = width // (2 * HEAD_DIM)
-    base = 2 * (groups_in - 1) + 5
+    base = done
     factor = math.log2(math.e) / math.sqrt(HEAD_DIM)
     lane = lax.broadcasted_iota(jnp.int32, (block, 2 * HEAD_DIM), 1)
 
@@ -384,7 +386,7 @@
         advance(base + 1 + 2 * g)
 
     keep(slope, slope_hbm, 6).start()
-    for step in range(base + 2 * groups_up, count + 3):
+    for step in range(base + 2 * groups_up, count + last):
         advance(step)
 
     def band_load(k, slot):
@@ -641,9 +643,11 @@
 
     stages = (first, second_stage, third, fourth, fifth)
 
+    lags = (0, 1, 3, 5, 7)
+
     def advance(step, low, high):
         for at in reversed(range(5)):
-            i = step - at
+            i = step - lags[at]
             if isinstance(step, int):
                 if low <= i < high:
                     stages[at](i)
@@ -889,10 +893,7 @@
     for j in range(3):
         make_unit((9 + j) % 2, wide, lambda f: f * each_in + j * gw)
         advance(18 + 2 * j, 18, 24)
-        if j:
-            advance(18 + 2 * j + 1, 18, 24)
-        else:
-            advance(19, 18, 24)
+        advance(19 + 2 * j, 18, 24)
     fetch(unit_one, unit, 4).wait()
     for j in range(3):
         fetch(weights.at[j], right, 2).wait()
@@ -903,7 +904,9 @@
 
         if j < 2:
             fetch(weights.at[j + 1], right, 2).start()
-        advance(24 + j, 18, 24)
+        advance(24 + 2 * j, 18, 24)
+        if j < 2:
+            advance(25 + 2 * j, 18, 24)
 
     def finish_one(m, grad, normal, moved):
         branch[rows_at(m), :] = (second[rows_at(m), :] + moved).astype(jnp.bfloat16)
@@ -931,8 +934,8 @@
     for at in range(4):
         for hop in hops[at]:
             small(*hop).start()
-        if at < 1:
-            advance(27, 18, 24)
+        if at < 2:
+            advance(29 + at, 18, 24)
         for hop in hops[at]:
             small(*hop).wait()
         found = lands[at]()

time: 458 us -> 364 us (0.79)
  Pallas kernels: 440 us -> 346 us
    pallas_call x1, Pallas kernels: 249 us -> 193 us  [backward(): pl.pallas_call(partial(backward_kernel, dims), out_shape=[jax.ShapeDtypeS...]
    pallas_call x1, Pallas kernels: 191 us -> 153 us  [forward(): pl.pallas_call(partial(forward_kernel, dims), out_shape=[shape(length, wi...]
where the time goes in v4:
time: 364 us
  Pallas kernels  346 us (95%)
  local copies, waits for them, and re-layouts  15.7 us (4%)
    pallas_call x1, Pallas kernels, backward(): pl.pallas_call(partial(backward_kernel, dims), out_shape=[jax.ShapeDtypeS...  193 us
    pallas_call x1, Pallas kernels, forward(): pl.pallas_call(partial(forward_kernel, dims), out_shape=[shape(length, wi...  153 us

profile of v4, /device:TPU:0, one launch (start us, length us, event | category | flops | bytes accessed | tf_op | source)
XLA Modules:
  0.0 363.8 jit_solution(2577385982879877035)
XLA Ops:
  0.6 1.7 copy.33.refs_0_
  2.4 0.7 fusion.1
  3.0 0.8 stack.35
  3.8 0.1 tile.10
  3.9 0.1 pad.2.clone
  4.0 0.7 maximum_maximum_fusion.refs_2_
  4.7 153.1 %forward.1 = (bf16[1024,1024]{1,0:T(8,128)(2,1)}, bf16[12,4,2,2,64,1024]{5,4,3,2,1,0:T(8,128)(2,1)}, bf16[4096,1024]{1,0:T(8,128)(2,1)}, bf16[1024,4096]{1,0:T(8...) custom-call(s32[1024,1]{1,0:T(8,128)} %copy.33.refs_0_, ...), custom_call_target="tpu_custom_call" | custom-call | tf_op jit(solution)/shard_map/forward/pallas_call | solution.py:456
  157.8 193.0 %backward.1 = (bf16[1024,1024]{1,0:T(8,128)(2,1)}, f32[24,64,256]{2,1,0:T(8,128)}, f32[16,1024]{1,0:T(8,128)}) custom-call(s32[1,1024]{1,0:T(1,128)} %refs_0_.1, bf16[1024,1024]{1,0:T(8,128)(2,1)} %refs_1_.3, bf16[4096,1024]{1,0:T(8,128)(2,1)} %get-tuple-element.32.refs_2_, bf16[1024,4096]{1,0:T(8,128)(2,1)} %get-tuple-element.33.refs_3_, ...), custom_call_target="tpu_custom_call" | custom-call | tf_op jit(solution)/shard_map/backward/pallas_call | solution.py:967
  350.8 0.8 slice.42
  351.6 0.1 constant_dynamic-slice_fusion
  351.6 0.5 slice_bitcast_fusion.1
  352.2 1.0 slice.45
  353.2 0.2 copy.34
  353.4 0.0 copy-start
  353.4 0.9 copy.36
  354.3 1.6 slice.48
  355.9 2.1 fusion.2
  358.0 0.8 copy.37
  358.8 0.8 slice_bitcast_fusion
  359.6 0.6 dynamic_slice.7
  360.2 0.0 copy-done
  360.2 0.0 copy-start.1
  360.2 1.3 copy.43
  361.5 1.0 copy-done.1
  362.5 1.3 copy.44
  (5 shorter events, 0.0 us)
Async XLA Ops:
  353.4 6.8 %copy-start = (bf16[1024,1024]{1,0:T(8,128)(2,1)S(1)}, bf16[1024,1024]{1,0:T(8,128)(2,1)}, u32[]{:S(2)}) copy-start(bf16[1024,1024]{1,0:T(8,128)(2,1)} %get-tuple-element.87) | copy-start | bytes 6291460
  360.2 2.3 copy-start.1

commit v5 on v4

--- a/solution.py
+++ b/solution.py
@@ -567,6 +567,12 @@
     def z_peer(k):
         return device((z + k) % deep, x, y, c)
 
+    groups_up = hidden // width
+    groups_in = qkv_hbm.shape[1] // width
+    first_in = 2 * groups_up + 1
+    first_up = groups_in + 1
+    first_down = first_up + groups_up
+    dp_count = deep * across
     barrier = pltpu.get_barrier_semaphore()
     everyone = [twin]
     everyone += [a_peer(k) for k in range(1, side)] + [b_peer(k) for k in range(1, side)]
@@ -639,15 +645,26 @@
         found = b_in[i, 0, z].astype(jnp.float32)
         for k in range(1, deep):
             found = found + z_in[i, k - 1].astype(jnp.float32)
-        owned[i] = found
-
-    stages = (first, second_stage, third, fourth, fifth)
-
-    lags = (0, 1, 3, 5, 7)
+        g = i // 2 - first_in
+        moved = 2 * ((g + inner) % groups_in - g)
+        if isinstance(i, int):
+            owned[i + (moved if g >= 0 else 0)] = found
+        else:
+            owned[i + (i // (2 * first_in)) * moved] = found
+
+    def launch(u):
+        for half in range(2):
+            first(2 * u + half)
+
+    def settle(u):
+        for half in range(2):
+            second_stage(2 * u + half)
+
+    stages = (third, fourth, fifth)
 
     def advance(step, low, high):
-        for at in reversed(range(5)):
-            i = step - lags[at]
+        for at in reversed(range(3)):
+            i = step - 2 * at
             if isinstance(step, int):
                 if low <= i < high:
                     stages[at](i)
@@ -658,12 +675,6 @@
 
     def fetch(source, target, at):
         return pltpu.make_async_copy(source, target, load.at[at])
-
-    groups_up = hidden // width
-    groups_in = qkv_hbm.shape[1] // width
-    first_up = groups_in + 1
-    first_down = first_up + groups_up
-    dp_count = deep * across
 
     def down_load(j):
         moves = []
@@ -713,13 +724,12 @@
 
     fetch(cot_hbm, cot, 0).start()
     fetch(band(act_hbm, 0), left, 1).start()
+    v_own[...] = jnp.zeros_like(v_own)
+    total[...] = jnp.zeros_like(total)
+    fetch(cot_hbm, cot, 0).wait()
     for move in down_load(0):
         move.start()
     fetch(slope_hbm, wide, 3).start()
-    fetch(unit_two, unit, 4).start()
-    v_own[...] = jnp.zeros_like(v_own)
-    total[...] = jnp.zeros_like(total)
-    fetch(cot_hbm, cot, 0).wait()
 
     @pl.loop(0, 4)
     def _(j):
@@ -734,7 +744,7 @@
         def _():
             fetch(two_hbm, left, 1).start()
 
-        advance(2 * j, 0, 18)
+        launch(j)
         fetch(weights.at[0], right, 2).wait()
 
         @pl.when(j == 0)
@@ -759,15 +769,17 @@
         def _():
             fetch(weights.at[first_up], right, 2).start()
 
-        advance(2 * j + 1, 0, 18)
+        settle(j)
+        advance(j - 1, 0, 24)
 
     fetch(two_hbm, left, 1).wait()
+    fetch(unit_two, unit, 4).start()
     each_up = hidden // fsdp
 
     @pl.loop(0, 4)
     def _(j):
         make_unit(j % 2, wide, lambda f: pl.multiple_of(f * each_up + j * gw, 128))
-        advance(8 + 2 * j, 0, 18)
+        launch(4 + j)
         fetch(weights.at[first_up + j], right, 2).wait()
 
         @pl.loop(0, steps)
@@ -782,7 +794,8 @@
         def _():
             fetch(weights.at[groups_in], right, 2).start()
 
-        advance(9 + 2 * j, 0, 18)
+        settle(4 + j)
+        advance(3 + j, 0, 24)
 
     triple = qkv_hbm.shape[1]
     packed = wide.at[:, pl.ds(0, triple)]
@@ -812,11 +825,12 @@
         v_own[7:8, :] += columns(incoming)
 
     norm_back(rate_two, gains[5:6, :], finish_two)
+    advance(7, 0, 24)
     fetch(unit_one, unit, 4).start()
     fetch(mixed_hbm, left, 1).wait()
     make_unit(0, branch, lambda f: f * gw)
     fetch(one_hbm, left, 1).start()
-    advance(16, 0, 18)
+    launch(8)
     fetch(weights.at[groups_in], right, 2).wait()
 
     @pl.loop(0, steps)
@@ -825,9 +839,20 @@
         branch[rows_at(m), :] = found.astype(jnp.bfloat16)
 
     fetch(weights.at[0], right, 2).start()
-    advance(17, 0, 18)
+    settle(8)
+    advance(8, 0, 24)
     fetch(qkv_hbm, packed, 3).wait()
+    fetch(one_hbm, left, 1).wait()
     pairs = width // (2 * HEAD_DIM)
+    each_in = triple // fsdp
+    ready = [
+        max((f * each_in + (g + f) % groups_in * gw) % width + gw for f in range(fsdp))
+        // (2 * HEAD_DIM)
+        - 1
+        for g in range(groups_in)
+    ]
+    ready = [max(ready[: g + 1]) for g in range(groups_in)]
+    late = ready[0] > 5 or ready[1] > 6
     scale = 1.0 / math.sqrt(HEAD_DIM)
     factor = scale * math.log2(math.e)
     lane = lax.broadcasted_iota(jnp.int32, (block, 2 * HEAD_DIM), 1)
@@ -846,6 +871,7 @@
             given = branch[rows, at_q]
             seen = wide[pl.ds(0, span), at_k]
             held = wide[pl.ds(0, span), at_v]
+            seen_t = seen.T
             col = at * block + lax.broadcasted_iota(jnp.int32, (span, block), 1)
             row = lax.broadcasted_iota(jnp.int32, (span, block), 0)
             begin = at * block + lax.broadcasted_iota(jnp.int32, (1, block), 1)
@@ -867,11 +893,10 @@
                 grad_s = (probs * (grad_p - delta)).astype(jnp.bfloat16)
                 part_v = matmul(probs.astype(jnp.bfloat16), ours, (1, 0))
                 part_k = matmul(grad_s, mine, (1, 0))
-                grad_q.append(matmul(grad_s, seen, (0, 0)))
+                grad_q.append(matmul(seen_t[half * HEAD_DIM : (half + 1) * HEAD_DIM, :], grad_s, (1, 0)))
                 grad_v = part_v if grad_v is None else grad_v + part_v
                 grad_k = part_k if grad_k is None else grad_k + part_k
-            found = jnp.where(lane < HEAD_DIM, grad_q[0], grad_q[1]) * scale
-            found = found.astype(jnp.bfloat16)
+            found = (jnp.concatenate(grad_q, axis=0) * scale).T.astype(jnp.bfloat16)
             wide[rows, at_q] = found
             sum_q = sum_q + columns(found.astype(jnp.float32))
             if at:
@@ -885,15 +910,37 @@
         wide[:, at_v] = low
         v_own[2:3, at_q] = sum_q
         v_own[3:4, at_q] = columns(low.astype(jnp.float32))
-        advance(18 + j, 0, 18)
+        for g in range(groups_in):
+            tied = g > 0 and ready[g] == ready[g - 1]
+            if g and not tied:
+                @pl.when(j == ready[g - 1] + 1)
+                def _(g=g):
+                    settle(8 + g)
+
+            @pl.when(j == ready[g])
+            def _(g=g, tied=tied):
+                if tied:
+                    settle(8 + g)
+                make_unit(
+                    (9 + g) % 2, wide, lambda f: f * each_in + (g + f) % groups_in * gw
+                )
+                launch(9 + g)
+
+        step = 9 + (3 * j) // 2
+        if late:
+            advance(step, 0, 18)
+        else:
+            advance(step, 0, 24)
+
+        @pl.when(j % 2 == 1)
+        def _():
+            advance(step + 1, 0, 18 if late else 24)
 
     total[...] = jnp.zeros_like(total)
-    each_in = triple // fsdp
-    fetch(one_hbm, left, 1).wait()
-    for j in range(3):
-        make_unit((9 + j) % 2, wide, lambda f: f * each_in + j * gw)
-        advance(18 + 2 * j, 18, 24)
-        advance(19 + 2 * j, 18, 24)
+    settle(11)
+    if late:
+        for step in range(18, 21):
+            advance(step, 18, 24)
     fetch(unit_one, unit, 4).wait()
     for j in range(3):
         fetch(weights.at[j], right, 2).wait()
@@ -904,9 +951,7 @@
 
         if j < 2:
             fetch(weights.at[j + 1], right, 2).start()
-        advance(24 + 2 * j, 18, 24)
-        if j < 2:
-            advance(25 + 2 * j, 18, 24)
+        advance(21 + j, 0, 24)
 
     def finish_one(m, grad, normal, moved):
         branch[rows_at(m), :] = (second[rows_at(m), :] + moved).astype(jnp.bfloat16)
@@ -934,8 +979,7 @@
     for at in range(4):
         for hop in hops[at]:
             small(*hop).start()
-        if at < 2:
-            advance(29 + at, 18, 24)
+        advance(24 + at, 0, 24)
         for hop in hops[at]:
             small(*hop).wait()
         found = lands[at]()

time: 364 us -> 336 us (0.923)
  Pallas kernels: 346 us -> 318 us
    pallas_call x1, Pallas kernels: 193 us -> 165 us  [backward(): pl.pallas_call(partial(backward_kernel, dims), out_shape=[jax.ShapeDtypeS...]
where the time goes in v5:
time: 336 us; the launch traced here: 335 us
  Pallas kernels  318 us (95%)
  local copies, waits for them, and re-layouts  15.7 us (5%)
    pallas_call x1, Pallas kernels, backward(): pl.pallas_call(partial(backward_kernel, dims), out_shape=[jax.ShapeDtypeS...  165 us
    pallas_call x1, Pallas kernels, forward(): pl.pallas_call(partial(forward_kernel, dims), out_shape=[shape(length, wi...  153 us

profile of v5, /device:TPU:0, one launch (start us, length us, event | category | flops | bytes accessed | tf_op | source)
XLA Modules:
  0.0 335.4 jit_solution(10943109202227885071)
XLA Ops:
  0.6 1.7 copy.33.refs_0_
  2.4 0.7 fusion.1
  3.0 0.8 stack.35
  3.8 0.1 tile.10
  3.9 0.1 pad.2.clone
  4.0 0.7 maximum_maximum_fusion.refs_2_
  4.7 153.1 %forward.1 = (bf16[1024,1024]{1,0:T(8,128)(2,1)}, bf16[12,4,2,2,64,1024]{5,4,3,2,1,0:T(8,128)(2,1)}, bf16[4096,1024]{1,0:T(8,128)(2,1)}, bf16[1024,4096]{1,0:T(8...) custom-call(s32[1024,1]{1,0:T(8,128)} %copy.33.refs_0_, ...), custom_call_target="tpu_custom_call" | custom-call | tf_op jit(solution)/shard_map/forward/pallas_call | solution.py:456
  157.8 164.5 %backward.1 = (bf16[1024,1024]{1,0:T(8,128)(2,1)}, f32[24,64,256]{2,1,0:T(8,128)}, f32[16,1024]{1,0:T(8,128)}) custom-call(s32[1,1024]{1,0:T(1,128)} %refs_0_.1, bf16[1024,1024]{1,0:T(8,128)(2,1)} %refs_1_.3, bf16[4096,1024]{1,0:T(8,128)(2,1)} %get-tuple-element.32.refs_2_, bf16[1024,4096]{1,0:T(8,128)(2,1)} %get-tuple-element.33.refs_3_, ...), custom_call_target="tpu_custom_call" | custom-call | tf_op jit(solution)/shard_map/backward/pallas_call | solution.py:1011
  322.4 0.8 slice.42
  323.1 0.1 constant_dynamic-slice_fusion
  323.2 0.5 slice_bitcast_fusion.1
  323.7 1.0 slice.45
  324.8 0.2 copy.34
  324.9 0.0 copy-start
  324.9 0.9 copy.36
  325.9 1.6 slice.48
  327.4 2.1 fusion.2
  329.5 0.8 copy.37
  330.4 0.8 slice_bitcast_fusion
  331.1 0.6 dynamic_slice.7
  331.7 0.0 copy-done
  331.7 0.0 copy-start.1
  331.7 1.3 copy.43
  333.0 1.0 copy-done.1
  334.1 1.3 copy.44
  (5 shorter events, 0.0 us)
Async XLA Ops:
  324.9 6.8 %copy-start = (bf16[1024,1024]{1,0:T(8,128)(2,1)S(1)}, bf16[1024,1024]{1,0:T(8,128)(2,1)}, u32[]{:S(2)}) copy-start(bf16[1024,1024]{1,0:T(8,128)(2,1)} %get-tuple-element.87) | copy-start | bytes 6291460
  331.7 2.3 copy-start.1

commit v6 on v5

--- a/solution.py
+++ b/solution.py
@@ -159,12 +159,12 @@
             copy(sheet, sheet, s_send.at[i, s], s_recv.at[i, s], twin).wait()
 
     stages = (first, second, third, fourth)
-    lag = 2
-    last = 3 * lag
+    lags = (0, 2, 5, 7)
+    last = lags[3]
 
     def advance(step):
         for at in reversed(range(4)):
-            i = step - lag * at
+            i = step - lags[at]
             if isinstance(step, int):
                 if 0 <= i < count:
                     stages[at](i)

time: 336 us -> 332 us (0.988)
  Pallas kernels: 318 us -> 313 us
    pallas_call x1, Pallas kernels: 153 us -> 149 us  [forward(): pl.pallas_call(partial(forward_kernel, dims), out_shape=[shape(length, wi...]
where the time goes in v6:
time: 332 us; the launch traced here: 331 us
  Pallas kernels  313 us (94%)
  local copies, waits for them, and re-layouts  15.7 us (5%)
    pallas_call x1, Pallas kernels, backward(): pl.pallas_call(partial(backward_kernel, dims), out_shape=[jax.ShapeDtypeS...  164 us
    pallas_call x1, Pallas kernels, forward(): pl.pallas_call(partial(forward_kernel, dims), out_shape=[shape(length, wi...  149 us

profile of v6, /device:TPU:0, one launch (start us, length us, event | category | flops | bytes accessed | tf_op | source)
XLA Modules:
  0.0 331.0 jit_solution(2155627914219210916)
XLA Ops:
  0.6 1.7 copy.33.refs_0_
  2.4 0.7 fusion.1
  3.0 0.8 stack.35
  3.8 0.1 tile.10
  3.9 0.1 pad.2.clone
  4.0 0.7 maximum_maximum_fusion.refs_2_
  4.7 149.1 %forward.1 = (bf16[1024,1024]{1,0:T(8,128)(2,1)}, bf16[12,4,2,2,64,1024]{5,4,3,2,1,0:T(8,128)(2,1)}, bf16[4096,1024]{1,0:T(8,128)(2,1)}, bf16[1024,4096]{1,0:T(8...) custom-call(s32[1024,1]{1,0:T(8,128)} %copy.33.refs_0_, ...), custom_call_target="tpu_custom_call" | custom-call | tf_op jit(solution)/shard_map/forward/pallas_call | solution.py:456
  153.8 164.1 %backward.1 = (bf16[1024,1024]{1,0:T(8,128)(2,1)}, f32[24,64,256]{2,1,0:T(8,128)}, f32[16,1024]{1,0:T(8,128)}) custom-call(s32[1,1024]{1,0:T(1,128)} %refs_0_.1, bf16[1024,1024]{1,0:T(8,128)(2,1)} %refs_1_.3, bf16[4096,1024]{1,0:T(8,128)(2,1)} %get-tuple-element.32.refs_2_, bf16[1024,4096]{1,0:T(8,128)(2,1)} %get-tuple-element.33.refs_3_, ...), custom_call_target="tpu_custom_call" | custom-call | tf_op jit(solution)/shard_map/backward/pallas_call | solution.py:1011
  317.9 0.8 slice.42
  318.7 0.1 constant_dynamic-slice_fusion
  318.8 0.5 slice_bitcast_fusion.1
  319.3 1.0 slice.45
  320.3 0.2 copy.34
  320.5 0.0 copy-start
  320.5 0.9 copy.36
  321.4 1.6 slice.48
  323.0 2.1 fusion.2
  325.1 0.8 copy.37
  325.9 0.8 slice_bitcast_fusion
  326.7 0.6 dynamic_slice.7
  327.3 0.0 copy-done
  327.3 0.0 copy-start.1
  327.3 1.3 copy.43
  328.6 1.0 copy-done.1
  329.6 1.3 copy.44
  (5 shorter events, 0.0 us)
Async XLA Ops:
  320.5 6.8 %copy-start = (bf16[1024,1024]{1,0:T(8,128)(2,1)S(1)}, bf16[1024,1024]{1,0:T(8,128)(2,1)}, u32[]{:S(2)}) copy-start(bf16[1024,1024]{1,0:T(8,128)(2,1)} %get-tuple-element.87) | copy-start | bytes 6291460
  327.3 2.3 copy-start.1
